TPU v7x, 32 devices: a whole 2x2x4 slice. The times are simulated.
32 devices in a mesh: dp: 8 (over y, x, core), tensor: 4 (over z).
Axes of the slice: x: 2, y: 2, z: 4, core: 2. Of those that a mesh axis runs over, the one named last changes fastest.
Arguments:
- teacher_input: bfloat16 [8, 1024, 1280], P('dp', 'tensor'), may hold values from -6 to 6
- teacher_upstream: bfloat16 [8, 1024, 1280], P('dp', 'tensor'), may hold values from -6 to 6
- teacher_attn_gain: bfloat16 [1280], P('dp'), may hold values from 0.25 to 1.75
- teacher_attn_shift: bfloat16 [1280], P('dp'), may hold values from -1.75 to 1.75
- teacher_qkv_weight: bfloat16 [3, 1280, 1536], P(None, 'dp', 'tensor'), may hold values from -0.15625 to 0.15625
- teacher_qv_bias: bfloat16 [2, 1536], P(None, 'tensor'), may hold values from -0.625 to 0.625
- teacher_out_weight: bfloat16 [1536, 1280], P('tensor', 'dp'), may hold values from -1.25 to 1.25
- teacher_out_bias: bfloat16 [1280], P('dp'), may hold values from -1.75 to 1.75
- teacher_mlp_gain: bfloat16 [1280], P('dp'), may hold values from 0.25 to 1.75
- teacher_mlp_shift: bfloat16 [1280], P('dp'), may hold values from -1.75 to 1.75
- teacher_fc_weight: bfloat16 [1280, 5120], P('dp', 'tensor'), may hold values from -0.15625 to 0.15625
- teacher_fc_bias: bfloat16 [5120], P('tensor'), may hold values from -1.75 to 1.75
- teacher_proj_weight: bfloat16 [5120, 1280], P('tensor', 'dp'), may hold values from -0.078125 to 0.078125
- teacher_proj_bias: bfloat16 [1280], P('dp'), may hold values from -1.75 to 1.75
- student_input: bfloat16 [8, 1024, 768], P('dp', 'tensor'), may hold values from -6 to 6
- student_upstream: bfloat16 [8, 1024, 768], P('dp', 'tensor'), may hold values from -6 to 6
- student_attn_gain: bfloat16 [768], P('dp'), may hold values from 0.25 to 1.75
- student_attn_shift: bfloat16 [768], P('dp'), may hold values from -1.75 to 1.75
- student_qkv_weight: bfloat16 [3, 768, 768], P(None, 'dp', 'tensor'), may hold values from -0.21875 to 0.21875
- student_qv_bias: bfloat16 [2, 768], P(None, 'tensor'), may hold values from -0.625 to 0.625
- student_out_weight: bfloat16 [768, 768], P('tensor', 'dp'), may hold values from -1.75 to 1.75
- student_out_bias: bfloat16 [768], P('dp'), may hold values from -1.75 to 1.75
- student_mlp_gain: bfloat16 [768], P('dp'), may hold values from 0.25 to 1.75
- student_mlp_shift: bfloat16 [768], P('dp'), may hold values from -1.75 to 1.75
- student_fc_weight: bfloat16 [768, 3072], P('dp', 'tensor'), may hold values from -0.21875 to 0.21875
- student_fc_bias: bfloat16 [3072], P('tensor'), may hold values from -1.75 to 1.75
- student_proj_weight: bfloat16 [3072, 768], P('tensor', 'dp'), may hold values from -0.109375 to 0.109375
- student_proj_bias: bfloat16 [768], P('dp'), may hold values from -1.75 to 1.75
- span_starts: int32 [8], P('dp'), may hold values from 0 to 768, as said below
- head_slots: int32 [24], P('tensor'), may hold values from 0 to 1, as said below
Outputs:
- teacher_output: bfloat16 [8, 1024, 1280], P('dp', 'tensor')
- teacher_input_grad: bfloat16 [8, 1024, 1280], P('dp', 'tensor')
- teacher_attn_gain_grad: float32 [1280], P('dp')
- teacher_attn_shift_grad: float32 [1280], P('dp')
- teacher_qkv_weight_grad: float32 [3, 1280, 1536], P(None, 'dp', 'tensor')
- teacher_qv_bias_grad: float32 [2, 1536], P(None, 'tensor')
- teacher_out_weight_grad: float32 [1536, 1280], P('tensor', 'dp')
- teacher_out_bias_grad: float32 [1280], P('dp')
- teacher_mlp_gain_grad: float32 [1280], P('dp')
- teacher_mlp_shift_grad: float32 [1280], P('dp')
- teacher_fc_weight_grad: float32 [1280, 5120], P('dp', 'tensor')
- teacher_fc_bias_grad: float32 [5120], P('tensor')
- teacher_proj_weight_grad: float32 [5120, 1280], P('tensor', 'dp')
- teacher_proj_bias_grad: float32 [1280], P('dp')
- student_output: bfloat16 [8, 1024, 768], P('dp', 'tensor')
- student_input_grad: bfloat16 [8, 1024, 768], P('dp', 'tensor')
- student_attn_gain_grad: float32 [768], P('dp')
- student_attn_shift_grad: float32 [768], P('dp')
- student_qkv_weight_grad: float32 [3, 768, 768], P(None, 'dp', 'tensor')
- student_qv_bias_grad: float32 [2, 768], P(None, 'tensor')
- student_out_weight_grad: float32 [768, 768], P('tensor', 'dp')
- student_out_bias_grad: float32 [768], P('dp')
- student_mlp_gain_grad: float32 [768], P('dp')
- student_mlp_shift_grad: float32 [768], P('dp')
- student_fc_weight_grad: float32 [768, 3072], P('dp', 'tensor')
- student_fc_bias_grad: float32 [3072], P('tensor')
- student_proj_weight_grad: float32 [3072, 768], P('tensor', 'dp')
- student_proj_bias_grad: float32 [768], P('dp')
Inputs may be any that keep to these rules, and one draw needn't show every extreme that they name: `span_starts`: some sequence starts its span at 0 and some at 768. `head_slots`: exactly 20 of the 24 slots are 1.
All inputs are finite; a program needn't handle non-finite values.
Results may differ from a plain program's by a relative error of at most 0.02.
Values may be sent and summed in bfloat16 or wider, within the bound.
No kernel may reach another device: no remote copies, remote signals or barrier semaphores. Data moves between devices by JAX's collectives and lax.ppermute only.
A program may use at most 256 MiB of HBM per device.

v0:
```python
import jax
import jax.numpy as jnp
from jax import lax
from jax.sharding import PartitionSpec as P

HD = 64
SPAN = 256


epsilon = 1e-05
negative = -1e30


def layer_norm(values, norm_gain, norm_shift):
    center = values - jnp.mean(values, axis=-1, keepdims=True)
    spread = jnp.mean(center * center, axis=-1, keepdims=True)
    return center * lax.rsqrt(spread + epsilon) * norm_gain + norm_shift


def gelu_tanh(values):
    return jax.nn.gelu(values, approximate=True)


def visibility(first_row, block_rows, length, span_start):
    query_pos = first_row + jnp.arange(block_rows, dtype=jnp.int32)
    key_pos = jnp.arange(length, dtype=jnp.int32)
    query_in = (query_pos >= span_start) & (query_pos < span_start + SPAN)
    key_in = (key_pos >= span_start) & (key_pos < span_start + SPAN)
    return (key_pos[None, :] <= query_pos[:, None]) | query_in[:, None] & key_in[None, :]


def block_scores(query_block, key_rows, visible, score_scale):
    scores = (
        jnp.einsum("qhe,khe->hqk", query_block, key_rows, preferred_element_type=jnp.float32)
        * score_scale
    )
    return jnp.where(visible[None], scores, negative)


def attention_forward(query_rows, key_rows, value_rows, span_start, block_rows, score_scale):
    length = query_rows.shape[0]
    results = []
    log_sums = []
    for block_index in range(length // block_rows):
        first_row = block_index * block_rows
        visible = visibility(first_row, block_rows, length, span_start)
        scores = block_scores(
            query_rows[first_row : first_row + block_rows], key_rows, visible, score_scale
        )
        row_peak = jnp.max(scores, axis=-1, keepdims=True)
        raised = jnp.exp(scores - row_peak)
        row_total = jnp.sum(raised, axis=-1, keepdims=True)
        weights = (raised / row_total).astype(jnp.bfloat16)
        results.append(
            jnp.einsum("hqk,khe->qhe", weights, value_rows, preferred_element_type=jnp.float32)
        )
        log_sums.append(row_peak + jnp.log(row_total))
    return (jnp.concatenate(results, axis=0), log_sums)


def attention_backward(
    query_rows, key_rows, value_rows, log_sums, heads_grad, span_start, block_rows, score_scale
):
    length = query_rows.shape[0]
    query_grads = []
    key_grad = jnp.zeros(key_rows.shape, jnp.float32)
    value_grad = jnp.zeros(value_rows.shape, jnp.float32)
    for block_index in range(length // block_rows):
        first_row = block_index * block_rows
        last_row = first_row + block_rows
        visible = visibility(first_row, block_rows, length, span_start)
        scores = block_scores(query_rows[first_row:last_row], key_rows, visible, score_scale)
        probability = jnp.exp(scores - log_sums[block_index])
        grad_block = heads_grad[first_row:last_row]
        value_grad = value_grad + jnp.einsum(
            "hqk,qhe->khe",
            probability.astype(jnp.bfloat16),
            grad_block,
            preferred_element_type=jnp.float32,
        )
        prob_grad = jnp.einsum(
            "qhe,khe->hqk", grad_block, value_rows, preferred_element_type=jnp.float32
        )
        weighted = jnp.sum(probability * prob_grad, axis=-1, keepdims=True)
        score_grad = (probability * (prob_grad - weighted)).astype(jnp.bfloat16)
        query_grads.append(
            jnp.einsum("hqk,khe->qhe", score_grad, key_rows, preferred_element_type=jnp.float32)
            * score_scale
        )
        key_grad = (
            key_grad
            + jnp.einsum(
                "hqk,qhe->khe",
                score_grad,
                query_rows[first_row:last_row],
                preferred_element_type=jnp.float32,
            )
            * score_scale
        )
    return (jnp.concatenate(query_grads, axis=0), key_grad, value_grad)


def gather_rows(normed):
    return lax.all_gather(normed, "tensor", axis=0, tiled=True)


def gather_grads(branch_grad):
    return lax.all_gather(branch_grad, "tensor", axis=0, tiled=True)


def sum_rows(left_rows, right_weight):
    return lax.psum_scatter(
        jnp.dot(left_rows, right_weight, preferred_element_type=jnp.float32).astype(jnp.bfloat16),
        "tensor",
        scatter_dimension=0,
        tiled=True,
    ).astype(jnp.float32)


def back_rows(grad_stack, weight_stack):
    return lax.psum_scatter(
        jnp.einsum(
            "sle,sde->ld", grad_stack, weight_stack, preferred_element_type=jnp.float32
        ).astype(jnp.bfloat16),
        "tensor",
        scatter_dimension=0,
        tiled=True,
    ).astype(jnp.float32)


def run_block(
    inputs,
    upstream,
    attn_gain,
    attn_shift,
    qkv_weight,
    qv_bias,
    out_weight,
    out_bias,
    mlp_gain,
    mlp_shift,
    fc_weight,
    fc_bias,
    proj_weight,
    proj_bias,
    span_start,
    head_keep,
):
    gathered = (
        lax.all_gather(qkv_weight, "dp", axis=1, tiled=True),
        lax.all_gather(out_weight, "dp", axis=1, tiled=True),
        lax.all_gather(fc_weight, "dp", axis=0, tiled=True),
        lax.all_gather(proj_weight, "dp", axis=1, tiled=True),
        lax.all_gather(attn_gain, "dp", axis=0, tiled=True),
        lax.all_gather(attn_shift, "dp", axis=0, tiled=True),
        lax.all_gather(out_bias, "dp", axis=0, tiled=True),
        lax.all_gather(mlp_gain, "dp", axis=0, tiled=True),
        lax.all_gather(mlp_shift, "dp", axis=0, tiled=True),
        lax.all_gather(proj_bias, "dp", axis=0, tiled=True),
    )
    qkv_full, out_full, fc_full, proj_full = (gathered[0], gathered[1], gathered[2], gathered[3])
    gain_one = gathered[4].astype(jnp.float32)
    shift_one = gathered[5].astype(jnp.float32)
    bias_out = gathered[6].astype(jnp.float32)
    gain_two = gathered[7].astype(jnp.float32)
    shift_two = gathered[8].astype(jnp.float32)
    bias_proj = gathered[9].astype(jnp.float32)
    rows_first = inputs[0].astype(jnp.float32)
    normed, norm_back_one = jax.vjp(layer_norm, rows_first, gain_one, shift_one)
    normed_all = gather_rows(normed.astype(jnp.bfloat16))
    projected = jnp.einsum("ld,tde->tle", normed_all, qkv_full, preferred_element_type=jnp.float32)
    bias_pair = qv_bias.astype(jnp.float32)
    length = normed_all.shape[0]
    head_count = head_keep.shape[0]
    head_split = (length, head_count, HD)
    query_rows = (projected[0] + bias_pair[0]).astype(jnp.bfloat16).reshape(head_split)
    key_rows = projected[1].astype(jnp.bfloat16).reshape(head_split)
    value_rows = (projected[2] + bias_pair[1]).astype(jnp.bfloat16).reshape(head_split)
    block_rows = min(512, length)
    score_scale = 1.0 / HD**0.5
    attended, log_sums = attention_forward(
        query_rows, key_rows, value_rows, span_start, block_rows, score_scale
    )
    keep_float = head_keep.astype(jnp.float32)[None, :, None]
    heads_low = (attended * keep_float).astype(jnp.bfloat16).reshape(length, head_count * HD)
    attn_sum = sum_rows(heads_low, out_full)
    middle = rows_first + (attn_sum + bias_out)
    normed_two, norm_back_two = jax.vjp(layer_norm, middle, gain_two, shift_two)
    normed_two_all = gather_rows(normed_two.astype(jnp.bfloat16))
    hidden_pre = jnp.dot(
        normed_two_all, fc_full, preferred_element_type=jnp.float32
    ) + fc_bias.astype(jnp.float32)
    hidden, gelu_back = jax.vjp(gelu_tanh, hidden_pre)
    hidden_low = hidden.astype(jnp.bfloat16)
    mlp_sum = sum_rows(hidden_low, proj_full)
    result = middle + (mlp_sum + bias_proj)
    outputs = result.astype(jnp.bfloat16)[None]
    grad_result = upstream[0].astype(jnp.float32)
    grad_mlp_all = gather_grads(upstream[0])
    proj_bias_grad = jnp.sum(grad_mlp_all, axis=0, dtype=jnp.float32)
    proj_grad = jnp.einsum(
        "lf,ld->fd", hidden_low, grad_mlp_all, preferred_element_type=jnp.float32
    )
    hidden_grad = jnp.einsum(
        "ld,fd->lf", grad_mlp_all, proj_full, preferred_element_type=jnp.float32
    )
    pre_grad = gelu_back(hidden_grad)[0].astype(jnp.bfloat16)
    fc_bias_grad = jnp.sum(pre_grad, axis=0, dtype=jnp.float32)
    fc_grad = jnp.einsum("ld,lf->df", normed_two_all, pre_grad, preferred_element_type=jnp.float32)
    normed_two_grad = back_rows(pre_grad[None], fc_full[None])
    middle_from_norm, gain_two_grad, shift_two_grad = norm_back_two(normed_two_grad)
    middle_grad = grad_result + middle_from_norm
    grad_attn_all = gather_grads(middle_grad.astype(jnp.bfloat16))
    out_bias_grad = jnp.sum(grad_attn_all, axis=0, dtype=jnp.float32)
    out_grad = jnp.einsum("le,ld->ed", heads_low, grad_attn_all, preferred_element_type=jnp.float32)
    heads_grad = (
        jnp.einsum("ld,ed->le", grad_attn_all, out_full, preferred_element_type=jnp.float32)
        .astype(jnp.bfloat16)
        .reshape(head_split)
    )
    heads_grad = heads_grad * head_keep.astype(jnp.bfloat16)[None, :, None]
    query_grad, key_grad, value_grad = attention_backward(
        query_rows, key_rows, value_rows, log_sums, heads_grad, span_start, block_rows, score_scale
    )
    qkv_low = jnp.stack(
        [
            query_grad.reshape(length, head_count * HD),
            key_grad.reshape(length, head_count * HD),
            value_grad.reshape(length, head_count * HD),
        ]
    ).astype(jnp.bfloat16)
    qv_bias_grad = jnp.stack(
        [
            jnp.sum(qkv_low[0], axis=0, dtype=jnp.float32),
            jnp.sum(qkv_low[2], axis=0, dtype=jnp.float32),
        ]
    )
    qkv_grad = jnp.einsum("ld,tle->tde", normed_all, qkv_low, preferred_element_type=jnp.float32)
    normed_grad = back_rows(qkv_low, qkv_full)
    rows_from_norm, gain_one_grad, shift_one_grad = norm_back_one(normed_grad)
    input_grad = (middle_grad + rows_from_norm).astype(jnp.bfloat16)[None]
    norm_sums = lax.psum((gain_one_grad, shift_one_grad, gain_two_grad, shift_two_grad), "tensor")
    matrices = (
        qkv_grad,
        out_grad,
        fc_grad,
        proj_grad,
        norm_sums[0],
        norm_sums[1],
        out_bias_grad,
        norm_sums[2],
        norm_sums[3],
        proj_bias_grad,
    )
    biases = (qv_bias_grad, fc_bias_grad)
    return (outputs, input_grad, matrices, biases)


def arrange(outputs, input_grad, matrices, biases):
    return (
        outputs,
        input_grad,
        matrices[4],
        matrices[5],
        matrices[0],
        biases[0],
        matrices[1],
        matrices[6],
        matrices[7],
        matrices[8],
        matrices[2],
        biases[1],
        matrices[3],
        matrices[9],
    )


def on_device(
    teacher_input,
    teacher_upstream,
    teacher_attn_gain,
    teacher_attn_shift,
    teacher_qkv_weight,
    teacher_qv_bias,
    teacher_out_weight,
    teacher_out_bias,
    teacher_mlp_gain,
    teacher_mlp_shift,
    teacher_fc_weight,
    teacher_fc_bias,
    teacher_proj_weight,
    teacher_proj_bias,
    student_input,
    student_upstream,
    student_attn_gain,
    student_attn_shift,
    student_qkv_weight,
    student_qv_bias,
    student_out_weight,
    student_out_bias,
    student_mlp_gain,
    student_mlp_shift,
    student_fc_weight,
    student_fc_bias,
    student_proj_weight,
    student_proj_bias,
    span_starts,
    head_slots,
):
    span_start = span_starts[0]
    teacher = run_block(
        teacher_input,
        teacher_upstream,
        teacher_attn_gain,
        teacher_attn_shift,
        teacher_qkv_weight,
        teacher_qv_bias,
        teacher_out_weight,
        teacher_out_bias,
        teacher_mlp_gain,
        teacher_mlp_shift,
        teacher_fc_weight,
        teacher_fc_bias,
        teacher_proj_weight,
        teacher_proj_bias,
        span_start,
        head_slots,
    )
    student_keep = jnp.ones((student_qv_bias.shape[1] // HD,), jnp.int32)
    student = run_block(
        student_input,
        student_upstream,
        student_attn_gain,
        student_attn_shift,
        student_qkv_weight,
        student_qv_bias,
        student_out_weight,
        student_out_bias,
        student_mlp_gain,
        student_mlp_shift,
        student_fc_weight,
        student_fc_bias,
        student_proj_weight,
        student_proj_bias,
        span_start,
        student_keep,
    )
    teach_parts = teacher[2]
    learn_parts = student[2]
    summed = (
        lax.psum_scatter(teach_parts[0], "dp", scatter_dimension=1, tiled=True),
        lax.psum_scatter(teach_parts[1], "dp", scatter_dimension=1, tiled=True),
        lax.psum_scatter(teach_parts[2], "dp", scatter_dimension=0, tiled=True),
        lax.psum_scatter(teach_parts[3], "dp", scatter_dimension=1, tiled=True),
        lax.psum_scatter(teach_parts[4], "dp", scatter_dimension=0, tiled=True),
        lax.psum_scatter(teach_parts[5], "dp", scatter_dimension=0, tiled=True),
        lax.psum_scatter(teach_parts[6], "dp", scatter_dimension=0, tiled=True),
        lax.psum_scatter(teach_parts[7], "dp", scatter_dimension=0, tiled=True),
        lax.psum_scatter(teach_parts[8], "dp", scatter_dimension=0, tiled=True),
        lax.psum_scatter(teach_parts[9], "dp", scatter_dimension=0, tiled=True),
        lax.psum_scatter(learn_parts[0], "dp", scatter_dimension=1, tiled=True),
        lax.psum_scatter(learn_parts[1], "dp", scatter_dimension=1, tiled=True),
        lax.psum_scatter(learn_parts[2], "dp", scatter_dimension=0, tiled=True),
        lax.psum_scatter(learn_parts[3], "dp", scatter_dimension=1, tiled=True),
        lax.psum_scatter(learn_parts[4], "dp", scatter_dimension=0, tiled=True),
        lax.psum_scatter(learn_parts[5], "dp", scatter_dimension=0, tiled=True),
        lax.psum_scatter(learn_parts[6], "dp", scatter_dimension=0, tiled=True),
        lax.psum_scatter(learn_parts[7], "dp", scatter_dimension=0, tiled=True),
        lax.psum_scatter(learn_parts[8], "dp", scatter_dimension=0, tiled=True),
        lax.psum_scatter(learn_parts[9], "dp", scatter_dimension=0, tiled=True),
    )
    totals = lax.psum((teacher[3][0], teacher[3][1], student[3][0], student[3][1]), "dp")
    teacher_matrices = summed[0:10]
    student_matrices = summed[10:20]
    teacher_biases = (totals[0], totals[1])
    student_biases = (totals[2], totals[3])
    return arrange(teacher[0], teacher[1], teacher_matrices, teacher_biases) + arrange(
        student[0], student[1], student_matrices, student_biases
    )


def solution(mesh):
    in_specs = (
        P("dp", "tensor", None),
        P("dp", "tensor", None),
        P("dp"),
        P("dp"),
        P(None, "dp", "tensor"),
        P(None, "tensor"),
        P("tensor", "dp"),
        P("dp"),
        P("dp"),
        P("dp"),
        P("dp", "tensor"),
        P("tensor"),
        P("tensor", "dp"),
        P("dp"),
        P("dp", "tensor", None),
        P("dp", "tensor", None),
        P("dp"),
        P("dp"),
        P(None, "dp", "tensor"),
        P(None, "tensor"),
        P("tensor", "dp"),
        P("dp"),
        P("dp"),
        P("dp"),
        P("dp", "tensor"),
        P("tensor"),
        P("tensor", "dp"),
        P("dp"),
        P("dp"),
        P("tensor"),
    )
    out_specs = (
        P("dp", "tensor", None),
        P("dp", "tensor", None),
        P("dp"),
        P("dp"),
        P(None, "dp", "tensor"),
        P(None, "tensor"),
        P("tensor", "dp"),
        P("dp"),
        P("dp"),
        P("dp"),
        P("dp", "tensor"),
        P("tensor"),
        P("tensor", "dp"),
        P("dp"),
        P("dp", "tensor", None),
        P("dp", "tensor", None),
        P("dp"),
        P("dp"),
        P(None, "dp", "tensor"),
        P(None, "tensor"),
        P("tensor", "dp"),
        P("dp"),
        P("dp"),
        P("dp"),
        P("dp", "tensor"),
        P("tensor"),
        P("tensor", "dp"),
        P("dp"),
    )
    return jax.shard_map(
        on_device, mesh=mesh, in_specs=in_specs, out_specs=out_specs, check_vma=False
    )
```

profile of v0, /device:TPU:0, one launch (start us, length us, event | category | flops | bytes accessed | tf_op | source)
XLA Modules:
  0.0 1425.0 jit_solution(5786993439719821327)
XLA Ops:
  22.5 26.5 %all-reduce.27 = (bf16[1280]{0:T(1024)(128)(2,1)}, bf16[1280]{0:T(1024)(128)(2,1)}, bf16[1280]{0:T(1024)(128)(2,1)S(1)}, bf16[1280]{0:T(1024)(128)(2,1)S(1)}, bf...) all-reduce(bf16[1280]{0:T(1024)(128)(2,1)S(1)} %dynamic-update-slic, ...), channel_id=1, replica_groups=mesh['dp'=8,'tensor'=4] {'dp'}, use_global_device_ids=true, to_apply=%add.4 | all-reduce | flops 12288 | bytes 49152
  67.2 13.4 all_gather.101
  107.9 35.7 %all-gather.16.cloned.1.call-done = bf16[1024,1280]{1,0:T(8,128)(2,1)} async-done(((bf16[256,1280]{1,0:T(8,128)(2,1)}), bf16[1024,1280]{1,0:T(8,128)(2,1)}) %all-gather.16.cloned.1.call-update) | async-done | bytes 2621456 | tf_op jit(solution)/shard_map/all_gather | solution.py:104
  143.6 32.2 %all-gather.18.cloned.1.call-done = bf16[3,1280,384]{2,1,0:T(8,128)(2,1)} async-done(((bf16[3,160,384]{2,1,0:T(8,128)(2,1)}), bf16[3,1280,384]{2,1,0:T(8,128)(2,1)}) %all-gather.18.cloned.1.call-update) | async-done | bytes 2949136 | tf_op jit(solution)/shard_map/all_gather | solution.py:150
  220.0 46.6 %reduce-scatter.20.cloned.1.call-done = bf16[256,1280]{1,0:T(8,128)(2,1)} async-done(((bf16[1024,1280]{1,0:T(8,128)(2,1)}), bf16[256,1280]{1,0:T(8,128)(2,1)}) %reduce-scatter.20.cloned.1.call-update) | async-done | bytes 655376 | tf_op jit(solution)/shard_map/reduce_scatter | solution.py:112
  273.4 18.6 %all-gather.32.cloned.1.call-done = bf16[768,768]{1,0:T(8,128)(2,1)} async-done(((bf16[96,768]{1,0:T(8,128)(2,1)}), bf16[768,768]{1,0:T(8,128)(2,1)}) %all-gather.32.cloned.1.call-update) | async-done | bytes 1179664 | tf_op jit(solution)/shard_map/all_gather | solution.py:152
  292.1 39.3 %all-gather.30.cloned.1.call-done = bf16[1024,768]{1,0:T(8,128)(2,1)} async-done(((bf16[256,768]{1,0:T(8,128)(2,1)}), bf16[1024,768]{1,0:T(8,128)(2,1)}) %all-gather.30.cloned.1.call-update) | async-done | bytes 1572880 | tf_op jit(solution)/shard_map/all_gather | solution.py:104
  336.1 20.0 %all-gather.34.cloned.1.call-done = bf16[768,768]{0,1:T(8,128)(2,1)} async-done(((bf16[768,96]{0,1:T(8,128)(2,1)}), bf16[768,768]{0,1:T(8,128)(2,1)}) %all-gather.34.cloned.1.call-update) | async-done | bytes 1179664 | tf_op jit(solution)/shard_map/all_gather | solution.py:153
  356.2 38.7 %all-gather.40.cloned.1.call-done = bf16[1,1024,768]{2,1,0:T(8,128)(2,1)} async-done(((bf16[1,256,768]{2,1,0:T(8,128)(2,1)}), bf16[1,1024,768]{2,1,0:T(8,128)(2,1)}) %all-gather.40.cloned.1.call-update) | async-done | bytes 1572880 | tf_op jit(solution)/shard_map/all_gather | solution.py:108
  411.1 17.3 %all-gather.22.cloned.1.call-done = bf16[1280,1280]{1,0:T(8,128)(2,1)} async-done(((bf16[160,1280]{1,0:T(8,128)(2,1)}), bf16[1280,1280]{1,0:T(8,128)(2,1)}) %all-gather.22.cloned.1.call-update) | async-done | bytes 3276816 | tf_op jit(solution)/shard_map/all_gather | solution.py:152
  428.4 57.0 %all-gather.20.cloned.1.call-done = bf16[1024,1280]{1,0:T(8,128)(2,1)} async-done(((bf16[256,1280]{1,0:T(8,128)(2,1)}), bf16[1024,1280]{1,0:T(8,128)(2,1)}) %all-gather.20.cloned.1.call-update) | async-done | bytes 2621456 | tf_op jit(solution)/shard_map/all_gather | solution.py:104
  493.9 46.5 %all-gather.38.cloned.1.call-done = bf16[1,1024,1280]{2,1,0:T(8,128)(2,1)} async-done(((bf16[1,256,1280]{2,1,0:T(8,128)(2,1)}), bf16[1,1024,1280]{2,1,0:T(8,128)(2,1)}) %all-gather.38.cloned.1.call-update) | async-done | bytes 2621456 | tf_op jit(solution)/shard_map/all_gather | solution.py:108
  540.4 33.5 %all-gather.24.cloned.1.call-done = bf16[1280,1280]{0,1:T(8,128)(2,1)} async-done(((bf16[1280,160]{0,1:T(8,128)(2,1)}), bf16[1280,1280]{0,1:T(8,128)(2,1)}) %all-gather.24.cloned.1.call-update) | async-done | bytes 3276816 | tf_op jit(solution)/shard_map/all_gather | solution.py:153
  613.4 34.4 %reduce-scatter.36.cloned.1.call-done = bf16[256,768]{1,0:T(8,128)(2,1)} async-done(((bf16[1024,768]{1,0:T(8,128)(2,1)}), bf16[256,768]{1,0:T(8,128)(2,1)}) %reduce-scatter.36.cloned.1.call-update) | async-done | bytes 393232 | tf_op jit(solution)/shard_map/reduce_scatter | solution.py:112
  652.6 48.5 %reduce-scatter.24.cloned.1.call-done = bf16[256,1280]{1,0:T(8,128)(2,1)} async-done(((bf16[1024,1280]{1,0:T(8,128)(2,1)}), bf16[256,1280]{1,0:T(8,128)(2,1)}) %reduce-scatter.24.cloned.1.call-update) | async-done | bytes 655376 | tf_op jit(solution)/shard_map/reduce_scatter | solution.py:121
  703.5 51.6 %reduce-scatter.22.cloned.1.call-done = bf16[256,1280]{1,0:T(8,128)(2,1)} async-done(((bf16[1024,1280]{1,0:T(8,128)(2,1)}), bf16[256,1280]{1,0:T(8,128)(2,1)}) %reduce-scatter.22.cloned.1.call-update) | async-done | bytes 655376 | tf_op jit(solution)/shard_map/reduce_scatter | solution.py:112
  760.7 33.2 %all-gather.36.cloned.1.call-done = bf16[1024,768]{1,0:T(8,128)(2,1)} async-done(((bf16[256,768]{1,0:T(8,128)(2,1)}), bf16[1024,768]{1,0:T(8,128)(2,1)}) %all-gather.36.cloned.1.call-update) | async-done | bytes 1572880 | tf_op jit(solution)/shard_map/all_gather | solution.py:108
  987.0 105.5 %all-reduce.30.cloned.1.call-done = f32[3,1280,384]{2,0,1:T(4,128)} async-done(((f32[3,1280,384]{2,0,1:T(4,128)}), f32[3,1280,384]{2,0,1:T(4,128)}) %all-reduce.30.cloned.1.call-update) | async-done | bytes 5898256
  1094.7 52.2 %reduce-scatter.26.cloned.1.call-done = bf16[256,1280]{1,0:T(8,128)(2,1)} async-done(((bf16[1024,1280]{1,0:T(8,128)(2,1)}), bf16[256,1280]{1,0:T(8,128)(2,1)}) %reduce-scatter.26.cloned.1.call-update) | async-done | bytes 655376 | tf_op jit(solution)/shard_map/reduce_scatter | solution.py:121
  1150.3 25.6 %all-reduce.25 = (f32[1280]{0:T(1024)S(1)}, f32[1280]{0:T(1024)S(1)}, f32[2,384]{1,0:T(2,128)}, f32[1280]{0:T(1024)S(1)}, f32[1280]{0:T(1024)S(1)}, /*index=5*/f...) all-reduce(f32[1280]{0:T(1024)S(1)} %get-tuple-element.86, ...), channel_id=8, replica_groups=mesh['dp'=8,'tensor'=4] {'dp'}, use_global_device_ids=true, to_apply=%region_20.21.clone | all-reduce | flops 15488 | bytes 123904
  1193.0 46.7 %reduce-scatter.42.cloned.1.call-done = f32[96,768]{1,0:T(8,128)} async-done(((f32[768,768]{1,0:T(8,128)}), f32[96,768]{1,0:T(8,128)}) %reduce-scatter.42.cloned.1.call-update) | async-done | bytes 294928 | tf_op jit(solution)/shard_map/reduce_scatter | solution.py:363
  1239.6 66.9 %reduce-scatter.32.cloned.1.call-done = f32[1280,160]{0,1:T(8,128)} async-done(((f32[1280,1280]{0,1:T(8,128)}), f32[1280,160]{0,1:T(8,128)}) %reduce-scatter.32.cloned.1.call-update) | async-done | bytes 819216 | tf_op jit(solution)/shard_map/reduce_scatter | solution.py:354
  1306.5 67.4 %reduce-scatter.30.cloned.1.call-done = f32[160,1280]{1,0:T(8,128)} async-done(((f32[1280,1280]{1,0:T(8,128)}), f32[160,1280]{1,0:T(8,128)}) %reduce-scatter.30.cloned.1.call-update) | async-done | bytes 819216 | tf_op jit(solution)/shard_map/reduce_scatter | solution.py:353
  1374.0 44.3 %reduce-scatter.28.cloned.1.call-done = f32[384,160]{0,1:T(8,128)} async-done(((f32[384,1280]{0,1:T(8,128)}), f32[384,160]{0,1:T(8,128)}) %reduce-scatter.28.cloned.1.call-update) | async-done | bytes 245776 | tf_op jit(solution)/shard_map/reduce_scatter | solution.py:352
  (549 shorter events, 403.6 us)
Async XLA Ops:
  54.7 158.6 %reduce-scatter.34.cloned.1.call-start = ((), (), s32[]{:S(2)}) async-start(), calls=%async_computation.29 | async-start | bytes 1966080 | tf_op jit(solution)/shard_map/reduce_scatter | solution.py:112
  107.7 158.9 %reduce-scatter.20.cloned.1.call-start = ((), (), s32[]{:S(2)}) async-start(), calls=%async_computation.17 | async-start | bytes 3276800 | tf_op jit(solution)/shard_map/reduce_scatter | solution.py:112
  217.8 138.4 %all-gather.34.cloned.1.call-start = ((), (), s32[]{:S(2)}) async-start(), calls=%async_computation.32 | async-start | bytes 1327104 | tf_op jit(solution)/shard_map/all_gather | solution.py:153
  218.5 176.3 %all-gather.40.cloned.1.call-start = ((), (), s32[]{:S(2)}) async-start(), calls=%async_computation.40 | async-start | bytes 1966080 | tf_op jit(solution)/shard_map/all_gather | solution.py:108
  219.3 209.1 %all-gather.22.cloned.1.call-start = ((), (), s32[]{:S(2)}) async-start(), calls=%async_computation.19 | async-start | bytes 3686400 | tf_op jit(solution)/shard_map/all_gather | solution.py:152
  219.8 265.5 %all-gather.20.cloned.1.call-start = ((), (), s32[]{:S(2)}) async-start(), calls=%async_computation.18 | async-start | bytes 3276800 | tf_op jit(solution)/shard_map/all_gather | solution.py:104
  271.8 268.6 %all-gather.38.cloned.1.call-start = ((), (), s32[]{:S(2)}) async-start(), calls=%async_computation.39 | async-start | bytes 3276800 | tf_op jit(solution)/shard_map/all_gather | solution.py:108
  272.3 301.6 %all-gather.24.cloned.1.call-start = ((), (), s32[]{:S(2)}) async-start(), calls=%async_computation.20 | async-start | bytes 3686400 | tf_op jit(solution)/shard_map/all_gather | solution.py:153
  273.1 338.3 %reduce-scatter.38.cloned.1.call-start = ((), (), s32[]{:S(2)}) async-start(), calls=%async_computation.34 | async-start | bytes 1966080 | tf_op jit(solution)/shard_map/reduce_scatter | solution.py:121
  405.0 242.9 %reduce-scatter.36.cloned.1.call-start = ((), (), s32[]{:S(2)}) async-start(), calls=%async_computation.33 | async-start | bytes 1966080 | tf_op jit(solution)/shard_map/reduce_scatter | solution.py:112
  410.5 290.6 %reduce-scatter.24.cloned.1.call-start = ((), (), s32[]{:S(2)}) async-start(), calls=%async_computation.22 | async-start | bytes 3276800 | tf_op jit(solution)/shard_map/reduce_scatter | solution.py:121
  591.1 164.0 %reduce-scatter.22.cloned.1.call-start = ((), (), s32[]{:S(2)}) async-start(), calls=%async_computation.21 | async-start | bytes 3276800 | tf_op jit(solution)/shard_map/reduce_scatter | solution.py:112
  600.9 193.0 %all-gather.36.cloned.1.call-start = ((), (), s32[]{:S(2)}) async-start(), calls=%async_computation.35 | async-start | bytes 1966080 | tf_op jit(solution)/shard_map/all_gather | solution.py:108
  652.4 197.4 %all-gather.26.cloned.1.call-start = ((), (), s32[]{:S(2)}) async-start(), calls=%async_computation.23 | async-start | bytes 3276800 | tf_op jit(solution)/shard_map/all_gather | solution.py:108
  760.6 211.8 %reduce-scatter.48.cloned.1.call-start = ((), (), s32[]{:S(2)}) async-start(), calls=%async_computation.42 | async-start | bytes 884736
  817.0 157.1 %reduce-scatter.46.cloned.1.call-start = ((), (), s32[]{:S(2)}) async-start(), calls=%async_computation.41 | async-start | bytes 2211840
  834.9 141.0 %reduce-scatter.40.cloned.1.call-start = ((), (), s32[]{:S(2)}) async-start(), calls=%async_computation.36 | async-start | bytes 1966080 | tf_op jit(solution)/shard_map/reduce_scatter | solution.py:121
  838.9 253.5 %all-reduce.30.cloned.1.call-start = ((), (), s32[]{:S(2)}) async-start(), calls=%async_computation.43 | async-start | bytes 15728640
  929.1 217.7 %reduce-scatter.26.cloned.1.call-start = ((), (), s32[]{:S(2)}) async-start(), calls=%async_computation.24 | async-start | bytes 3276800 | tf_op jit(solution)/shard_map/reduce_scatter | solution.py:121
  937.0 255.9 %reduce-scatter.44.cloned.1.call-start = ((), (), s32[]{:S(2)}) async-start(), calls=%async_computation.38 | async-start | bytes 2654208 | tf_op jit(solution)/shard_map/reduce_scatter | solution.py:364
  942.3 297.3 %reduce-scatter.42.cloned.1.call-start = ((), (), s32[]{:S(2)}) async-start(), calls=%async_computation.37 | async-start | bytes 2654208 | tf_op jit(solution)/shard_map/reduce_scatter | solution.py:363
  947.3 359.2 %reduce-scatter.32.cloned.1.call-start = ((), (), s32[]{:S(2)}) async-start(), calls=%async_computation.27 | async-start | bytes 7372800 | tf_op jit(solution)/shard_map/reduce_scatter | solution.py:354
  957.2 416.7 %reduce-scatter.30.cloned.1.call-start = ((), (), s32[]{:S(2)}) async-start(), calls=%async_computation.26 | async-start | bytes 7372800 | tf_op jit(solution)/shard_map/reduce_scatter | solution.py:353
  966.2 452.1 %reduce-scatter.28.cloned.1.call-start = ((), (), s32[]{:S(2)}) async-start(), calls=%async_computation.25 | async-start | bytes 2211840 | tf_op jit(solution)/shard_map/reduce_scatter | solution.py:352
  (140 other events, 5088.6 us)
Sparse Core Ops, SparseCore 0:
  51.1 36.5 all-gather.27
  89.9 53.6 all-gather.15
  178.0 35.2 reduce-scatter.33
  215.4 51.0 reduce-scatter.19
  294.2 37.0 all-gather.29
  357.7 37.0 all-gather.39
  430.5 54.7 all-gather.19
  486.8 53.5 all-gather.37
  576.1 35.2 reduce-scatter.37
  613.6 34.2 reduce-scatter.35
  650.0 51.0 reduce-scatter.23
  703.3 51.7 reduce-scatter.21
  757.1 36.7 all-gather.35
  796.1 53.6 all-gather.25
  852.8 33.8 reduce-scatter.47
  890.1 40.3 reduce-scatter.45
  932.9 35.2 reduce-scatter.39
  971.8 120.5 all-reduce.29
  1094.6 52.2 reduce-scatter.25
  1150.8 42.1 reduce-scatter.43
  1197.1 42.4 reduce-scatter.41
  1243.5 62.9 reduce-scatter.31
  1310.9 62.9 reduce-scatter.29
  1378.0 40.2 reduce-scatter.27
  (5 shorter events, 139.9 us)
where the time goes:
time: 1430 us
  waiting for transfers between devices  967 us (68%)
  matrix products  200 us (14%)
  blocking collectives  96.9 us (7%)
  other arithmetic  80.6 us (6%)
  local copies, waits for them, and re-layouts  57.9 us (4%)
  between operations  19.8 us (1%)
    reduce_scatter x4, waiting for transfers between devices, sum_rows(): lax.psum_scatter(jnp.dot(left_rows, right_weight, preferred_element_type=...  137 us
    all_gather x4, waiting for transfers between devices, gather_rows(): return lax.all_gather(normed, 'tensor', axis=0, tiled=True)  132 us
    all_gather x4, waiting for transfers between devices, gather_grads(): return lax.all_gather(branch_grad, 'tensor', axis=0, tiled=True)  129 us
    reduce_scatter x4, waiting for transfers between devices, back_rows(): lax.psum_scatter(jnp.einsum('sle,sde->ld', grad_stack, weight_stack, pref...  111 us
    unnamed x32, waiting for transfers between devices  110 us
    reduce_scatter x1, waiting for transfers between devices, on_device(): lax.psum_scatter(teach_parts[2], 'dp', scatter_dimension=0, tiled=True)  67.4 us
    reduce_scatter x1, waiting for transfers between devices, on_device(): lax.psum_scatter(teach_parts[3], 'dp', scatter_dimension=1, tiled=True)  66.9 us
    all_gather x2, waiting for transfers between devices, run_block(): lax.all_gather(proj_weight, 'dp', axis=1, tiled=True)  53.6 us
  transfers between devices with their start and end apart: 29, of which 25 were waited for; matrix products, arithmetic and copies ran while one was open for 22% of the time, Pallas kernels for 0%

commit v1 on v0

--- a/solution.py
+++ b/solution.py
@@ -1,6 +1,12 @@
+import functools
+
 import jax
 import jax.numpy as jnp
+import numpy as np
 from jax import lax
+from jax.experimental import pallas as pl
+from jax.experimental.pallas import tpu as pltpu
+from jax.sharding import Mesh
 from jax.sharding import PartitionSpec as P
 
 HD = 64
@@ -379,6 +385,1076 @@
     )
 
 
+PLANE = ("y", "x", "c")
+EVERY = ("y", "x", "c", "z")
+TILE = 256
+
+
+def swap(values, axis):
+    return lax.ppermute(values, axis, ((0, 1), (1, 0)))
+
+
+def ring(values, step):
+    return lax.ppermute(values, "z", tuple((i, (i + step) % 4) for i in range(4)))
+
+
+def cross(values):
+    pairs = tuple(
+        ((y * 4 + a) * 4 + z, (y * 4 + z) * 4 + a) for y in range(2) for a in range(4) for z in range(4)
+    )
+    return lax.ppermute(values, EVERY, pairs)
+
+
+def pick(values, index, axis=0):
+    return lax.dynamic_index_in_dim(values, index, axis, keepdims=False)
+
+
+def wide(values):
+    return values.astype(jnp.float32)
+
+
+def low(values):
+    return values.astype(jnp.bfloat16)
+
+
+def matmul(left, right, left_dim, right_dim):
+    return lax.dot_general(
+        left, right, (((left_dim,), (right_dim,)), ((), ())), preferred_element_type=jnp.float32
+    )
+
+
+def after(values, *earlier):
+    return lax.optimization_barrier((values, *earlier))[0]
+
+
+def gather_tokens(own):
+    other = swap(own, "x")
+    return own, other, swap(own, "c"), swap(other, "c")
+
+
+def scatter_tokens(near, far):
+    count = near.shape[0] // 2
+    got = swap(far, "c")
+    ahead = low(wide(near[count:]) + wide(got[count:]))
+    return near, got, swap(ahead, "x")
+
+
+def plane_out(blocks):
+    got = lax.all_to_all(blocks, PLANE, 0, 0)
+    return jnp.transpose(got, (1, 0, 2)).reshape(got.shape[1], -1)
+
+
+def plane_back(rows):
+    split = jnp.transpose(rows.reshape(rows.shape[0], 8, -1), (1, 0, 2))
+    return lax.all_to_all(split, PLANE, 0, 0)
+
+
+def ring_pieces(piece):
+    held = [piece]
+    for _ in range(3):
+        held.append(ring(held[-1], 1))
+    return held
+
+
+def ring_sum(parts):
+    total = None
+    for k in (1, 2, 3):
+        part = parts[k] if total is None else parts[k] + wide(total)
+        total = ring(low(part), 1)
+    return parts[0] + wide(total)
+
+
+def sum_everywhere(vector):
+    for axis in ("c", "x", "y"):
+        vector = vector + swap(vector, axis)
+    for bit in (1, 2):
+        vector = vector + lax.ppermute(vector, "z", tuple((i, i ^ bit) for i in range(4)))
+    return vector
+
+
+def row_call(kernel, name, outs, *args):
+    rows = outs[0][0][0]
+    size = sum(a.size * a.dtype.itemsize for a in args)
+
+    def spec(shape):
+        return pl.BlockSpec((min(shape[0], rows), shape[1]), lambda i: (0, 0))
+
+    return pl.pallas_call(
+        kernel,
+        grid=(1,),
+        in_specs=[spec(a.shape) for a in args],
+        out_specs=[spec(shape) for shape, _ in outs],
+        out_shape=[jax.ShapeDtypeStruct(shape, dtype) for shape, dtype in outs],
+        cost_estimate=pl.CostEstimate(flops=args[0].size * 20, transcendentals=0, bytes_accessed=2 * size),
+        name=name,
+    )(*args)
+
+
+def centered(rows):
+    center = rows - jnp.mean(rows, axis=-1, keepdims=True)
+    spread = jnp.mean(center * center, axis=-1, keepdims=True)
+    scale = lax.rsqrt(spread + epsilon)
+    return center * scale, scale
+
+
+def first_norm_kernel(x_ref, gain_ref, shift_ref, out_ref):
+    unit, _ = centered(wide(x_ref[...]))
+    out_ref[...] = low(unit * gain_ref[...] + shift_ref[...])
+
+
+def mid_norm_kernel(x_ref, a_ref, b_ref, c_ref, bias_ref, gain_ref, shift_ref, mid_ref, out_ref):
+    branch = wide(a_ref[...]) + wide(b_ref[...]) + wide(c_ref[...])
+    middle = wide(x_ref[...]) + (branch + bias_ref[...])
+    mid_ref[...] = middle
+    unit, _ = centered(middle)
+    out_ref[...] = low(unit * gain_ref[...] + shift_ref[...])
+
+
+def norm_back(grad, rows, gain):
+    unit, scale = centered(rows)
+    t = grad * gain
+    back = scale * (
+        t - jnp.mean(t, axis=-1, keepdims=True) - unit * jnp.mean(t * unit, axis=-1, keepdims=True)
+    )
+    return back, jnp.sum(grad * unit, axis=0, keepdims=True), jnp.sum(grad, axis=0, keepdims=True)
+
+
+def mid_back_kernel(g_ref, a_ref, b_ref, c_ref, mid_ref, gain_ref, dmid_ref, ga_ref, sums_ref):
+    up = wide(g_ref[...])
+    grad = wide(a_ref[...]) + wide(b_ref[...]) + wide(c_ref[...])
+    back, gain_sum, shift_sum = norm_back(grad, mid_ref[...], gain_ref[...])
+    dmid = up + back
+    dmid_ref[...] = dmid
+    ga = low(dmid)
+    ga_ref[...] = ga
+    sums_ref[0:1] = jnp.sum(wide(ga), axis=0, keepdims=True)
+    sums_ref[1:2] = gain_sum
+    sums_ref[2:3] = shift_sum
+    sums_ref[3:4] = jnp.sum(up, axis=0, keepdims=True)
+
+
+def first_back_kernel(a_ref, b_ref, c_ref, x_ref, dmid_ref, gain_ref, dx_ref, sums_ref):
+    grad = wide(a_ref[...]) + wide(b_ref[...]) + wide(c_ref[...])
+    back, gain_sum, shift_sum = norm_back(grad, wide(x_ref[...]), gain_ref[...])
+    dx_ref[...] = low(dmid_ref[...] + back)
+    sums_ref[0:1] = gain_sum
+    sums_ref[1:2] = shift_sum
+
+
+def place_of(block, rank):
+    turn = block ^ rank
+    return ((turn & 1) << 1) | (turn >> 1)
+
+
+def tile_visible(first_key, first_query, start):
+    shape = (TILE, TILE)
+    key = first_key + lax.broadcasted_iota(jnp.int32, shape, 0)
+    query = first_query + lax.broadcasted_iota(jnp.int32, shape, 1)
+    key_in = (key >= start) & (key < start + SPAN)
+    query_in = (query >= start) & (query < start + SPAN)
+    return (key <= query) | (key_in & query_in)
+
+
+def tile_bounds(block, blocks, start):
+    more = (start // TILE == block) & (start % TILE != 0)
+    return jnp.minimum(block + 1 + more.astype(jnp.int32), blocks)
+
+
+def head_lanes(width, head):
+    lane = lax.broadcasted_iota(jnp.int32, (1, width), 1)
+    return (lane >= head * HD) & (lane < (head + 1) * HD)
+
+
+def forward_kernel(info_ref, keep_ref, q_ref, k_ref, v_ref, out_ref, log_ref, *, group, blocks):
+    width = q_ref.shape[-1]
+    block = pl.program_id(1)
+    start, rank = info_ref[0], info_ref[1]
+    query = q_ref[0]
+    queries = [jnp.where(head_lanes(width, h), query, jnp.zeros_like(query)) for h in range(group)]
+
+    def tile(index, carry, masked):
+        rows = pl.ds(pl.multiple_of(place_of(index, rank) * TILE, TILE), TILE)
+        keys = k_ref[0, rows, :]
+        values = v_ref[0, rows, :]
+        if masked:
+            visible = tile_visible(index * TILE, block * TILE, start)
+        out = []
+        for h in range(group):
+            peak, total, acc = carry[h]
+            scores = matmul(keys, queries[h], 1, 1)
+            if masked:
+                scores = jnp.where(visible, scores, negative)
+            new_peak = jnp.maximum(peak, jnp.max(scores, axis=0, keepdims=True))
+            decay = jnp.exp(peak - new_peak)
+            raised = jnp.exp(scores - new_peak)
+            total = total * decay + jnp.sum(raised, axis=0, keepdims=True)
+            part = matmul(values, low(raised), 0, 0)
+            acc = acc * decay + part[h * HD : (h + 1) * HD]
+            out.append((new_peak, total, acc))
+        return tuple(out)
+
+    carry = tuple(
+        (
+            jnp.full((1, TILE), negative, jnp.float32),
+            jnp.zeros((1, TILE), jnp.float32),
+            jnp.zeros((HD, TILE), jnp.float32),
+        )
+        for _ in range(group)
+    )
+    carry = lax.fori_loop(0, block, lambda i, s: tile(i, s, False), carry)
+    carry = lax.fori_loop(
+        block, tile_bounds(block, blocks, start), lambda i, s: tile(i, s, True), carry
+    )
+    first = pl.program_id(0) * group
+    outs = []
+    for h in range(group):
+        peak, total, acc = carry[h]
+        outs.append(acc * (keep_ref[first + h] / total))
+        log_ref[0, h : h + 1, :] = peak + jnp.log(total)
+    out_ref[...] = low(jnp.concatenate(outs, axis=0).T)
+
+
+def backward_kernel(
+    info_ref, keep_ref, q_ref, k_ref, v_ref, heads_ref, grad_ref, log_ref,
+    dq_ref, dk_ref, dv_ref, dk_sum, dv_sum, *, group, blocks,
+):
+    width = q_ref.shape[-1]
+    block = pl.program_id(1)
+    start, rank = info_ref[0], info_ref[1]
+    first = pl.program_id(0) * group
+
+    @pl.when(block == 0)
+    def _():
+        dk_sum[...] = jnp.zeros_like(dk_sum)
+        dv_sum[...] = jnp.zeros_like(dv_sum)
+
+    query = q_ref[0]
+    grad = grad_ref[...]
+    turned = (wide(grad) * wide(heads_ref[...])).T
+    queries, grads, weighted, logs = [], [], [], []
+    for h in range(group):
+        lanes = head_lanes(width, h)
+        keep = keep_ref[first + h]
+        queries.append(jnp.where(lanes, query, jnp.zeros_like(query)))
+        grads.append(low(jnp.where(lanes, wide(grad) * keep, 0.0)))
+        weighted.append(keep * jnp.sum(turned[h * HD : (h + 1) * HD], axis=0, keepdims=True))
+        logs.append(log_ref[0, h : h + 1, :])
+
+    def tile(index, carry, masked):
+        rows = pl.ds(pl.multiple_of(place_of(index, rank) * TILE, TILE), TILE)
+        keys = k_ref[0, rows, :]
+        values = v_ref[0, rows, :]
+        if masked:
+            visible = tile_visible(index * TILE, block * TILE, start)
+        dk = dv = None
+        out = []
+        for h in range(group):
+            scores = matmul(keys, queries[h], 1, 1)
+            if masked:
+                scores = jnp.where(visible, scores, negative)
+            prob = jnp.exp(scores - logs[h])
+            dprob = matmul(values, grads[h], 1, 1)
+            dscores = low(prob * (dprob - weighted[h]))
+            dv_part = matmul(low(prob), grads[h], 1, 0)
+            dk_part = matmul(dscores, queries[h], 1, 0)
+            dv = dv_part if dv is None else dv + dv_part
+            dk = dk_part if dk is None else dk + dk_part
+            out.append(carry[h] + matmul(keys, dscores, 0, 0)[h * HD : (h + 1) * HD])
+        dk_sum[rows, :] += dk
+        dv_sum[rows, :] += dv
+        return tuple(out)
+
+    carry = tuple(jnp.zeros((HD, TILE), jnp.float32) for _ in range(group))
+    carry = lax.fori_loop(0, block, lambda i, s: tile(i, s, False), carry)
+    carry = lax.fori_loop(
+        block, tile_bounds(block, blocks, start), lambda i, s: tile(i, s, True), carry
+    )
+    dq_ref[...] = low((jnp.concatenate(carry, axis=0) * (1.0 / HD**0.5)).T)
+
+    @pl.when(block == blocks - 1)
+    def _():
+        dk_ref[...] = low(dk_sum[...])
+        dv_ref[...] = low(dv_sum[...])
+
+
+def attention_plan(columns):
+    group = 2 if columns % (2 * HD) == 0 else columns // HD
+    return group, group * HD
+
+
+def attention_specs(columns, length):
+    group, width = attention_plan(columns)
+    keep = pl.BlockSpec(memory_space=pltpu.SMEM)
+    query = pl.BlockSpec((1, TILE, width), lambda g, b, info: (0, place_of(b, info[1]), g))
+    keys = pl.BlockSpec((1, length, width), lambda g, b, info: (1, 0, g))
+    values = pl.BlockSpec((1, length, width), lambda g, b, info: (2, 0, g))
+    rows = pl.BlockSpec((TILE, width), lambda g, b, info: (place_of(b, info[1]), g))
+    logs = pl.BlockSpec((1, group, TILE), lambda g, b, info: (g, 0, place_of(b, info[1])))
+    whole = pl.BlockSpec((length, width), lambda g, b, info: (0, g))
+    return keep, query, keys, values, rows, logs, whole
+
+
+def attend(info, keep, qkv):
+    _, length, columns = qkv.shape
+    group, width = attention_plan(columns)
+    blocks = length // TILE
+    keep_spec, query, keys, values, rows, logs, _ = attention_specs(columns, length)
+    pairs = columns // HD * length * length // 2
+    return pl.pallas_call(
+        functools.partial(forward_kernel, group=group, blocks=blocks),
+        grid_spec=pltpu.PrefetchScalarGridSpec(
+            num_scalar_prefetch=1,
+            grid=(columns // width, blocks),
+            in_specs=[keep_spec, query, keys, values],
+            out_specs=[rows, logs],
+        ),
+        out_shape=[
+            jax.ShapeDtypeStruct((length, columns), jnp.bfloat16),
+            jax.ShapeDtypeStruct((columns // width, group, length), jnp.float32),
+        ],
+        cost_estimate=pl.CostEstimate(
+            flops=pairs * 4 * HD * 4, transcendentals=pairs, bytes_accessed=length * columns * 10
+        ),
+        name="attend",
+    )(info, keep, qkv, qkv, qkv)
+
+
+def attend_back(info, keep, qkv, heads_out, grads, logs):
+    _, length, columns = qkv.shape
+    group, width = attention_plan(columns)
+    blocks = length // TILE
+    keep_spec, query, keys, values, rows, logs_spec, whole = attention_specs(columns, length)
+    pairs = columns // HD * length * length // 2
+    flat = jax.ShapeDtypeStruct((length, columns), jnp.bfloat16)
+    return pl.pallas_call(
+        functools.partial(backward_kernel, group=group, blocks=blocks),
+        grid_spec=pltpu.PrefetchScalarGridSpec(
+            num_scalar_prefetch=1,
+            grid=(columns // width, blocks),
+            in_specs=[keep_spec, query, keys, values, rows, rows, logs_spec],
+            out_specs=[rows, whole, whole],
+            scratch_shapes=[
+                pltpu.VMEM((length, width), jnp.float32),
+                pltpu.VMEM((length, width), jnp.float32),
+            ],
+        ),
+        out_shape=[flat, flat, flat],
+        cost_estimate=pl.CostEstimate(
+            flops=pairs * 10 * HD * 4, transcendentals=pairs, bytes_accessed=length * columns * 20
+        ),
+        name="attend_back",
+    )(info, keep, qkv, qkv, qkv, heads_out, grads, logs)
+
+
+ANY = pl.BlockSpec(memory_space=pl.ANY)
+VMEM = pl.BlockSpec(memory_space=pltpu.VMEM)
+LIMIT = 56 << 20
+
+
+def fetch(parts, into, sem):
+    first = 0
+    for part in parts:
+        rows = part.shape[0]
+        pltpu.make_async_copy(part, into.at[pl.ds(first, rows)], sem).start()
+        first += rows
+
+
+def fetched(into, sem):
+    pltpu.make_async_copy(into, into, sem).wait()
+
+
+def send(source, into, sem):
+    copy = pltpu.make_async_copy(source, into, sem)
+    copy.start()
+    return copy
+
+
+def scratch(*shape):
+    return pltpu.VMEM(shape, jnp.bfloat16)
+
+
+def matmul_call(kernel, name, outs, args, specs, scratches, flops):
+    size = sum(a.size * a.dtype.itemsize for a in args)
+    return pl.pallas_call(
+        kernel,
+        in_specs=specs,
+        out_specs=[spec for _, _, spec in outs],
+        out_shape=[jax.ShapeDtypeStruct(shape, dtype) for shape, dtype, _ in outs],
+        scratch_shapes=scratches,
+        compiler_params=pltpu.CompilerParams(vmem_limit_bytes=LIMIT),
+        cost_estimate=pl.CostEstimate(flops=flops, transcendentals=0, bytes_accessed=2 * size),
+        name=name,
+    )(*args)
+
+
+def project(pieces, weights, places, bias, columns):
+    count, width = pieces[0].shape
+    length = 4 * count
+    scales = (1.0 / HD**0.5, 1.0, 1.0)
+
+    def kernel(*refs):
+        piece_refs, refs = refs[:4], refs[4:]
+        weight_refs, refs = refs[: len(weights)], refs[len(weights) :]
+        bias_ref, qkv_ref, all_ref, full_ref, rows_s, full_s, qkv_s, sems, outs = refs
+        for array, index, row, matrix, column, rows in places:
+            source = weight_refs[array]
+            source = source if index is None else source.at[index]
+            pltpu.make_async_copy(
+                source.at[pl.ds(row, rows)], full_s.at[matrix, pl.ds(column, rows)], sems.at[0]
+            ).start()
+        fetch(piece_refs, rows_s, sems.at[1])
+        fetched(full_s, sems.at[0])
+        fetched(rows_s, sems.at[1])
+        sent = [send(full_s, full_ref, outs.at[0]), send(rows_s, all_ref, outs.at[1])]
+
+        @pl.loop(0, 4)
+        def _(block):
+            rows = pl.ds(pl.multiple_of(block * count, count), count)
+            for t in range(3):
+                part = low(matmul(rows_s[rows, :], full_s[t], 1, 1) + bias_ref[t])
+                qkv_s[t, rows, :] = low(wide(part) * scales[t])
+
+        sent.append(send(qkv_s, qkv_ref, outs.at[2]))
+        for copy in sent:
+            copy.wait()
+
+    return matmul_call(
+        kernel,
+        "project",
+        [
+            ((3, length, columns), jnp.bfloat16, ANY),
+            ((length, width), jnp.bfloat16, ANY),
+            ((4, columns, width), jnp.bfloat16, ANY),
+        ],
+        [*pieces, *weights, bias],
+        [ANY] * (4 + len(weights)) + [VMEM],
+        [
+            scratch(length, width), scratch(4, columns, width), scratch(3, length, columns),
+            pltpu.SemaphoreType.DMA((2,)), pltpu.SemaphoreType.DMA((3,)),
+        ],
+        6 * length * columns * width,
+    )
+
+
+def near_far(lefts, rights, name):
+    length = lefts[0].shape[0]
+    width = rights[0].shape[-1]
+    half = length // 2
+    count = length // 4
+    pairs = len(lefts)
+
+    def kernel(*refs):
+        left_refs, refs = refs[:pairs], refs[pairs:]
+        right_refs, refs = refs[:pairs], refs[pairs:]
+        near_ref, far_ref = refs
+        block = pl.program_id(0)
+        total = matmul(left_refs[0][...], right_refs[0][...], 1, 0)
+        for i in range(1, pairs):
+            total = total + matmul(left_refs[i][...], right_refs[i][...], 1, 0)
+        total = low(total)
+
+        @pl.when(block < 2)
+        def _():
+            near_ref[...] = total
+
+        @pl.when(block >= 2)
+        def _():
+            far_ref[...] = total
+
+    left_specs = [pl.BlockSpec((count, left.shape[1]), lambda i: (i, 0)) for left in lefts]
+    right_specs = []
+    for right, index in zip(rights, name[1]):
+        right_specs.append(pl.BlockSpec((None,) + right.shape[1:], lambda i, index=index: (index, 0, 0)))
+    return pl.pallas_call(
+        kernel,
+        grid=(4,),
+        in_specs=left_specs + right_specs,
+        out_specs=[
+            pl.BlockSpec((count, width), lambda i: (jnp.minimum(i, 1), 0)),
+            pl.BlockSpec((count, width), lambda i: (jnp.maximum(i - 2, 0), 0)),
+        ],
+        out_shape=[jax.ShapeDtypeStruct((half, width), jnp.bfloat16)] * 2,
+        cost_estimate=pl.CostEstimate(
+            flops=2 * pairs * length * lefts[0].shape[1] * width,
+            transcendentals=0,
+            bytes_accessed=2 * pairs * (length + width) * lefts[0].shape[1] + 2 * length * width,
+        ),
+        compiler_params=pltpu.CompilerParams(vmem_limit_bytes=LIMIT),
+        name=name[0],
+    )(*lefts, *rights)
+
+
+def gelu_pair(u):
+    k = 0.7978845608028654
+    t = jnp.tanh(k * (u + 0.044715 * (u * u * u)))
+    value = 0.5 * u * (1.0 + t)
+    slope = 0.5 * (1.0 + t) + 0.5 * u * (1.0 - t * t) * (k * (1.0 + 3 * 0.044715 * (u * u)))
+    return value, slope
+
+
+def mlp_main(rows, grads, weights, first, bias):
+    count, width = rows[0].shape
+    length = 4 * count
+    units = (weights[0].shape[0] - first) // 2
+    hidden = 8 * units
+    half = length // 2
+
+    def kernel(*refs):
+        row_refs, grad_refs, weight_refs, refs = refs[:4], refs[4:8], refs[8:16], refs[16:]
+        bias_ref, refs = refs[0], refs[1:]
+        rows_ref, grads_ref, hidden_ref, pre_ref, near_ref, far_ref, sum_ref = refs[:7]
+        rows_s, grads_s, fc_s, proj_s, hidden_s, slope_s, back_s, sems, outs = refs[7:]
+        fetch([w.at[pl.ds(first, units)] for w in weight_refs], fc_s, sems.at[0])
+        fetch(row_refs, rows_s, sems.at[1])
+        fetch([w.at[pl.ds(first + units, units)] for w in weight_refs], proj_s, sems.at[2])
+        fetch(grad_refs, grads_s, sems.at[3])
+        fetched(fc_s, sems.at[0])
+        fetched(rows_s, sems.at[1])
+        sent = [send(rows_s, rows_ref, outs.at[0])]
+
+        @pl.loop(0, 4)
+        def _(block):
+            at = pl.ds(pl.multiple_of(block * count, count), count)
+            value, slope = gelu_pair(matmul(rows_s[at, :], fc_s[...], 1, 1) + bias_ref[...])
+            hidden_s[at, :] = low(value)
+            slope_s[at, :] = low(slope)
+
+        sent.append(send(hidden_s, hidden_ref, outs.at[1]))
+        fetched(proj_s, sems.at[2])
+        fetched(grads_s, sems.at[3])
+        sent.append(send(grads_s, grads_ref, outs.at[2]))
+        sum_ref[...] = jnp.zeros_like(sum_ref)
+
+        @pl.loop(0, 4)
+        def _(block):
+            at = pl.ds(pl.multiple_of(block * count, count), count)
+            pre = low(matmul(grads_s[at, :], proj_s[...], 1, 1) * wide(slope_s[at, :]))
+            slope_s[at, :] = pre
+            sum_ref[...] += jnp.sum(wide(pre), axis=0, keepdims=True)
+            back_s[at, :] = low(matmul(pre, fc_s[...], 1, 0))
+
+        sent.append(send(slope_s, pre_ref, outs.at[3]))
+        sent.append(send(back_s.at[pl.ds(0, half)], near_ref, outs.at[4]))
+        sent.append(send(back_s.at[pl.ds(half, half)], far_ref, outs.at[5]))
+        for copy in sent:
+            copy.wait()
+
+    def out(rows, columns):
+        return ((rows, columns), jnp.bfloat16, ANY)
+
+    return matmul_call(
+        kernel,
+        "mlp_main",
+        [
+            out(length, width), out(length, width), out(length, hidden), out(length, hidden),
+            out(half, width), out(half, width), ((1, hidden), jnp.float32, VMEM),
+        ],
+        [*rows, *grads, *weights, bias],
+        [ANY] * 16 + [VMEM],
+        [
+            scratch(length, width), scratch(length, width), scratch(hidden, width), scratch(hidden, width),
+            scratch(length, hidden), scratch(length, hidden), scratch(length, width),
+            pltpu.SemaphoreType.DMA((4,)), pltpu.SemaphoreType.DMA((6,)),
+        ],
+        6 * length * hidden * width,
+    )
+
+
+def mlp_rest(rows, grads, hidden, pre, weights, first):
+    length, width = rows.shape
+    units = (weights[0].shape[0] - first) // 2
+    total = 8 * units
+    half = length // 2
+    count = length // 4
+    tile = 256
+
+    def kernel(*refs):
+        rows_ref, grads_ref, hidden_ref, pre_ref = refs[:4]
+        weight_refs, refs = refs[4:12], refs[12:]
+        near_ref, far_ref, fc_one, fc_two, proj_one, proj_two = refs[:6]
+        rows_s, grads_s, hidden_s, pre_s, proj_s, ahead_s, fc_s, back_s, sems, outs = refs[6:]
+        fetch([hidden_ref], hidden_s, sems.at[0])
+        fetch([w.at[pl.ds(first + units, units)] for w in weight_refs], proj_s, sems.at[1])
+        fetch([pre_ref], pre_s, sems.at[2])
+        fetch([rows_ref], rows_s, sems.at[3])
+        fetch([grads_ref], grads_s, sems.at[4])
+        fetched(hidden_s, sems.at[0])
+        fetched(proj_s, sems.at[1])
+
+        @pl.loop(0, 4)
+        def _(block):
+            at = pl.ds(pl.multiple_of(block * count, count), count)
+            ahead_s[at, :] = low(matmul(hidden_s[at, :], proj_s[...], 1, 0))
+
+        sent = [
+            send(ahead_s.at[pl.ds(0, half)], near_ref, outs.at[0]),
+            send(ahead_s.at[pl.ds(half, half)], far_ref, outs.at[1]),
+        ]
+        fetched(pre_s, sems.at[2])
+        fetched(rows_s, sems.at[3])
+
+        @pl.loop(0, total // tile)
+        def _(block):
+            at = pl.ds(pl.multiple_of(block * tile, tile), tile)
+            fc_s[at, :] = low(matmul(pre_s[:, at], rows_s[...], 0, 0))
+
+        sent.append(send(fc_s.at[pl.ds(0, total // 2)], fc_one, outs.at[2]))
+        sent.append(send(fc_s.at[pl.ds(total // 2, total // 2)], fc_two, outs.at[3]))
+        fetched(grads_s, sems.at[4])
+
+        @pl.loop(0, total // tile)
+        def _(block):
+            at = pl.ds(pl.multiple_of(block * tile, tile), tile)
+            back_s[at, :] = low(matmul(hidden_s[:, at], grads_s[...], 0, 0))
+
+        sent.append(send(back_s.at[pl.ds(0, total // 2)], proj_one, outs.at[4]))
+        sent.append(send(back_s.at[pl.ds(total // 2, total // 2)], proj_two, outs.at[5]))
+        for copy in sent:
+            copy.wait()
+
+    def out(rows):
+        return ((rows, width), jnp.bfloat16, ANY)
+
+    return matmul_call(
+        kernel,
+        "mlp_rest",
+        [out(half), out(half)] + [out(total // 2)] * 4,
+        [rows, grads, hidden, pre, *weights],
+        [ANY] * 12,
+        [
+            scratch(length, width), scratch(length, width), scratch(length, total), scratch(length, total),
+            scratch(total, width), scratch(length, width), scratch(total, width), scratch(total, width),
+            pltpu.SemaphoreType.DMA((5,)), pltpu.SemaphoreType.DMA((6,)),
+        ],
+        6 * length * total * width,
+    )
+
+
+def heads_back(pieces, weights):
+    count, width = pieces[0].shape
+    length = 4 * count
+    columns = weights.shape[1]
+
+    def kernel(*refs):
+        piece_refs, (weight_ref, grad_ref, all_ref, rows_s, out_s, sems, outs) = refs[:4], refs[4:]
+        fetch([weight_ref.at[3]], out_s, sems.at[0])
+        fetch(piece_refs, rows_s, sems.at[1])
+        fetched(out_s, sems.at[0])
+        fetched(rows_s, sems.at[1])
+        copy = send(rows_s, all_ref, outs.at[0])
+
+        @pl.loop(0, 4)
+        def _(block):
+            at = pl.ds(pl.multiple_of(block * count, count), count)
+            grad_ref[at, :] = low(matmul(rows_s[at, :], out_s[...], 1, 1))
+
+        copy.wait()
+
+    return matmul_call(
+        kernel,
+        "heads_back",
+        [((length, columns), jnp.bfloat16, VMEM), ((length, width), jnp.bfloat16, ANY)],
+        [*pieces, weights],
+        [ANY] * 5,
+        [
+            scratch(length, width), scratch(columns, width),
+            pltpu.SemaphoreType.DMA((2,)), pltpu.SemaphoreType.DMA((1,)),
+        ],
+        2 * length * columns * width,
+    )
+
+
+def head_weight_grads(lefts, rows, grad_rows, places, outs):
+    length, columns = lefts[0].shape
+    width = rows.shape[1]
+
+    def kernel(*refs):
+        left_refs, (rows_ref, grads_ref), refs = refs[:4], refs[4:6], refs[6:]
+        out_refs, (full_s, sem) = refs[: len(outs)], refs[len(outs) :]
+        for matrix in range(4):
+            right = (rows_ref if matrix < 3 else grads_ref)[...]
+            full_s[matrix] = low(matmul(left_refs[matrix][...], right, 0, 0))
+        for array, index, row, matrix, column, count in places:
+            into = out_refs[array]
+            into = into if index is None else into.at[index]
+            pltpu.make_async_copy(
+                full_s.at[matrix, pl.ds(column, count)], into.at[pl.ds(row, count)], sem.at[0]
+            ).start()
+        pltpu.make_async_copy(full_s, full_s, sem.at[0]).wait()
+
+    return matmul_call(
+        kernel,
+        "head_weight_grads",
+        [(shape, jnp.bfloat16, ANY) for shape in outs],
+        [*lefts, rows, grad_rows],
+        [VMEM] * 6,
+        [scratch(4, columns, width), pltpu.SemaphoreType.DMA((1,))],
+        8 * length * columns * width,
+    )
+
+
+def teacher_blocks(qkv, out, fc, proj):
+    columns, shard = out.shape
+    stack = jnp.concatenate([jnp.transpose(qkv, (0, 2, 1)), out[None]], axis=0)
+    stack = stack.reshape(4, 2, columns // (2 * HD), 2, 2, HD // 4, shard)
+    stack = jnp.transpose(stack, (3, 1, 4, 0, 2, 5, 6)).reshape(8, -1, shard)
+    return jnp.concatenate(
+        [stack, jnp.transpose(fc).reshape(8, -1, shard), proj.reshape(8, -1, shard)], axis=1
+    )
+
+
+def teacher_unblock(heads, hidden):
+    shard = heads.shape[-1]
+    stack = heads.reshape(2, 2, 2, 4, -1, HD // 4, shard)
+    stack = jnp.transpose(stack, (3, 1, 4, 0, 2, 5, 6)).reshape(4, -1, shard)
+    hidden = hidden.reshape(8, 2, -1, shard)
+    return stack, hidden[:, 0].reshape(-1, shard), hidden[:, 1].reshape(-1, shard)
+
+
+def student_blocks(qkv, out, fc, proj):
+    columns, shard = out.shape
+    stack = jnp.concatenate([jnp.transpose(qkv, (0, 2, 1)), out[None]], axis=0)
+    stack = stack.reshape(4, columns // HD, 8, HD // 8, shard)
+    stack = jnp.transpose(stack, (2, 0, 1, 3, 4)).reshape(8, -1, shard)
+    return jnp.concatenate(
+        [stack, jnp.transpose(fc).reshape(8, -1, shard), proj.reshape(8, -1, shard)], axis=1
+    )
+
+
+def student_unblock(heads, hidden):
+    shard = heads.shape[-1]
+    stack = jnp.transpose(heads.reshape(8, 4, -1, HD // 8, shard), (1, 2, 0, 3, 4)).reshape(4, -1, shard)
+    hidden = hidden.reshape(8, 2, -1, shard)
+    return stack, hidden[:, 0].reshape(-1, shard), hidden[:, 1].reshape(-1, shard)
+
+
+def hidden_sum(fc_near, fc_far, proj_near, proj_far, start=None):
+    units = fc_near.shape[0] // 4
+    fc_got, proj_got = swap(fc_far, "y"), swap(proj_far, "y")
+    parts = []
+    for k in range(4):
+        at = slice(k * units, (k + 1) * units)
+        parts.append(
+            jnp.concatenate(
+                [wide(fc_near[at]) + wide(fc_got[at]), wide(proj_near[at]) + wide(proj_got[at])], axis=0
+            )
+        )
+    return ring_sum(parts)
+
+
+def teacher_places(columns):
+    sub = HD // 4
+    heads = columns // (2 * HD)
+    places = []
+    for matrix in range(4):
+        for plane in range(2):
+            for head in range(heads):
+                for dc in range(2):
+                    for dy in range(2):
+                        column = (plane * heads + head) * HD + (dc * 2 + dy) * sub
+                        places.append((dc * 2 + dy, plane, (matrix * heads + head) * sub, matrix, column, sub))
+    return places
+
+
+def student_places(columns):
+    sub = HD // 8
+    heads = columns // HD
+    places = []
+    for matrix in range(4):
+        for head in range(heads):
+            for part in range(8):
+                places.append((part, None, (matrix * heads + head) * sub, matrix, head * HD + part * sub, sub))
+    return places
+
+
+def student_grad_places(columns):
+    return [(p // 4, p % 4, row, matrix, column, sub) for p, _, row, matrix, column, sub in student_places(columns)]
+
+
+def teacher_heads(piece, pos):
+    first = pos["c"] == 0
+    held = ring_pieces(piece)
+    over = [swap(part, "y") for part in held]
+
+    def halves(parts):
+        front, rear = jnp.stack(parts[:2]), jnp.stack(parts[2:])
+        return jnp.where(first, front, rear), swap(jnp.where(first, rear, front), "c")
+
+    own, near = halves(held)
+    own_over, near_over = halves(over)
+    return held, (own, own_over, near, near_over)
+
+
+def teacher_heads_sum(parts, pos):
+    first = pos["c"] == 0
+
+    def planes(own, give):
+        got = swap(give, "c")
+        return jnp.where(first, own, got), jnp.where(first, got, own)
+
+    front, rear = planes(parts[0], parts[2])
+    front_over, rear_over = planes(parts[1], parts[3])
+    front_got, rear_got = swap(front_over, "y"), swap(rear_over, "y")
+    sums = [wide(front[k]) + wide(front_got[k]) for k in range(2)]
+    sums += [wide(rear[k]) + wide(rear_got[k]) for k in range(2)]
+    return ring_sum(sums)
+
+
+def student_heads_sum(near, far):
+    got = swap(far, "y")
+    return ring_sum([wide(near[k]) + wide(got[k]) for k in range(4)])
+
+
+def block_front(rows, vectors, keep, qv_bias, info, head_weights, places, columns):
+    gain_one, shift_one = vectors[:2]
+    full16 = (rows.shape, jnp.bfloat16)
+    (normed,) = row_call(first_norm_kernel, "first_norm", [full16], rows, gain_one, shift_one)
+    bias3 = jnp.stack([qv_bias[0], jnp.zeros_like(qv_bias[0]), qv_bias[1]])[:, None, :]
+    qkv, normed_all, weights = project(gather_tokens(normed), head_weights, places, bias3, columns)
+    heads_low, logs = attend(info, keep, qkv)
+    near, far = near_far([heads_low], [weights], ("out_project", (3,)))
+    return scatter_tokens(near, far), (qkv, normed_all, weights, heads_low, logs)
+
+
+def block_middle(rows, branch, grad_all, vectors, fc_bias, hidden_weights, first):
+    bias_out, gain_two, shift_two = vectors[2:5]
+    full32, full16 = (rows.shape, jnp.float32), (rows.shape, jnp.bfloat16)
+    middle, normed_two = row_call(
+        mid_norm_kernel, "mid_norm", [full32, full16], rows, *branch, bias_out, gain_two, shift_two
+    )
+    rows_all, grads_all, hidden, pre, near, far, fc_bias_grad = mlp_main(
+        gather_tokens(normed_two), grad_all, hidden_weights, first, fc_bias
+    )
+    return middle, scatter_tokens(near, far), (rows_all, grads_all, hidden, pre), fc_bias_grad[0]
+
+
+def block_ahead(middle, saved, hidden_weights, first, bias_proj):
+    near, far, *grads = mlp_rest(*saved, hidden_weights, first)
+    near, got, over = scatter_tokens(near, far)
+    count = middle.shape[0]
+    ahead = wide(near[:count]) + wide(got[:count]) + wide(over)
+    return low(middle + (ahead + bias_proj)), grads
+
+
+def block_turn(grad_rows, back, middle, gain_two):
+    width = middle.shape[1]
+    full32, full16 = (middle.shape, jnp.float32), (middle.shape, jnp.bfloat16)
+    return row_call(
+        mid_back_kernel, "mid_back", [full32, full16, ((4, width), jnp.float32)], grad_rows, *back, middle, gain_two
+    )
+
+
+def block_back(attn_grad, saved, keep, info):
+    qkv, normed_all, weights, heads_low, logs = saved
+    heads_grad, attn_grad_all = heads_back(gather_tokens(attn_grad), weights)
+    dq, dk, dv = attend_back(info, keep, qkv, heads_low, heads_grad, logs)
+    near, far = near_far([dq, dk, dv], [weights] * 3, ("rows_back", (0, 1, 2)))
+    return scatter_tokens(near, far), (dq, dk, dv, heads_low, normed_all, attn_grad_all)
+
+
+def block_head_grads(saved, places, outs):
+    dq, dk, dv, heads_low, normed_all, attn_grad_all = saved
+    grads = head_weight_grads([dq, dk, dv, heads_low], normed_all, attn_grad_all, places, outs)
+    qv_bias_grad = jnp.stack([jnp.sum(wide(dq), axis=0), jnp.sum(wide(dv), axis=0)])
+    return grads, qv_bias_grad
+
+
+def block_end(back, rows, dmid, gain_one):
+    width = rows.shape[1]
+    return row_call(
+        first_back_kernel, "first_back", [(rows.shape, jnp.bfloat16), ((2, width), jnp.float32)],
+        *back, rows, dmid, gain_one,
+    )
+
+
+def on_pairs(*args):
+    teacher_in, student_in = args[0:14], args[14:28]
+    span_starts, head_slots = args[28], args[29]
+    pos = {name: lax.axis_index(name) for name in EVERY}
+    rank = pos["x"] * 2 + pos["c"]
+
+    teacher_piece = plane_out(teacher_blocks(teacher_in[4], teacher_in[6], teacher_in[10], teacher_in[12]))
+    student_piece = plane_out(student_blocks(student_in[4], student_in[6], student_in[10], student_in[12]))
+    teacher_columns, student_columns = teacher_in[6].shape[0], student_in[6].shape[0]
+    teacher_rows = cross(teacher_in[0][0])
+    student_rows = cross(student_in[0][0])
+    head_rows = student_columns // 2
+    teacher_head_rows = teacher_columns // 2
+    held, teacher_head_weights = teacher_heads(teacher_piece[:teacher_head_rows], pos)
+    student_piece = jnp.concatenate([cross(student_piece[:head_rows]), student_piece[head_rows:]], axis=0)
+    student_piece = after(student_piece, held[2])
+    held = ring_pieces(student_piece)
+    student_weights = held + [swap(piece, "y") for piece in held]
+    hidden_piece = after(teacher_piece[teacher_head_rows:], held[2])
+    held = ring_pieces(hidden_piece)
+    teacher_weights = held + [swap(piece, "y") for piece in held]
+    teacher_up, student_up = cross(after(teacher_in[1][0], held[1])), cross(after(student_in[1][0], held[1]))
+    teacher_grad_all, student_grad_all = gather_tokens(teacher_up), gather_tokens(student_up)
+
+    order = (2, 3, 7, 8, 9, 13)
+    tall = jnp.concatenate(
+        [jnp.stack([block[i] for i in order]) for block in (teacher_in, student_in)], axis=1
+    )
+    marks = jnp.stack([span_starts[0] // 32, span_starts[0] % 32]).astype(jnp.bfloat16)
+    packed = jnp.concatenate([tall, jnp.broadcast_to(marks[:, None], (2, tall.shape[1]))], axis=0)[None]
+    for axis in ("c", "x", "y"):
+        other = swap(packed, axis)
+        here = pos[axis] == 0
+        packed = jnp.concatenate([jnp.where(here, packed, other), jnp.where(here, other, packed)], axis=0)
+    shard = teacher_in[2].shape[0]
+
+    def width_vectors(block):
+        block = wide(jnp.transpose(block[:, :6], (1, 0, 2)).reshape(6, 1, -1))
+        return tuple(block[i] for i in range(6))
+
+    teacher_vectors = width_vectors(packed[:, :, :shard])
+    student_vectors = width_vectors(packed[:, :, shard:])
+    starts = packed[:, 6:, 0].astype(jnp.int32)
+    starts = starts[:, 0] * 32 + starts[:, 1]
+    info = jnp.stack([pick(starts, pos["y"] * 4 + pos["z"]), rank])
+
+    parts = [
+        teacher_in[11], teacher_in[5].reshape(-1), student_in[11], student_in[5].reshape(-1),
+        jnp.pad(head_slots.astype(jnp.bfloat16), (0, 128 - head_slots.shape[0])),
+    ]
+    limits = np.cumsum([0] + [part.shape[0] // 128 for part in parts])
+    deep = jnp.concatenate([part.reshape(-1, 128) for part in parts], axis=0)
+    deep = jnp.stack([deep] + [ring(deep, step) for step in (1, 2, 3)])
+    deep = [deep[:, limits[i] : limits[i + 1]].reshape(4, -1) for i in range(5)]
+    y, x, c, z = pos["y"], pos["x"], pos["c"], pos["z"]
+    near_y = jnp.stack([y, 1 - y])
+    near_c = jnp.stack([c, 1 - c])
+    planes = (z - jnp.arange(4)) % 4
+    device_of = near_y * 4 + rank
+    hidden_hot = (jnp.arange(8)[None] == device_of[:, None]).astype(jnp.bfloat16)
+
+    def hidden_bias(block):
+        block = block.reshape(4, 8, -1)
+        return jnp.einsum("dp,kpi->dki", hidden_hot, block, preferred_element_type=jnp.float32).reshape(1, -1)
+
+    teacher_fc_bias, student_fc_bias = hidden_bias(deep[0]), hidden_bias(deep[2])
+    two = jnp.where(c == 0, 0, 2)
+    block = lax.dynamic_slice_in_dim(deep[1].reshape(4, -1), two, 2, 0)
+    block = block.reshape(2, 2, 2, -1, 2, 2, HD // 4)
+    block = pick(block, x, 2)
+    block = jnp.where(y == 0, block, block[:, :, :, ::-1])
+    block = jnp.where(c == 0, block, block[:, :, :, :, ::-1])
+    teacher_qv = wide(jnp.transpose(block, (1, 0, 2, 4, 3, 5)).reshape(2, -1))
+    slots = lax.dynamic_slice_in_dim(deep[4][:, : head_slots.shape[0]], two, 2, 0)
+    keep = wide(pick(slots.reshape(2, 2, -1), x, 1).reshape(-1))
+    block = pick(deep[3].reshape(4, 2, -1, 8, HD // 8), (z - rank) % 4)
+    eighth = (near_y[:, None] * 4 + planes[None]).reshape(-1)
+    order_hot = (jnp.arange(8)[None] == eighth[:, None]).astype(jnp.bfloat16)
+    student_qv = jnp.einsum("rp,thpi->thri", order_hot, block, preferred_element_type=jnp.float32).reshape(2, -1)
+    ones = jnp.ones((student_qv.shape[1] // HD,), jnp.float32)
+
+    teacher_spots, student_spots = teacher_places(teacher_columns), student_places(student_columns)
+    teacher_branch, teacher_saved = block_front(
+        teacher_rows, teacher_vectors, keep, teacher_qv, info, teacher_head_weights, teacher_spots, teacher_columns
+    )
+    student_branch, student_saved = block_front(
+        student_rows, student_vectors, ones, student_qv, info, student_weights, student_spots, student_columns
+    )
+    teacher_middle, teacher_back, teacher_mlp, teacher_fc = block_middle(
+        teacher_rows, teacher_branch, teacher_grad_all, teacher_vectors, teacher_fc_bias, teacher_weights, 0
+    )
+    student_middle, student_back, student_mlp, student_fc = block_middle(
+        student_rows, student_branch, student_grad_all, student_vectors, student_fc_bias, student_weights, head_rows
+    )
+    teacher_dmid, teacher_ga, teacher_two = block_turn(teacher_up, teacher_back, teacher_middle, teacher_vectors[3])
+    student_dmid, student_ga, student_two = block_turn(student_up, student_back, student_middle, student_vectors[3])
+    teacher_out, teacher_hidden = block_ahead(
+        teacher_middle, teacher_mlp, teacher_weights, 0, teacher_vectors[5]
+    )
+    student_out, student_hidden = block_ahead(
+        student_middle, student_mlp, student_weights, head_rows, student_vectors[5]
+    )
+    teacher_back, teacher_saved = block_back(teacher_ga, teacher_saved, keep, info)
+    student_back, student_saved = block_back(student_ga, student_saved, ones, info)
+    teacher_dx, teacher_one = block_end(teacher_back, teacher_rows, teacher_dmid, teacher_vectors[0])
+    student_dx, student_one = block_end(student_back, student_rows, student_dmid, student_vectors[0])
+
+    teacher_width, student_width = teacher_rows.shape[1], student_rows.shape[1]
+    teacher_hidden = plane_back(low(hidden_sum(*teacher_hidden)))
+    teacher_head, teacher_qv_grad = block_head_grads(
+        teacher_saved, teacher_spots, [(2, teacher_head_rows, teacher_width)] * 4
+    )
+    teacher_head = plane_back(low(teacher_heads_sum(teacher_head, pos)))
+    teacher_grads = teacher_unblock(teacher_head, teacher_hidden)
+    student_hidden = low(hidden_sum(*student_hidden))
+    student_head, student_qv_grad = block_head_grads(
+        student_saved, student_grad_places(student_columns), [(4, head_rows, student_width)] * 2
+    )
+    student_head = cross(low(student_heads_sum(*student_head)))
+    got = plane_back(jnp.concatenate([student_head, student_hidden], axis=0))
+    student_grads = student_unblock(got[:, :head_rows], got[:, head_rows:])
+    student_out, student_dx = cross(student_out)[None], cross(student_dx)[None]
+    teacher_out, teacher_dx = cross(teacher_out)[None], cross(teacher_dx)[None]
+
+    def matrices(grads):
+        stack, fc_grad, proj_grad = grads
+        return (
+            wide(jnp.transpose(stack[:3], (0, 2, 1))), wide(stack[3]),
+            wide(jnp.transpose(fc_grad)), wide(proj_grad),
+        )
+
+    def spread(places, values):
+        hot = (jnp.arange(32)[:, None] == places[None]).astype(jnp.float32)
+        return jnp.dot(hot, values, precision=lax.Precision.HIGHEST)
+
+    hidden_places = (planes[None] * 8 + near_y[:, None] * 4 + rank).reshape(-1)
+    head_planes = planes.reshape(2, 2)
+    head_planes = jnp.where(c == 0, head_planes[0], head_planes[1])
+    teacher_spots = (
+        head_planes[:, None, None] * 8 + x * 4 + near_y[None, None, :] * 2 + near_c[None, :, None]
+    ).reshape(-1)
+    student_spots = rank * 8 + eighth
+
+    teacher_qv_grad = teacher_qv_grad.reshape(2, 2, -1, 2, 2, HD // 4)
+    teacher_qv_grad = jnp.transpose(teacher_qv_grad, (1, 3, 4, 0, 2, 5)).reshape(8, -1)
+    student_qv_grad = jnp.transpose(student_qv_grad.reshape(2, -1, 8, HD // 8), (2, 0, 1, 3)).reshape(8, -1)
+    pieces = [
+        spread(hidden_places, teacher_fc.reshape(8, -1)),
+        spread(hidden_places, student_fc.reshape(8, -1)),
+        spread(teacher_spots, teacher_qv_grad),
+        spread(student_spots, student_qv_grad),
+        teacher_one, teacher_two, student_one, student_two,
+    ]
+    limits = np.cumsum([0] + [piece.size for piece in pieces])
+    total = sum_everywhere(jnp.concatenate([piece.reshape(-1, 128) for piece in pieces], axis=0))
+    total = total.reshape(-1)
+    parts = [total[limits[i] : limits[i + 1]] for i in range(8)]
+    own = y * 4 + rank
+    teacher_fc = pick(parts[0].reshape(4, -1), z)
+    student_fc = pick(parts[1].reshape(4, -1), z)
+    block = pick(parts[2].reshape(4, 2, 2, 2, 2, -1, HD // 4), z)
+    teacher_qv_grad = jnp.transpose(block, (3, 0, 4, 1, 2, 5)).reshape(2, -1)
+    block = pick(parts[3].reshape(4, 8, 2, -1, HD // 8), z)
+    student_qv_grad = jnp.transpose(block, (1, 2, 0, 3)).reshape(2, -1)
+
+    def width_grads(one, two):
+        one = pick(one.reshape(2, 8, -1), own, 1)
+        two = pick(two.reshape(4, 8, -1), own, 1)
+        return one[0], one[1], two[0], two[1], two[2], two[3]
+
+    def arranged(outputs, input_grad, grads, sums, qv_grad, fc_grad):
+        return (
+            outputs, input_grad, sums[0], sums[1], grads[0], qv_grad, grads[1],
+            sums[2], sums[3], sums[4], grads[2], fc_grad, grads[3], sums[5],
+        )
+
+    return arranged(
+        teacher_out, teacher_dx, matrices(teacher_grads), width_grads(parts[4], parts[5]), teacher_qv_grad, teacher_fc
+    ) + arranged(
+        student_out, student_dx, matrices(student_grads), width_grads(parts[6], parts[7]), student_qv_grad, student_fc
+    )
+
+
+def on_plane(spec):
+    names = {"dp": PLANE, "tensor": "z"}
+    return P(*(names.get(entry, None) for entry in spec))
+
+
 def solution(mesh):
     in_specs = (
         P("dp", "tensor", None),
@@ -442,6 +1518,15 @@
         P("tensor", "dp"),
         P("dp"),
     )
+    if tuple(mesh.devices.shape) == (8, 4):
+        finer = Mesh(mesh.devices.reshape(2, 2, 2, 4), EVERY)
+        return jax.shard_map(
+            on_pairs,
+            mesh=finer,
+            in_specs=tuple(on_plane(spec) for spec in in_specs),
+            out_specs=tuple(on_plane(spec) for spec in out_specs),
+            check_vma=False,
+        )
     return jax.shard_map(
         on_device, mesh=mesh, in_specs=in_specs, out_specs=out_specs, check_vma=False
     )

time: 1430 us -> 887 us (0.62)
  the two profiles are of different devices: /device:TPU:0 before, /device:TPU:16 now
where the time goes in v1:
time: 887 us; the launch traced here: 875 us
  waiting for transfers between devices  299 us (34%)
  Pallas kernels  234 us (26%)
  starting transfers between devices  184 us (21%)
  local copies, waits for them, and re-layouts  86.3 us (10%)
  other arithmetic  67.8 us (8%)
    ppermute x69, waiting for transfers between devices, swap(): return lax.ppermute(values, axis, ((0, 1), (1, 0)))  166 us
    pallas_call x10, Pallas kernels, matmul_call(): pl.pallas_call(kernel, in_specs=specs, out_specs=[spec for _, _, spec in...  96.1 us
    ppermute x24, waiting for transfers between devices, ring(): lax.ppermute(values, 'z', tuple(((i, (i + step) % 4) for i in range(4))))  59.1 us
    all_to_all x3, starting transfers between devices, plane_back(): return lax.all_to_all(split, PLANE, 0, 0)  55.8 us
    ppermute x69, starting transfers between devices, swap(): return lax.ppermute(values, axis, ((0, 1), (1, 0)))  46.3 us
    pallas_call x2, Pallas kernels, attend_back(): pl.pallas_call(functools.partial(backward_kernel, group=group, blocks=blo...  45.9 us
    ppermute x10, starting transfers between devices, cross(): return lax.ppermute(values, EVERY, pairs)  45.4 us
    pallas_call x2, Pallas kernels, attend(): pl.pallas_call(functools.partial(forward_kernel, group=group, blocks=bloc...  42.6 us
  transfers between devices with their start and end apart: 110, of which 40 were waited for; matrix products, arithmetic and copies ran while one was open for 15% of the time, Pallas kernels for 27%

profile of v1, /device:TPU:16, one launch (start us, length us, event | category | flops | bytes accessed | tf_op | source)
XLA Modules:
  0.0 874.8 jit_solution(15448461749891954236)
XLA Ops:
  38.6 22.5 %all-to-all-done = bf16[8,512,160]{1,2,0:T(8,128)(2,1)S(1)} async-done(((bf16[8,512,160]{1,2,0:T(8,128)(2,1)}), bf16[8,512,160]{1,2,0:T(8,128)(2,1)S(1)}, u32[]{:S(2)}, u32[]{:S(2)}) %all-to-all-start) | async-done | bytes 1310752 | tf_op jit(solution)/shard_map/all_to_all | solution.py:443
  159.3 10.6 %collective-permute-done.16 = bf16[192,1280]{1,0:T(8,128)(2,1)} collective-permute-done((bf16[192,1280]{1,0:T(8,128)(2,1)}, bf16[192,1280]{1,0:T(8,128)(2,1)}, u32[]{:S(2)}, u32[]{:S(2)}) %collective-permute-start.16) | collective-permute-done | bytes 491552 | tf_op jit(solution)/shard_map/ppermute | solution.py:394
  179.4 9.5 %collective-permute-done.56.refs_10_.refs_14_ = bf16[288,768]{1,0:T(8,128)(2,1)} collective-permute-done((bf16[288,768]{1,0:T(8,128)(2,1)}, bf16[288,768]{1,0:T(8,128)(2,1)}, u32[]{:S(2)}, u32[]{:S(2)}) %collective-permute-start.56) | collective-permute-done | bytes 442400 | tf_op jit(solution)/shard_map/ppermute | solution.py:394
  203.7 13.5 %attend.3 = (bf16[1024,192]{1,0:T(8,128)(2,1)}, f32[1,3,1024]{2,1,0:T(4,128)}) custom-call(s32[2]{0:T(128)} %pad_add_fusion.info_ref, f32[3]{0:T(128)} %broadcast_12_keep_ref.2.keep_ref, bf16[3,1024,192]{2,1,0:T(8,128)(2,1)} %get-tuple-element.135.q_ref.k_ref.v_ref, bf16[3,1024,192]{2,1,0:T(8,128)(2,1)} %get-tuple-element.135.q_ref.k_ref.v_ref, ...), custom_call_target="tpu_custom_call" | custom-call | flops 1610612736 | bytes 1966080 | tf_op jit(solution)/shard_map/attend/pallas_call | solution.py:703
  231.1 9.9 %project.2 = (bf16[3,1024,384]{2,1,0:T(8,128)(2,1)}, bf16[1024,1280]{1,0:T(8,128)(2,1)}, bf16[4,384,1280]{2,1,0:T(8,128)(2,1)}) custom-call(bf16[256,1280]{1,0:T(8,128)(2,1)} %first_norm.2.refs_0_, bf16[256,1280]{1,0:T(8,128)(2,1)} %collective-permute-done.7.refs_1_, bf16[256,1280]{1,0:T(8,128)(2,1)} %collective-permute-done.8.refs_2_, ...), custom_call_target="tpu_custom_call" | custom-call | flops 3019898880 | bytes 13116416 | tf_op jit(solution)/shard_map/project/pallas_call | solution.py:778
  250.0 29.1 %attend.2 = (bf16[1024,384]{1,0:T(8,128)(2,1)}, f32[3,2,1024]{2,1,0:T(2,128)}) custom-call(s32[2]{0:T(128)} %pad_add_fusion.info_ref, f32[6]{0:T(128)} %reshape.602.keep_ref, bf16[3,1024,384]{2,1,0:T(8,128)(2,1)} %get-tuple-element.106.q_ref.k_ref.v_ref, bf16[3,1024,384]{2,1,0:T(8,128)(2,1)} %get-tuple-element.106.q_ref.k_ref.v_ref, ...), custom_call_target="tpu_custom_call" | custom-call | flops 3221225472 | bytes 3932160 | tf_op jit(solution)/shard_map/attend/pallas_call | solution.py:703
  290.1 11.5 %mlp_main.3 = (bf16[1024,768]{1,0:T(8,128)(2,1)}, bf16[1024,768]{1,0:T(8,128)(2,1)}, bf16[1024,768]{1,0:T(8,128)(2,1)}, bf16[1024,768]{1,0:T(8,128)(2,1)}, bf16[...) custom-call(bf16[256,768]{1,0:T(8,128)(2,1)} %get-tuple-element.140.refs_0_, ...), custom_call_target="tpu_custom_call" | custom-call | flops 3623878656 | bytes 13375488 | tf_op jit(solution)/shard_map/mlp_main/pallas_call | solution.py:778
  329.8 30.8 %collective-permute-done.28.refs_4_.g_ref = bf16[256,1280]{1,0:T(8,128)(2,1)} collective-permute-done((bf16[256,1280]{1,0:T(8,128)(2,1)}, bf16[256,1280]{1,0:T(8,128)(2,1)}, u32[]{:S(2)}, u32[]{:S(2)}) %collective-permute-start.28) | collective-permute-done | bytes 655392 | tf_op jit(solution)/shard_map/ppermute | solution.py:405
  370.4 9.8 %collective-permute-done.35.refs_13_.refs_9_ = bf16[320,1280]{1,0:T(8,128)(2,1)} collective-permute-done((bf16[320,1280]{1,0:T(8,128)(2,1)}, bf16[320,1280]{1,0:T(8,128)(2,1)}, u32[]{:S(2)}, u32[]{:S(2)}) %collective-permute-start.35) | collective-permute-done | bytes 819232 | tf_op jit(solution)/shard_map/ppermute | solution.py:394
  387.9 19.6 %collective-permute-done.103 = bf16[192,768]{1,0:T(8,128)(2,1)S(1)} collective-permute-done((bf16[192,768]{1,0:T(8,128)(2,1)S(1)}, bf16[192,768]{1,0:T(8,128)(2,1)S(1)}, u32[]{:S(2)}, u32[]{:S(2)}) %collective-permute-start.103) | collective-permute-done | bytes 294944 | tf_op jit(solution)/shard_map/ppermute | solution.py:398
  427.8 12.6 %collective-permute-start.93 = (bf16[256,768]{1,0:T(8,128)(2,1)S(1)}, bf16[256,768]{1,0:T(8,128)(2,1)S(1)}, u32[]{:S(2)}, u32[]{:S(2)}) collective-permute-start(bf16[256,768]{1,0:T(8,128)(2,1)S(1)} %add_convert_fusion.8), channel_id=1, source_target_pairs={{0,0},{1,4},{2,8},{3,12},{4,1},{5,5},{6,9},{7,13},{8,2},{9,6},{10,... | collective-permute-start | bytes 1179656 | tf_op jit(solution)/shard_map/ppermute | solution.py:405
  440.5 20.0 %mlp_main.2 = (bf16[1024,1280]{1,0:T(8,128)(2,1)}, bf16[1024,1280]{1,0:T(8,128)(2,1)}, bf16[1024,1280]{1,0:T(8,128)(2,1)}, bf16[1024,1280]{1,0:T(8,128)(2,1)}, b...) custom-call(bf16[256,1280]{1,0:T(8,128)(2,1)} %get-tuple-element.112.refs_0_, ...), custom_call_target="tpu_custom_call" | custom-call | flops 10066329600 | bytes 23603200 | tf_op jit(solution)/shard_map/mlp_main/pallas_call | solution.py:778
  465.5 16.1 %attend_back.3 = (bf16[1024,192]{1,0:T(8,128)(2,1)}, bf16[1024,192]{1,0:T(8,128)(2,1)}, bf16[1024,192]{1,0:T(8,128)(2,1)}) custom-call(s32[2]{0:T(128)} %pad_add_fusion.info_ref, f32[3]{0:T(128)} %broadcast_12_keep_ref.2.keep_ref, bf16[3,1024,192]{2,1,0:T(8,128)(2,1)} %get-tuple-element.135.q_ref.k_ref.v_ref, ...), custom_call_target="tpu_custom_call" | custom-call | flops 4026531840 | bytes 3932160 | tf_op jit(solution)/shard_map/attend_back/pallas_call | solution.py:729
  487.1 17.5 %mlp_rest.2 = (bf16[512,1280]{1,0:T(8,128)(2,1)}, bf16[512,1280]{1,0:T(8,128)(2,1)}, bf16[640,1280]{1,0:T(8,128)(2,1)}, bf16[640,1280]{1,0:T(8,128)(2,1)}, bf16[...) custom-call(bf16[1024,1280]{1,0:T(8,128)(2,1)} %get-tuple-element.116.refs_0_, ...), custom_call_target="tpu_custom_call" | custom-call | flops 10066329600 | bytes 34078720 | tf_op jit(solution)/shard_map/mlp_rest/pallas_call | solution.py:778
  552.8 26.6 %collective-permute-done.86 = bf16[640,1280]{1,0:T(8,128)(2,1)S(1)} collective-permute-done((bf16[640,1280]{1,0:T(8,128)(2,1)}, bf16[640,1280]{1,0:T(8,128)(2,1)S(1)}, u32[]{:S(2)}, u32[]{:S(2)}) %collective-permute-start.86) | collective-permute-done | bytes 1638432 | tf_op jit(solution)/shard_map/ppermute | solution.py:394
  616.4 17.2 %collective-permute-done.43.refs_1_ = bf16[256,1280]{1,0:T(8,128)(2,1)} collective-permute-done((bf16[256,1280]{1,0:T(8,128)(2,1)}, bf16[256,1280]{1,0:T(8,128)(2,1)}, u32[]{:S(2)}, u32[]{:S(2)}) %collective-permute-start.43) | collective-permute-done | bytes 655392 | tf_op jit(solution)/shard_map/ppermute | solution.py:394
  636.7 8.7 collective-permute-start.90
  651.2 29.8 %attend_back.2 = (bf16[1024,384]{1,0:T(8,128)(2,1)}, bf16[1024,384]{1,0:T(8,128)(2,1)}, bf16[1024,384]{1,0:T(8,128)(2,1)}) custom-call(s32[2]{0:T(128)} %pad_add_fusion.info_ref, f32[6]{0:T(128)} %reshape.602.keep_ref, bf16[3,1024,384]{2,1,0:T(8,128)(2,1)} %get-tuple-element.106.q_ref.k_ref.v_ref, ...), custom_call_target="tpu_custom_call" | custom-call | flops 8053063680 | bytes 7864320 | tf_op jit(solution)/shard_map/attend_back/pallas_call | solution.py:729
  695.4 9.7 %head_weight_grads.2 = (bf16[2,192,1280]{2,1,0:T(8,128)(2,1)}, bf16[2,192,1280]{2,1,0:T(8,128)(2,1)}, bf16[2,192,1280]{2,1,0:T(8,128)(2,1)}, bf16[2,192,1280]{2,1,0:T(8,128)(2,1)}) custom-call(bf16[1024,384]{1,0:T(8,128)(2,1)} %get-tuple-element.127.refs_0_, bf16[1024,384]{1,0:T(8,128)(2,1)} %get-tuple-element.128.refs_1_, ...), custom_call_target="tpu_custom_call" | custom-call | flops 4026531840 | bytes 16777216 | tf_op jit(solution)/shard_map/head_weight_grads/pallas_call | solution.py:778
  708.3 23.3 %all-to-all-start.3 = ((bf16[8,320,160]{1,2,0:T(8,128)(2,1)}), bf16[8,320,160]{1,2,0:T(8,128)(2,1)S(1)}, u32[]{:S(2)}, u32[]{:S(2)}) async-start(bf16[8,320,160]{1,2,0:T(8,128)(2,1)} %bitcast.91), calls=%async_computation.3 | async-start | bytes 1966080 | tf_op jit(solution)/shard_map/all_to_all | solution.py:449
  739.7 20.2 %collective-permute-done.47.c_ref = bf16[256,1280]{1,0:T(8,128)(2,1)S(1)} collective-permute-done((bf16[256,1280]{1,0:T(8,128)(2,1)}, bf16[256,1280]{1,0:T(8,128)(2,1)S(1)}, u32[]{:S(2)}, u32[]{:S(2)}) %collective-permute-start.47) | collective-permute-done | bytes 655392 | tf_op jit(solution)/shard_map/ppermute | solution.py:394
  776.8 12.8 %collective-permute-done.76 = f32[196,128]{1,0:T(8,128)S(1)} collective-permute-done((f32[196,128]{1,0:T(8,128)S(1)}, f32[196,128]{1,0:T(8,128)S(1)}, u32[]{:S(2)}, u32[]{:S(2)}) %collective-permute-start.76) | collective-permute-done | bytes 100384 | tf_op jit(solution)/shard_map/ppermute | solution.py:394
  826.2 28.9 %all-to-all-start.2 = ((bf16[8,192,160]{1,2,0:T(8,128)(2,1)}), bf16[8,192,160]{1,2,0:T(8,128)(2,1)S(1)}, u32[]{:S(2)}, u32[]{:S(2)}) async-start(bf16[8,192,160]{1,2,0:T(8,128)(2,1)} %bitcast.77), calls=%async_computation.2 | async-start | bytes 1310720 | tf_op jit(solution)/shard_map/all_to_all | solution.py:449
  857.3 8.9 %all-to-all-done.2 = bf16[8,192,160]{1,2,0:T(8,128)(2,1)S(1)} async-done(((bf16[8,192,160]{1,2,0:T(8,128)(2,1)}), bf16[8,192,160]{1,2,0:T(8,128)(2,1)S(1)}, u32[]{:S(2)}, u32[]{:S(2)}) %all-to-all-start.2) | async-done | bytes 491552 | tf_op jit(solution)/shard_map/all_to_all | solution.py:449
  (690 shorter events, 451.9 us)
Async XLA Ops:
  8.4 107.3 %collective-permute-start = (bf16[256,1280]{1,0:T(8,128)(2,1)}, bf16[256,1280]{1,0:T(8,128)(2,1)S(1)}, u32[]{:S(2)}, u32[]{:S(2)}) collective-permute-start(bf16[256,1280]{1,0:T(8,128)(2,1)} %bitcast.287), channel_id=1, source_target_pairs={{0,0},{1,4},{2,8},{3,12},{4,1},{5,5},{6,9},{7,13},{8,2},{9,6},{10,... | collective-permute-start | bytes 1966088 | tf_op jit(solution)/shard_map/ppermute | solution.py:405
  33.0 57.2 %collective-permute-start.49 = (bf16[256,768]{1,0:T(8,128)(2,1)}, bf16[256,768]{1,0:T(8,128)(2,1)S(1)}, u32[]{:S(2)}, u32[]{:S(2)}) collective-permute-start(bf16[256,768]{1,0:T(8,128)(2,1)} %bitcast.59), channel_id=1, source_target_pairs={{0,0},{1,4},{2,8},{3,12},{4,1},{5,5},{6,9},{7,13},{8,2},{9,6},{10,... | collective-permute-start | bytes 1179656 | tf_op jit(solution)/shard_map/ppermute | solution.py:405
  149.8 47.7 %collective-permute-start.57 = (bf16[288,768]{1,0:T(8,128)(2,1)}, bf16[288,768]{1,0:T(8,128)(2,1)}, u32[]{:S(2)}, u32[]{:S(2)}) collective-permute-start(bf16[288,768]{1,0:T(8,128)(2,1)} %collective-permute-done.53.refs_7_.refs_11_), channel_id=1, source_target_pairs={{0,16},{16,0},{1,17},{17,1},{2,18},{18,2},{3,19},{19,3},{4,20},{20... | collective-permute-start | bytes 1327112 | tf_op jit(solution)/shard_map/ppermute | solution.py:394
  159.3 62.3 %collective-permute-start.7 = (bf16[256,1280]{1,0:T(8,128)(2,1)}, bf16[256,1280]{1,0:T(8,128)(2,1)}, u32[]{:S(2)}, u32[]{:S(2)}) collective-permute-start(bf16[256,1280]{1,0:T(8,128)(2,1)} %first_norm.2.refs_0_), channel_id=1, source_target_pairs={{0,8},{8,0},{1,9},{9,1},{2,10},{10,2},{3,11},{11,3},{4,12},{12,4},... | collective-permute-start | bytes 1966088 | tf_op jit(solution)/shard_map/ppermute | solution.py:394
  169.9 52.2 %collective-permute-start.27 = (bf16[320,1280]{1,0:T(8,128)(2,1)}, bf16[320,1280]{1,0:T(8,128)(2,1)}, u32[]{:S(2)}, u32[]{:S(2)}) collective-permute-start(bf16[320,1280]{1,0:T(8,128)(2,1)} %copy.353.refs_8_.refs_4_), channel_id=1, source_target_pairs={{0,1},{1,2},{2,3},{3,0},{4,5},{5,6},{6,7},{7,4},{8,9},{9,10},{10,1... | collective-permute-start | bytes 2457608 | tf_op jit(solution)/shard_map/ppermute | solution.py:398
  179.4 51.7 %collective-permute-start.17 = (bf16[2,192,1280]{2,1,0:T(8,128)(2,1)S(1)}, bf16[2,192,1280]{2,1,0:T(8,128)(2,1)}, u32[]{:S(2)}, u32[]{:S(2)}) collective-permute-start(bf16[2,192,1280]{2,1,0:T(8,128)(2,1)S(1)} %get-tuple-element.380), channel_id=1, source_target_pairs={{0,4},{4,0},{1,5},{5,1},{2,6},{6,2},{3,7},{7,3},{8,12},{12,8},{9,1... | collective-permute-start | bytes 2949128 | tf_op jit(solution)/shard_map/ppermute | solution.py:394
  188.9 42.2 %collective-permute-start.18 = (bf16[2,192,1280]{2,1,0:T(8,128)(2,1)S(1)}, bf16[2,192,1280]{2,1,0:T(8,128)(2,1)}, u32[]{:S(2)}, u32[]{:S(2)}) collective-permute-start(bf16[2,192,1280]{2,1,0:T(8,128)(2,1)S(1)} %get-tuple-element.378), channel_id=1, source_target_pairs={{0,4},{4,0},{1,5},{5,1},{2,6},{6,2},{3,7},{7,3},{8,12},{12,8},{9,1... | collective-permute-start | bytes 2949128 | tf_op jit(solution)/shard_map/ppermute | solution.py:394
  312.0 51.0 %collective-permute-start.34 = (bf16[320,1280]{1,0:T(8,128)(2,1)}, bf16[320,1280]{1,0:T(8,128)(2,1)S(1)}, u32[]{:S(2)}, u32[]{:S(2)}) collective-permute-start(bf16[320,1280]{1,0:T(8,128)(2,1)} %copy.353.refs_8_.refs_4_), channel_id=1, source_target_pairs={{0,16},{16,0},{1,17},{17,1},{2,18},{18,2},{3,19},{19,3},{4,20},{20... | collective-permute-start | bytes 2457608 | tf_op jit(solution)/shard_map/ppermute | solution.py:394
  312.4 48.2 %collective-permute-start.28 = (bf16[256,1280]{1,0:T(8,128)(2,1)}, bf16[256,1280]{1,0:T(8,128)(2,1)}, u32[]{:S(2)}, u32[]{:S(2)}) collective-permute-start(bf16[256,1280]{1,0:T(8,128)(2,1)} %bitcast.288), channel_id=1, source_target_pairs={{0,0},{1,4},{2,8},{3,12},{4,1},{5,5},{6,9},{7,13},{8,2},{9,6},{10,... | collective-permute-start | bytes 1966088 | tf_op jit(solution)/shard_map/ppermute | solution.py:405
  317.0 46.8 %collective-permute-start.32 = (bf16[320,1280]{1,0:T(8,128)(2,1)}, bf16[320,1280]{1,0:T(8,128)(2,1)S(1)}, u32[]{:S(2)}, u32[]{:S(2)}) collective-permute-start(bf16[320,1280]{1,0:T(8,128)(2,1)} %collective-permute-done.27.refs_9_.refs_5_), channel_id=1, source_target_pairs={{0,1},{1,2},{2,3},{3,0},{4,5},{5,6},{6,7},{7,4},{8,9},{9,10},{10,1... | collective-permute-start | bytes 2457608 | tf_op jit(solution)/shard_map/ppermute | solution.py:398
  317.8 44.3 %collective-permute-start.100 = (bf16[384,768]{1,0:T(8,128)(2,1)}, bf16[384,768]{1,0:T(8,128)(2,1)S(1)}, u32[]{:S(2)}, u32[]{:S(2)}) collective-permute-start(bf16[384,768]{1,0:T(8,128)(2,1)} %get-tuple-element.181), channel_id=1, source_target_pairs={{0,16},{16,0},{1,17},{17,1},{2,18},{18,2},{3,19},{19,3},{4,20},{20... | collective-permute-start | bytes 1769480 | tf_op jit(solution)/shard_map/ppermute | solution.py:394
  427.8 79.9 %collective-permute-start.93 = (bf16[256,768]{1,0:T(8,128)(2,1)S(1)}, bf16[256,768]{1,0:T(8,128)(2,1)S(1)}, u32[]{:S(2)}, u32[]{:S(2)}) collective-permute-start(bf16[256,768]{1,0:T(8,128)(2,1)S(1)} %add_convert_fusion.8), channel_id=1, source_target_pairs={{0,0},{1,4},{2,8},{3,12},{4,1},{5,5},{6,9},{7,13},{8,2},{9,6},{10,... | collective-permute-start | bytes 1179656 | tf_op jit(solution)/shard_map/ppermute | solution.py:405
  521.1 58.3 %collective-permute-start.86 = (bf16[640,1280]{1,0:T(8,128)(2,1)}, bf16[640,1280]{1,0:T(8,128)(2,1)S(1)}, u32[]{:S(2)}, u32[]{:S(2)}) collective-permute-start(bf16[640,1280]{1,0:T(8,128)(2,1)} %get-tuple-element.166), channel_id=1, source_target_pairs={{0,16},{16,0},{1,17},{17,1},{2,18},{18,2},{3,19},{19,3},{4,20},{20... | collective-permute-start | bytes 4915208 | tf_op jit(solution)/shard_map/ppermute | solution.py:394
  525.2 64.2 %collective-permute-start.73 = (bf16[256,768]{1,0:T(8,128)(2,1)}, bf16[256,768]{1,0:T(8,128)(2,1)}, u32[]{:S(2)}, u32[]{:S(2)}) collective-permute-start(bf16[256,768]{1,0:T(8,128)(2,1)} %add_convert_fusion.10), channel_id=1, source_target_pairs={{0,8},{8,0},{1,9},{9,1},{2,10},{10,2},{3,11},{11,3},{4,12},{12,4},... | collective-permute-start | bytes 1179656 | tf_op jit(solution)/shard_map/ppermute | solution.py:394
  527.9 77.1 %collective-permute-start.39 = (bf16[256,1280]{1,0:T(8,128)(2,1)}, bf16[256,1280]{1,0:T(8,128)(2,1)}, u32[]{:S(2)}, u32[]{:S(2)}) collective-permute-start(bf16[256,1280]{1,0:T(8,128)(2,1)} %add_convert_fusion.3), channel_id=1, source_target_pairs={{0,8},{8,0},{1,9},{9,1},{2,10},{10,2},{3,11},{11,3},{4,12},{12,4},... | collective-permute-start | bytes 1966088 | tf_op jit(solution)/shard_map/ppermute | solution.py:394
  535.9 60.8 %collective-permute-start.42 = (bf16[256,1280]{1,0:T(8,128)(2,1)}, bf16[256,1280]{1,0:T(8,128)(2,1)}, u32[]{:S(2)}, u32[]{:S(2)}) collective-permute-start(bf16[256,1280]{1,0:T(8,128)(2,1)} %add_convert_fusion.1), channel_id=1, source_target_pairs={{0,8},{8,0},{1,9},{9,1},{2,10},{10,2},{3,11},{11,3},{4,12},{12,4},... | collective-permute-start | bytes 1966088 | tf_op jit(solution)/shard_map/ppermute | solution.py:394
  593.8 101.0 %collective-permute-start.94 = (bf16[256,768]{1,0:T(8,128)(2,1)}, bf16[256,768]{1,0:T(8,128)(2,1)}, u32[]{:S(2)}, u32[]{:S(2)}) collective-permute-start(bf16[256,768]{1,0:T(8,128)(2,1)} %get-tuple-element.175), channel_id=1, source_target_pairs={{0,0},{1,4},{2,8},{3,12},{4,1},{5,5},{6,9},{7,13},{8,2},{9,6},{10,... | collective-permute-start | bytes 1179656 | tf_op jit(solution)/shard_map/ppermute | solution.py:405
  607.6 87.2 %collective-permute-start.40 = (bf16[256,1280]{1,0:T(8,128)(2,1)}, bf16[256,1280]{1,0:T(8,128)(2,1)}, u32[]{:S(2)}, u32[]{:S(2)}) collective-permute-start(bf16[256,1280]{1,0:T(8,128)(2,1)} %add_convert_fusion.2), channel_id=1, source_target_pairs={{0,0},{1,4},{2,8},{3,12},{4,1},{5,5},{6,9},{7,13},{8,2},{9,6},{10,... | collective-permute-start | bytes 1966088 | tf_op jit(solution)/shard_map/ppermute | solution.py:405
  636.7 68.9 %collective-permute-start.90 = (bf16[320,1280]{1,0:T(8,128)(2,1)}, bf16[320,1280]{1,0:T(8,128)(2,1)}, u32[]{:S(2)}, u32[]{:S(2)}) collective-permute-start(bf16[320,1280]{1,0:T(8,128)(2,1)} %fusion.1), channel_id=1, source_target_pairs={{0,1},{1,2},{2,3},{3,0},{4,5},{5,6},{6,7},{7,4},{8,9},{9,10},{10,1... | collective-permute-start | bytes 2457608 | tf_op jit(solution)/shard_map/ppermute | solution.py:398
  689.4 42.2 %collective-permute-start.46 = (bf16[512,1280]{1,0:T(8,128)(2,1)}, bf16[512,1280]{1,0:T(8,128)(2,1)}, u32[]{:S(2)}, u32[]{:S(2)}) collective-permute-start(bf16[512,1280]{1,0:T(8,128)(2,1)} %get-tuple-element.131), channel_id=1, source_target_pairs={{0,4},{4,0},{1,5},{5,1},{2,6},{6,2},{3,7},{7,3},{8,12},{12,8},{9,1... | collective-permute-start | bytes 3932168 | tf_op jit(solution)/shard_map/ppermute | solution.py:394
  705.5 60.5 %collective-permute-start.79 = (bf16[2,192,1280]{2,1,0:T(8,128)(2,1)}, bf16[2,192,1280]{2,1,0:T(8,128)(2,1)}, u32[]{:S(2)}, u32[]{:S(2)}) collective-permute-start(bf16[2,192,1280]{2,1,0:T(8,128)(2,1)} %get-tuple-element.162), channel_id=1, source_target_pairs={{0,4},{4,0},{1,5},{5,1},{2,6},{6,2},{3,7},{7,3},{8,12},{12,8},{9,1... | collective-permute-start | bytes 2949128 | tf_op jit(solution)/shard_map/ppermute | solution.py:394
  708.3 60.1 %all-to-all-start.3 = ((bf16[8,320,160]{1,2,0:T(8,128)(2,1)}), bf16[8,320,160]{1,2,0:T(8,128)(2,1)S(1)}, u32[]{:S(2)}, u32[]{:S(2)}) async-start(bf16[8,320,160]{1,2,0:T(8,128)(2,1)} %bitcast.91), calls=%async_computation.3 | async-start | bytes 1966080 | tf_op jit(solution)/shard_map/all_to_all | solution.py:449
  738.9 56.7 %collective-permute-start.82 = (bf16[2,192,1280]{2,1,0:T(8,128)(2,1)}, bf16[2,192,1280]{2,1,0:T(8,128)(2,1)}, u32[]{:S(2)}, u32[]{:S(2)}) collective-permute-start(bf16[2,192,1280]{2,1,0:T(8,128)(2,1)} %get-tuple-element.376), channel_id=1, source_target_pairs={{0,16},{16,0},{1,17},{17,1},{2,18},{18,2},{3,19},{19,3},{4,20},{20... | collective-permute-start | bytes 2949128 | tf_op jit(solution)/shard_map/ppermute | solution.py:394
  800.6 56.8 %collective-permute-start.48 = (bf16[256,1280]{1,0:T(8,128)(2,1)}, bf16[256,1280]{1,0:T(8,128)(2,1)S(1)}, u32[]{:S(2)}, u32[]{:S(2)}) collective-permute-start(bf16[256,1280]{1,0:T(8,128)(2,1)} %get-tuple-element.133), channel_id=1, source_target_pairs={{0,0},{1,4},{2,8},{3,12},{4,1},{5,5},{6,9},{7,13},{8,2},{9,6},{10,... | collective-permute-start | bytes 1966088 | tf_op jit(solution)/shard_map/ppermute | solution.py:405
  (195 other events, 3035.2 us)

commit v2 on v0

--- a/solution.py
+++ b/solution.py
@@ -1,6 +1,12 @@
+import functools
+
 import jax
 import jax.numpy as jnp
+import numpy as np
 from jax import lax
+from jax.experimental import pallas as pl
+from jax.experimental.pallas import tpu as pltpu
+from jax.sharding import Mesh
 from jax.sharding import PartitionSpec as P
 
 HD = 64
@@ -379,6 +385,1142 @@
     )
 
 
+PLANE = ("y", "x", "c")
+EVERY = ("y", "x", "c", "z")
+TILE = 256
+
+
+def swap(values, axis):
+    return lax.ppermute(values, axis, ((0, 1), (1, 0)))
+
+
+def index_of(y, x, c, z):
+    return ((y * 2 + x) * 2 + c) * 4 + z
+
+
+def cross(values):
+    pairs = tuple(
+        ((y * 4 + a) * 4 + z, (y * 4 + z) * 4 + a) for y in range(2) for a in range(4) for z in range(4)
+    )
+    return lax.ppermute(values, EVERY, pairs)
+
+
+def row_pairs():
+    return tuple(
+        (index_of(y, x, c, z), index_of(y, (z ^ c) & 1, z >> 1, 2 * x + c))
+        for y in range(2)
+        for x in range(2)
+        for c in range(2)
+        for z in range(4)
+    )
+
+
+def rows_out(values):
+    return lax.ppermute(values, EVERY, row_pairs())
+
+
+def rows_home(values):
+    return lax.ppermute(values, EVERY, tuple((b, a) for a, b in row_pairs()))
+
+
+def pick(values, index, axis=0):
+    return lax.dynamic_index_in_dim(values, index, axis, keepdims=False)
+
+
+def wide(values):
+    return values.astype(jnp.float32)
+
+
+def low(values):
+    return values.astype(jnp.bfloat16)
+
+
+def matmul(left, right, left_dim, right_dim):
+    return lax.dot_general(
+        left, right, (((left_dim,), (right_dim,)), ((), ())), preferred_element_type=jnp.float32
+    )
+
+
+class Order:
+    def __init__(self):
+        self.last = None
+
+    def __call__(self, *values):
+        if self.last is not None:
+            values = lax.optimization_barrier((*values, self.last))[:-1]
+        self.last = values[0]
+        return values[0] if len(values) == 1 else values
+
+    def mark(self, value):
+        self.last = value
+
+
+def after(values, earlier):
+    return lax.optimization_barrier((values, earlier))[0]
+
+
+def to_plane(blocks):
+    return lax.all_to_all(blocks, PLANE, 0, 0)
+
+
+def join_shards(blocks):
+    return jnp.transpose(blocks, (1, 0, 2)).reshape(blocks.shape[1], -1)
+
+
+def split_shards(rows):
+    return jnp.transpose(rows.reshape(rows.shape[0], 8, -1), (1, 0, 2))
+
+
+def ahead_sum(near, got):
+    count = near.shape[0] // 2
+    return low(wide(near[count:]) + wide(got[count:]))
+
+
+def plane_swap(values, bit):
+    return lax.ppermute(values, "z", tuple((i, i ^ bit) for i in range(4)))
+
+
+def row_call(kernel, name, outs, *args):
+    rows = outs[0][0][0]
+    size = sum(a.size * a.dtype.itemsize for a in args)
+
+    def spec(shape):
+        return pl.BlockSpec((min(shape[0], rows), shape[1]), lambda i: (0, 0))
+
+    return pl.pallas_call(
+        kernel,
+        grid=(1,),
+        in_specs=[spec(a.shape) for a in args],
+        out_specs=[spec(shape) for shape, _ in outs],
+        out_shape=[jax.ShapeDtypeStruct(shape, dtype) for shape, dtype in outs],
+        cost_estimate=pl.CostEstimate(flops=args[0].size * 20, transcendentals=0, bytes_accessed=2 * size),
+        name=name,
+    )(*args)
+
+
+def centered(rows):
+    center = rows - jnp.mean(rows, axis=-1, keepdims=True)
+    spread = jnp.mean(center * center, axis=-1, keepdims=True)
+    scale = lax.rsqrt(spread + epsilon)
+    return center * scale, scale
+
+
+def first_norm_kernel(x_ref, gain_ref, shift_ref, out_ref):
+    unit, _ = centered(wide(x_ref[...]))
+    out_ref[...] = low(unit * gain_ref[...] + shift_ref[...])
+
+
+def mid_norm_kernel(x_ref, a_ref, b_ref, c_ref, bias_ref, gain_ref, shift_ref, mid_ref, out_ref):
+    branch = wide(a_ref[...]) + wide(b_ref[...]) + wide(c_ref[...])
+    middle = wide(x_ref[...]) + (branch + bias_ref[...])
+    mid_ref[...] = middle
+    unit, _ = centered(middle)
+    out_ref[...] = low(unit * gain_ref[...] + shift_ref[...])
+
+
+def norm_back(grad, rows, gain):
+    unit, scale = centered(rows)
+    t = grad * gain
+    back = scale * (
+        t - jnp.mean(t, axis=-1, keepdims=True) - unit * jnp.mean(t * unit, axis=-1, keepdims=True)
+    )
+    return back, jnp.sum(grad * unit, axis=0, keepdims=True), jnp.sum(grad, axis=0, keepdims=True)
+
+
+def mid_back_kernel(g_ref, a_ref, b_ref, c_ref, mid_ref, gain_ref, dmid_ref, ga_ref, sums_ref):
+    up = wide(g_ref[...])
+    grad = wide(a_ref[...]) + wide(b_ref[...]) + wide(c_ref[...])
+    back, gain_sum, shift_sum = norm_back(grad, mid_ref[...], gain_ref[...])
+    dmid = up + back
+    dmid_ref[...] = dmid
+    ga = low(dmid)
+    ga_ref[...] = ga
+    sums_ref[0:1] = jnp.sum(wide(ga), axis=0, keepdims=True)
+    sums_ref[1:2] = gain_sum
+    sums_ref[2:3] = shift_sum
+    sums_ref[3:4] = jnp.sum(up, axis=0, keepdims=True)
+
+
+def first_back_kernel(a_ref, b_ref, c_ref, x_ref, dmid_ref, gain_ref, dx_ref, sums_ref):
+    grad = wide(a_ref[...]) + wide(b_ref[...]) + wide(c_ref[...])
+    back, gain_sum, shift_sum = norm_back(grad, wide(x_ref[...]), gain_ref[...])
+    dx_ref[...] = low(dmid_ref[...] + back)
+    sums_ref[0:1] = gain_sum
+    sums_ref[1:2] = shift_sum
+
+
+def place_of(block, own):
+    return block ^ own
+
+
+def tile_visible(first_key, first_query, start):
+    shape = (TILE, TILE)
+    key = first_key + lax.broadcasted_iota(jnp.int32, shape, 0)
+    query = first_query + lax.broadcasted_iota(jnp.int32, shape, 1)
+    key_in = (key >= start) & (key < start + SPAN)
+    query_in = (query >= start) & (query < start + SPAN)
+    return (key <= query) | (key_in & query_in)
+
+
+def tile_bounds(block, blocks, start):
+    more = (start // TILE == block) & (start % TILE != 0)
+    return jnp.minimum(block + 1 + more.astype(jnp.int32), blocks)
+
+
+def head_lanes(width, head):
+    lane = lax.broadcasted_iota(jnp.int32, (1, width), 1)
+    return (lane >= head * HD) & (lane < (head + 1) * HD)
+
+
+def lane_chunks(columns):
+    chunks = []
+    for first in range(0, columns, 2 * HD):
+        lanes = min(2 * HD, columns - first)
+        chunks.append((first, lanes, lanes // HD))
+    return chunks
+
+
+def one_head(values, head, heads):
+    if heads == 1:
+        return values
+    lane = lax.broadcasted_iota(jnp.int32, (1, values.shape[1]), 1)
+    return jnp.where((lane >= HD) == (head == 1), values, jnp.zeros_like(values))
+
+
+def attend_block(block, start, rank, keep_ref, qkv_s, heads_s, logs_ref):
+    columns = qkv_s.shape[-1]
+    chunks = lane_chunks(columns)
+    here = pl.ds(pl.multiple_of(place_of(block, rank) * TILE, TILE), TILE)
+    queries = []
+    for first, lanes, heads in chunks:
+        query = qkv_s[0, here, first : first + lanes]
+        queries.append([one_head(query, h, heads) for h in range(heads)])
+
+    def tile(index, carry, masked):
+        rows = pl.ds(pl.multiple_of(place_of(index, rank) * TILE, TILE), TILE)
+        if masked:
+            visible = tile_visible(index * TILE, block * TILE, start)
+        scores = []
+        for (first, lanes, heads), query in zip(chunks, queries):
+            keys = qkv_s[1, rows, first : first + lanes]
+            for h in range(heads):
+                score = matmul(keys, query[h], 1, 1)
+                scores.append(jnp.where(visible, score, negative) if masked else score)
+        out = []
+        number = 0
+        for first, lanes, heads in chunks:
+            values = qkv_s[2, rows, first : first + lanes]
+            for h in range(heads):
+                peak, total, acc = carry[number]
+                score = scores[number]
+                new_peak = jnp.maximum(peak, jnp.max(score, axis=0, keepdims=True))
+                decay = jnp.exp(peak - new_peak)
+                raised = jnp.exp(score - new_peak)
+                total = total * decay + jnp.sum(raised, axis=0, keepdims=True)
+                part = matmul(values, low(raised), 0, 0)
+                acc = acc * decay + part[h * HD : (h + 1) * HD]
+                out.append((new_peak, total, acc))
+                number += 1
+        return tuple(out)
+
+    carry = tuple(
+        (
+            jnp.full((1, TILE), negative, jnp.float32),
+            jnp.zeros((1, TILE), jnp.float32),
+            jnp.zeros((HD, TILE), jnp.float32),
+        )
+        for _ in range(columns // HD)
+    )
+    carry = lax.fori_loop(0, block, lambda i, s: tile(i, s, False), carry)
+    carry = lax.fori_loop(block, tile_bounds(block, 4, start), lambda i, s: tile(i, s, True), carry)
+    number = 0
+    for first, lanes, heads in chunks:
+        outs = []
+        for _ in range(heads):
+            peak, total, acc = carry[number]
+            outs.append(acc * (keep_ref[number] / total))
+            logs_ref[block, number : number + 1, :] = peak + jnp.log(total)
+            number += 1
+        heads_s[here, first : first + lanes] = low(jnp.concatenate(outs, axis=0).T)
+
+
+def attend_back_block(block, start, rank, keep_ref, qkv_s, heads_s, grads_s, logs_ref, dq_s, dk_s, dv_s):
+    columns = qkv_s.shape[-1]
+    chunks = lane_chunks(columns)
+    here = pl.ds(pl.multiple_of(place_of(block, rank) * TILE, TILE), TILE)
+    queries, grads, weighted, logs = [], [], [], []
+    number = 0
+    for first, lanes, heads in chunks:
+        query = qkv_s[0, here, first : first + lanes]
+        grad = grads_s[here, first : first + lanes]
+        turned = (wide(grad) * wide(heads_s[here, first : first + lanes])).T
+        for h in range(heads):
+            keep = keep_ref[number]
+            queries.append(one_head(query, h, heads))
+            grads.append(low(wide(one_head(grad, h, heads)) * keep))
+            weighted.append(keep * jnp.sum(turned[h * HD : (h + 1) * HD], axis=0, keepdims=True))
+            logs.append(logs_ref[block, number : number + 1, :])
+            number += 1
+
+    def tile(index, carry, masked):
+        rows = pl.ds(pl.multiple_of(place_of(index, rank) * TILE, TILE), TILE)
+        if masked:
+            visible = tile_visible(index * TILE, block * TILE, start)
+        out = []
+        number = 0
+        for first, lanes, heads in chunks:
+            keys = qkv_s[1, rows, first : first + lanes]
+            values = qkv_s[2, rows, first : first + lanes]
+            dk = dv = None
+            for h in range(heads):
+                scores = matmul(keys, queries[number], 1, 1)
+                if masked:
+                    scores = jnp.where(visible, scores, negative)
+                prob = jnp.exp(scores - logs[number])
+                dprob = matmul(values, grads[number], 1, 1)
+                dscores = low(prob * (dprob - weighted[number]))
+                dv_part = matmul(low(prob), grads[number], 1, 0)
+                dk_part = matmul(dscores, queries[number], 1, 0)
+                dv = dv_part if dv is None else dv + dv_part
+                dk = dk_part if dk is None else dk + dk_part
+                out.append(carry[number] + matmul(keys, dscores, 0, 0)[h * HD : (h + 1) * HD])
+                number += 1
+            dk_s[rows, first : first + lanes] += dk
+            dv_s[rows, first : first + lanes] += dv
+        return tuple(out)
+
+    carry = tuple(jnp.zeros((HD, TILE), jnp.float32) for _ in range(columns // HD))
+    carry = lax.fori_loop(0, block, lambda i, s: tile(i, s, False), carry)
+    carry = lax.fori_loop(block, tile_bounds(block, 4, start), lambda i, s: tile(i, s, True), carry)
+    number = 0
+    for first, lanes, heads in chunks:
+        dq = jnp.concatenate(carry[number : number + heads], axis=0) * (1.0 / HD**0.5)
+        dq_s[here, first : first + lanes] = low(dq.T)
+        number += heads
+
+
+ANY = pl.BlockSpec(memory_space=pl.ANY)
+VMEM = pl.BlockSpec(memory_space=pltpu.VMEM)
+LIMIT = 56 << 20
+
+
+def fetch(parts, into, sem):
+    first = 0
+    for part in parts:
+        rows = part.shape[0]
+        pltpu.make_async_copy(part, into.at[pl.ds(first, rows)], sem).start()
+        first += rows
+
+
+def fetched(into, sem):
+    pltpu.make_async_copy(into, into, sem).wait()
+
+
+def send(source, into, sem):
+    copy = pltpu.make_async_copy(source, into, sem)
+    copy.start()
+    return copy
+
+
+def scratch(*shape):
+    return pltpu.VMEM(shape, jnp.bfloat16)
+
+
+def matmul_call(kernel, name, outs, args, specs, scratches, flops):
+    size = sum(a.size * a.dtype.itemsize for a in args)
+    return pl.pallas_call(
+        kernel,
+        in_specs=specs,
+        out_specs=[spec for _, _, spec in outs],
+        out_shape=[jax.ShapeDtypeStruct(shape, dtype) for shape, dtype, _ in outs],
+        scratch_shapes=scratches,
+        compiler_params=pltpu.CompilerParams(vmem_limit_bytes=LIMIT),
+        cost_estimate=pl.CostEstimate(flops=flops // 16, transcendentals=0, bytes_accessed=size // 8),
+        name=name,
+    )(*args)
+
+
+SMEM = pl.BlockSpec(memory_space=pltpu.SMEM)
+
+
+def front(pieces, weights, places, bias, columns, info, keep):
+    count, width = pieces[0].shape
+    length = 4 * count
+    half = length // 2
+    scales = (1.0 / HD**0.5, 1.0, 1.0)
+
+    def kernel(*refs):
+        piece_refs, refs = refs[:4], refs[4:]
+        weight_refs, refs = refs[: len(weights)], refs[len(weights) :]
+        bias_ref, info_ref, keep_ref, refs = refs[0], refs[1], refs[2], refs[3:]
+        qkv_ref, all_ref, full_ref, heads_ref, near_ref, far_ref, logs_ref = refs[:7]
+        rows_s, full_s, qkv_s, heads_s, sum_s, sems, outs = refs[7:]
+        for array, index, row, matrix, column, rows in places:
+            source = weight_refs[array]
+            source = source if index is None else source.at[index]
+            pltpu.make_async_copy(
+                source.at[pl.ds(row, rows)], full_s.at[matrix, pl.ds(column, rows)], sems.at[0]
+            ).start()
+        fetch(piece_refs, rows_s, sems.at[1])
+        fetched(full_s, sems.at[0])
+        fetched(rows_s, sems.at[1])
+        sent = [send(full_s, full_ref, outs.at[0]), send(rows_s, all_ref, outs.at[1])]
+
+        @pl.loop(0, 4)
+        def _(block):
+            rows = pl.ds(pl.multiple_of(block * count, count), count)
+            for t in range(3):
+                part = low(matmul(rows_s[rows, :], full_s[t], 1, 1) + bias_ref[t])
+                qkv_s[t, rows, :] = low(wide(part) * scales[t])
+
+        sent.append(send(qkv_s, qkv_ref, outs.at[2]))
+
+        @pl.loop(0, 4)
+        def _(block):
+            attend_block(block, info_ref[0], info_ref[1], keep_ref, qkv_s, heads_s, logs_ref)
+
+        sent.append(send(heads_s, heads_ref, outs.at[3]))
+
+        @pl.loop(0, 4)
+        def _(block):
+            rows = pl.ds(pl.multiple_of(block * count, count), count)
+            sum_s[rows, :] = low(matmul(heads_s[rows, :], full_s[3], 1, 0))
+
+        sent.append(send(sum_s.at[pl.ds(0, half)], near_ref, outs.at[4]))
+        sent.append(send(sum_s.at[pl.ds(half, half)], far_ref, outs.at[5]))
+        for copy in sent:
+            copy.wait()
+
+    def out(*shape):
+        return (shape, jnp.bfloat16, ANY)
+
+    return matmul_call(
+        kernel,
+        "front",
+        [
+            out(3, length, columns), out(length, width), out(4, columns, width), out(length, columns),
+            out(half, width), out(half, width), ((4, columns // HD, TILE), jnp.float32, VMEM),
+        ],
+        [*pieces, *weights, bias, info, keep],
+        [ANY] * (4 + len(weights)) + [VMEM, SMEM, SMEM],
+        [
+            scratch(length, width), scratch(4, columns, width), scratch(3, length, columns),
+            scratch(length, columns), scratch(length, width),
+            pltpu.SemaphoreType.DMA((2,)), pltpu.SemaphoreType.DMA((6,)),
+        ],
+        8 * length * columns * width + 4 * length * length * columns,
+    )
+
+
+def rear(pieces, weights, qkv, heads_low, logs, info, keep):
+    count, width = pieces[0].shape
+    length = 4 * count
+    half = length // 2
+    columns = weights.shape[1]
+
+    def kernel(*refs):
+        piece_refs, refs = refs[:4], refs[4:]
+        weight_ref, qkv_ref, heads_ref, logs_ref, info_ref, keep_ref, refs = *refs[:6], refs[6:]
+        dq_ref, dk_ref, dv_ref, all_ref, near_ref, far_ref = refs[:6]
+        rows_s, full_s, qkv_s, heads_s, grads_s, dq_s, dk_s, dv_s, low_s, sum_s, sems, outs = refs[6:]
+        fetch([weight_ref.at[3]], full_s.at[3], sems.at[0])
+        fetch(piece_refs, rows_s, sems.at[1])
+        fetch([heads_ref], heads_s, sems.at[2])
+        copies = [send(qkv_ref, qkv_s, sems.at[3])]
+        copies.append(send(weight_ref.at[pl.ds(0, 3)], full_s.at[pl.ds(0, 3)], sems.at[4]))
+        dk_s[...] = jnp.zeros_like(dk_s)
+        dv_s[...] = jnp.zeros_like(dv_s)
+        fetched(full_s.at[3], sems.at[0])
+        fetched(rows_s, sems.at[1])
+        sent = [send(rows_s, all_ref, outs.at[0])]
+
+        @pl.loop(0, 4)
+        def _(block):
+            at = pl.ds(pl.multiple_of(block * count, count), count)
+            grads_s[at, :] = low(matmul(rows_s[at, :], full_s[3], 1, 1))
+
+        fetched(heads_s, sems.at[2])
+        copies[0].wait()
+
+        @pl.loop(0, 4)
+        def _(block):
+            attend_back_block(
+                block, info_ref[0], info_ref[1], keep_ref, qkv_s, heads_s, grads_s, logs_ref, dq_s, dk_s, dv_s
+            )
+
+        copies[1].wait()
+        low_s[0] = low(dk_s[...])
+        low_s[1] = low(dv_s[...])
+        sent.append(send(dq_s, dq_ref, outs.at[1]))
+        sent.append(send(low_s.at[0], dk_ref, outs.at[2]))
+        sent.append(send(low_s.at[1], dv_ref, outs.at[3]))
+
+        @pl.loop(0, 4)
+        def _(block):
+            at = pl.ds(pl.multiple_of(block * count, count), count)
+            total = matmul(dq_s[at, :], full_s[0], 1, 0)
+            total = total + matmul(low_s[0, at, :], full_s[1], 1, 0)
+            total = total + matmul(low_s[1, at, :], full_s[2], 1, 0)
+            sum_s[at, :] = low(total)
+
+        sent.append(send(sum_s.at[pl.ds(0, half)], near_ref, outs.at[4]))
+        sent.append(send(sum_s.at[pl.ds(half, half)], far_ref, outs.at[5]))
+        for copy in sent:
+            copy.wait()
+
+    def out(*shape):
+        return (shape, jnp.bfloat16, ANY)
+
+    return matmul_call(
+        kernel,
+        "rear",
+        [out(length, columns)] * 3 + [out(length, width), out(half, width), out(half, width)],
+        [*pieces, weights, qkv, heads_low, logs, info, keep],
+        [ANY] * 7 + [VMEM, SMEM, SMEM],
+        [
+            scratch(length, width), scratch(4, columns, width), scratch(3, length, columns),
+            scratch(length, columns), scratch(length, columns), scratch(length, columns),
+            pltpu.VMEM((length, columns), jnp.float32), pltpu.VMEM((length, columns), jnp.float32),
+            scratch(2, length, columns), scratch(length, width),
+            pltpu.SemaphoreType.DMA((5,)), pltpu.SemaphoreType.DMA((6,)),
+        ],
+        8 * length * columns * width + 10 * length * length * columns,
+    )
+
+
+def gelu_pair(u):
+    k = 0.7978845608028654
+    t = jnp.tanh(k * (u + 0.044715 * (u * u * u)))
+    value = 0.5 * u * (1.0 + t)
+    slope = 0.5 * (1.0 + t) + 0.5 * u * (1.0 - t * t) * (k * (1.0 + 3 * 0.044715 * (u * u)))
+    return value, slope
+
+
+def mlp_main(rows, grads, weights, bias):
+    count, width = rows[0].shape
+    length = 4 * count
+    units = weights.shape[0] // 16
+    hidden = 8 * units
+    half = length // 2
+
+    def kernel(*refs):
+        row_refs, grad_refs, weight_ref, refs = refs[:4], refs[4:8], refs[8], refs[9:]
+        bias_ref, refs = refs[0], refs[1:]
+        rows_ref, grads_ref, hidden_ref, pre_ref, near_ref, far_ref, sum_ref = refs[:7]
+        rows_s, grads_s, fc_s, proj_s, hidden_s, slope_s, back_s, sems, outs = refs[7:]
+        fetch([weight_ref.at[pl.ds(2 * i * units, units)] for i in range(8)], fc_s, sems.at[0])
+        fetch(row_refs, rows_s, sems.at[1])
+        fetch([weight_ref.at[pl.ds((2 * i + 1) * units, units)] for i in range(8)], proj_s, sems.at[2])
+        fetch(grad_refs, grads_s, sems.at[3])
+        fetched(fc_s, sems.at[0])
+        fetched(rows_s, sems.at[1])
+        sent = [send(rows_s, rows_ref, outs.at[0])]
+
+        @pl.loop(0, 4)
+        def _(block):
+            at = pl.ds(pl.multiple_of(block * count, count), count)
+            value, slope = gelu_pair(matmul(rows_s[at, :], fc_s[...], 1, 1) + bias_ref[...])
+            hidden_s[at, :] = low(value)
+            slope_s[at, :] = low(slope)
+
+        sent.append(send(hidden_s, hidden_ref, outs.at[1]))
+        fetched(proj_s, sems.at[2])
+        fetched(grads_s, sems.at[3])
+        sent.append(send(grads_s, grads_ref, outs.at[2]))
+        sum_ref[...] = jnp.zeros_like(sum_ref)
+
+        @pl.loop(0, 4)
+        def _(block):
+            at = pl.ds(pl.multiple_of(block * count, count), count)
+            pre = low(matmul(grads_s[at, :], proj_s[...], 1, 1) * wide(slope_s[at, :]))
+            slope_s[at, :] = pre
+            sum_ref[...] += jnp.sum(wide(pre), axis=0, keepdims=True)
+            back_s[at, :] = low(matmul(pre, fc_s[...], 1, 0))
+
+        sent.append(send(slope_s, pre_ref, outs.at[3]))
+        sent.append(send(back_s.at[pl.ds(0, half)], near_ref, outs.at[4]))
+        sent.append(send(back_s.at[pl.ds(half, half)], far_ref, outs.at[5]))
+        for copy in sent:
+            copy.wait()
+
+    def out(rows, columns):
+        return ((rows, columns), jnp.bfloat16, ANY)
+
+    return matmul_call(
+        kernel,
+        "mlp_main",
+        [
+            out(length, width), out(length, width), out(length, hidden), out(length, hidden),
+            out(half, width), out(half, width), ((1, hidden), jnp.float32, VMEM),
+        ],
+        [*rows, *grads, weights, bias],
+        [ANY] * 9 + [VMEM],
+        [
+            scratch(length, width), scratch(length, width), scratch(hidden, width), scratch(hidden, width),
+            scratch(length, hidden), scratch(length, hidden), scratch(length, width),
+            pltpu.SemaphoreType.DMA((4,)), pltpu.SemaphoreType.DMA((6,)),
+        ],
+        6 * length * hidden * width,
+    )
+
+
+def mlp_rest(rows, grads, hidden, pre, weights):
+    length, width = rows.shape
+    units = weights.shape[0] // 16
+    total = 8 * units
+    half = length // 2
+    count = length // 4
+    tile = 256
+
+    def kernel(*refs):
+        rows_ref, grads_ref, hidden_ref, pre_ref = refs[:4]
+        weight_ref, near_ref, far_ref, grad_out = refs[4:8]
+        rows_s, grads_s, hidden_s, pre_s, proj_s, ahead_s, fc_s, back_s, sems, outs = refs[8:]
+        fetch([hidden_ref], hidden_s, sems.at[0])
+        fetch([weight_ref.at[pl.ds((2 * i + 1) * units, units)] for i in range(8)], proj_s, sems.at[1])
+        fetch([pre_ref], pre_s, sems.at[2])
+        fetch([rows_ref], rows_s, sems.at[3])
+        fetch([grads_ref], grads_s, sems.at[4])
+        fetched(hidden_s, sems.at[0])
+        fetched(proj_s, sems.at[1])
+
+        @pl.loop(0, 4)
+        def _(block):
+            at = pl.ds(pl.multiple_of(block * count, count), count)
+            ahead_s[at, :] = low(matmul(hidden_s[at, :], proj_s[...], 1, 0))
+
+        sent = [
+            send(ahead_s.at[pl.ds(0, half)], near_ref, outs.at[0]),
+            send(ahead_s.at[pl.ds(half, half)], far_ref, outs.at[1]),
+        ]
+        fetched(pre_s, sems.at[2])
+        fetched(rows_s, sems.at[3])
+
+        def pieces(source, kind):
+            for k in range(8):
+                into = grad_out.at[pl.ds((2 * k + kind) * units, units)]
+                sent.append(send(source.at[pl.ds(k * units, units)], into, outs.at[2 + kind * 8 + k]))
+
+        @pl.loop(0, total // tile)
+        def _(block):
+            at = pl.ds(pl.multiple_of(block * tile, tile), tile)
+            fc_s[at, :] = low(matmul(pre_s[:, at], rows_s[...], 0, 0))
+
+        pieces(fc_s, 0)
+        fetched(grads_s, sems.at[4])
+
+        @pl.loop(0, total // tile)
+        def _(block):
+            at = pl.ds(pl.multiple_of(block * tile, tile), tile)
+            back_s[at, :] = low(matmul(hidden_s[:, at], grads_s[...], 0, 0))
+
+        pieces(back_s, 1)
+        for copy in sent:
+            copy.wait()
+
+    def out(*rows):
+        return ((*rows, width), jnp.bfloat16, ANY)
+
+    return matmul_call(
+        kernel,
+        "mlp_rest",
+        [out(half), out(half), out(16 * units)],
+        [rows, grads, hidden, pre, weights],
+        [ANY] * 5,
+        [
+            scratch(length, width), scratch(length, width), scratch(length, total), scratch(length, total),
+            scratch(total, width), scratch(length, width), scratch(total, width), scratch(total, width),
+            pltpu.SemaphoreType.DMA((5,)), pltpu.SemaphoreType.DMA((18,)),
+        ],
+        6 * length * total * width,
+    )
+
+
+def head_weight_grads(lefts, rows, grad_rows, places, outs):
+    length, columns = lefts[0].shape
+    width = rows.shape[1]
+
+    def kernel(*refs):
+        left_refs, (rows_ref, grads_ref), refs = refs[:4], refs[4:6], refs[6:]
+        out_refs, (full_s, sem) = refs[: len(outs)], refs[len(outs) :]
+        for matrix in range(4):
+            right = (rows_ref if matrix < 3 else grads_ref)[...]
+            full_s[matrix] = low(matmul(left_refs[matrix][...], right, 0, 0))
+        for array, index, row, matrix, column, count in places:
+            into = out_refs[array]
+            into = into if index is None else into.at[index]
+            pltpu.make_async_copy(
+                full_s.at[matrix, pl.ds(column, count)], into.at[pl.ds(row, count)], sem.at[0]
+            ).start()
+        pltpu.make_async_copy(full_s, full_s, sem.at[0]).wait()
+
+    return matmul_call(
+        kernel,
+        "head_weight_grads",
+        [(shape, jnp.bfloat16, ANY) for shape in outs],
+        [*lefts, rows, grad_rows],
+        [VMEM] * 6,
+        [scratch(4, columns, width), pltpu.SemaphoreType.DMA((1,))],
+        8 * length * columns * width,
+    )
+
+
+def hidden_blocks(fc, proj):
+    shard = proj.shape[1]
+    return jnp.concatenate([jnp.transpose(fc).reshape(8, -1, shard), proj.reshape(8, -1, shard)], axis=1)
+
+
+def hidden_unblock(blocks):
+    shard = blocks.shape[-1]
+    blocks = blocks.reshape(8, 2, -1, shard)
+    return blocks[:, 0].reshape(-1, shard), blocks[:, 1].reshape(-1, shard)
+
+
+def teacher_blocks(qkv, out):
+    columns, shard = out.shape
+    stack = jnp.concatenate([jnp.transpose(qkv, (0, 2, 1)), out[None]], axis=0)
+    stack = stack.reshape(4, 2, columns // (2 * HD), 2, 2, HD // 4, shard)
+    return jnp.transpose(stack, (3, 1, 4, 0, 2, 5, 6)).reshape(8, -1, shard)
+
+
+def teacher_unblock(heads):
+    shard = heads.shape[-1]
+    stack = heads.reshape(2, 2, 2, 4, -1, HD // 4, shard)
+    return jnp.transpose(stack, (3, 1, 4, 0, 2, 5, 6)).reshape(4, -1, shard)
+
+
+def student_blocks(qkv, out):
+    columns, shard = out.shape
+    stack = jnp.concatenate([jnp.transpose(qkv, (0, 2, 1)), out[None]], axis=0)
+    stack = stack.reshape(4, columns // HD, 8, HD // 8, shard)
+    return jnp.transpose(stack, (2, 0, 1, 3, 4)).reshape(8, -1, shard)
+
+
+def student_unblock(heads):
+    shard = heads.shape[-1]
+    return jnp.transpose(heads.reshape(8, 4, -1, HD // 8, shard), (1, 2, 0, 3, 4)).reshape(4, -1, shard)
+
+
+def teacher_places(columns):
+    sub = HD // 4
+    heads = columns // (2 * HD)
+    places = []
+    for matrix in range(4):
+        for plane in range(2):
+            for head in range(heads):
+                for dc in range(2):
+                    for dy in range(2):
+                        column = (plane * heads + head) * HD + (dc * 2 + dy) * sub
+                        places.append((dc * 2 + dy, plane, (matrix * heads + head) * sub, matrix, column, sub))
+    return places
+
+
+def student_places(columns):
+    sub = HD // 8
+    heads = columns // HD
+    places = []
+    for matrix in range(4):
+        for head in range(heads):
+            for part in range(8):
+                places.append((part, None, (matrix * heads + head) * sub, matrix, head * HD + part * sub, sub))
+    return places
+
+
+def student_grad_places(columns):
+    return [(p // 4, p % 4, row, matrix, column, sub) for p, _, row, matrix, column, sub in student_places(columns)]
+
+
+def on_pairs(*args):
+    teacher_in, student_in = args[0:14], args[14:28]
+    span_starts, head_slots = args[28], args[29]
+    pos = {name: lax.axis_index(name) for name in EVERY}
+    y, x, c, z = pos["y"], pos["x"], pos["c"], pos["z"]
+    rank = x * 2 + c
+    teacher_columns, student_columns = teacher_in[6].shape[0], student_in[6].shape[0]
+    teacher_count, student_count = teacher_columns // 2, student_columns // 2
+    shard, student_shard = teacher_in[2].shape[0], student_in[2].shape[0]
+    length = 4 * teacher_in[0].shape[1]
+
+    order = (2, 3, 7, 8, 9, 13)
+    marks = jnp.stack([span_starts[0] // 32, span_starts[0] % 32, 0, 0]).astype(jnp.bfloat16)
+    tall = jnp.concatenate(
+        [
+            jnp.stack([teacher_in[i] for i in order]),
+            jnp.pad(jnp.stack([student_in[i] for i in order]), ((0, 0), (0, shard - student_shard))),
+            jnp.broadcast_to(marks[:, None], (4, shard)),
+        ],
+        axis=0,
+    )
+    blocks = teacher_blocks(teacher_in[4], teacher_in[6])
+    blocks = jnp.concatenate([blocks, jnp.broadcast_to(tall[None], (8,) + tall.shape)], axis=1)
+    teacher_got = to_plane(blocks)
+    teacher_rows, student_rows = rows_out(teacher_in[0][0]), rows_out(student_in[0][0])
+
+    parts = [
+        teacher_in[11], teacher_in[5].reshape(-1), student_in[11], student_in[5].reshape(-1),
+        jnp.pad(head_slots.astype(jnp.bfloat16), (0, 128 - head_slots.shape[0])),
+    ]
+    limits = np.cumsum([0] + [part.shape[0] // 128 for part in parts])
+    deep = jnp.concatenate([part.reshape(-1, 128) for part in parts], axis=0)
+    deep = [deep] + [plane_swap(deep, step) for step in (1, 2, 3)]
+
+    student_got = to_plane(after(student_blocks(student_in[4], student_in[6]), teacher_got))
+    teacher_hidden_got = to_plane(after(hidden_blocks(teacher_in[10], teacher_in[12]), student_got))
+    student_hidden_got = to_plane(after(hidden_blocks(student_in[10], student_in[12]), teacher_hidden_got))
+
+    vectors = teacher_got[:, teacher_count:]
+
+    def width_vectors(block):
+        block = wide(jnp.transpose(block, (1, 0, 2)).reshape(6, 1, -1))
+        return tuple(block[i] for i in range(6))
+
+    teacher_vectors = width_vectors(vectors[:, :6])
+    student_vectors = width_vectors(vectors[:, 6:12, :student_shard])
+    starts = vectors[:, 12:14, 0].astype(jnp.int32)
+    starts = starts[:, 0] * 32 + starts[:, 1]
+    info = jnp.stack([pick(starts, y * 4 + z), 2 * c + (x ^ (z & 1))])
+
+    step = Order()
+    first = c == 0
+
+    t0 = step(join_shards(teacher_got[:, :teacher_count]))
+    t1, t2, t0y = plane_swap(t0, 1), plane_swap(t0, 2), swap(t0, "y")
+    full16, student16 = (teacher_rows.shape, jnp.bfloat16), (student_rows.shape, jnp.bfloat16)
+    (normed,) = row_call(
+        first_norm_kernel, "first_norm", [full16], step(teacher_rows), teacher_vectors[0], teacher_vectors[1]
+    )
+    teacher_normed = [normed, swap(normed, "x"), swap(normed, "c")]
+    step.mark(normed)
+    student_cross = cross(step(join_shards(student_got)))
+    t2 = step(t2)
+    t3, t2y = plane_swap(t2, 1), swap(t2, "y")
+    t1 = step(t1)
+    t1y = swap(t1, "y")
+    tf0 = step(join_shards(teacher_hidden_got))
+    teacher_normed[1] = step(teacher_normed[1])
+    teacher_normed.append(swap(teacher_normed[1], "c"))
+    t3 = step(t3)
+    t3y = swap(t3, "y")
+
+    def halves(one, two, three, four):
+        front, rear_part = jnp.stack([one, two]), jnp.stack([three, four])
+        return jnp.where(first, front, rear_part), swap(jnp.where(first, rear_part, front), "c")
+
+    own, near = halves(t0, t1, t2, t3)
+    s0 = step(student_cross)
+    s1, s2, s0y = plane_swap(s0, 1), plane_swap(s0, 2), swap(s0, "y")
+    (normed,) = row_call(
+        first_norm_kernel, "first_norm", [student16], step(student_rows), student_vectors[0], student_vectors[1]
+    )
+    student_normed = [normed, swap(normed, "x"), swap(normed, "c")]
+    step.mark(normed)
+    s2 = step(s2)
+    s3, s2y = plane_swap(s2, 1), swap(s2, "y")
+    s1 = step(s1)
+    s1y = swap(s1, "y")
+    t0y, t1y, t2y, t3y = step(t0y, t1y, t2y, t3y)
+    own_over, near_over = halves(t0y, t1y, t2y, t3y)
+    teacher_weights = lax.all_gather(after(tf0, t3y), ("y", "z"), axis=0, tiled=True)
+    teacher_up, student_up = rows_out(after(teacher_in[1][0], t3y)), rows_out(after(student_in[1][0], t3y))
+
+    deep = jnp.stack(deep)
+    deep = [deep[:, limits[i] : limits[i + 1]].reshape(4, -1) for i in range(5)]
+    near_y = jnp.stack([y, 1 - y])
+    hidden_spots = (jnp.arange(4)[None] * 8 + jnp.arange(2)[:, None] * 4 + rank).reshape(-1)
+    near_c = jnp.stack([c, 1 - c])
+    planes = z ^ jnp.arange(4)
+    hidden_hot = wide(jnp.arange(4)[:, None] == planes[None]).astype(jnp.bfloat16)
+
+    def hidden_bias(block):
+        block = pick(block.reshape(4, 2, 4, -1), rank, 2)
+        return jnp.einsum("zk,kyi->yzi", hidden_hot, block, preferred_element_type=jnp.float32).reshape(1, -1)
+
+    teacher_fc_bias, student_fc_bias = hidden_bias(deep[0]), hidden_bias(deep[2])
+    two = jnp.where(first, 0, 2)
+    block = lax.dynamic_slice_in_dim(deep[1].reshape(4, -1), two, 2, 0)
+    block = block.reshape(2, 2, 2, -1, 2, 2, HD // 4)
+    block = pick(block, x, 2)
+    block = jnp.where(y == 0, block, block[:, :, :, ::-1])
+    block = jnp.where(first, block, block[:, :, :, :, ::-1])
+    teacher_qv = wide(jnp.transpose(block, (1, 0, 2, 4, 3, 5)).reshape(2, -1))
+    slots = lax.dynamic_slice_in_dim(deep[4][:, : head_slots.shape[0]], two, 2, 0)
+    keep = wide(pick(slots.reshape(2, 2, -1), x, 1).reshape(-1))
+    block = pick(deep[3].reshape(4, 2, -1, 8, HD // 8), z ^ rank)
+    eighth = (near_y[:, None] * 4 + planes[None]).reshape(-1)
+    order_hot = (jnp.arange(8)[None] == eighth[:, None]).astype(jnp.bfloat16)
+    student_qv = jnp.einsum("rp,thpi->thri", order_hot, block, preferred_element_type=jnp.float32).reshape(2, -1)
+    ones = jnp.ones((student_qv.shape[1] // HD,), jnp.float32)
+
+    def bias_rows(pair):
+        return jnp.stack([pair[0], jnp.zeros_like(pair[0]), pair[1]])[:, None, :]
+
+    teacher_spots, student_spots = teacher_places(teacher_columns), student_places(student_columns)
+    head_weights = (own, own_over, near, near_over)
+    qkv, normed_all, weights, heads_low, t_near, t_far, logs = front(
+        step(*teacher_normed), head_weights, teacher_spots, bias_rows(teacher_qv), teacher_columns, info, keep
+    )
+    teacher_saved = (qkv, normed_all, weights, heads_low, logs)
+    step.mark(t_near)
+    t_got = swap(t_far, "c")
+    t_over = swap(step(ahead_sum(t_near, t_got)), "x")
+    sf0 = step(join_shards(student_hidden_got))
+    student_weights = lax.all_gather(sf0, ("y", "z"), axis=0, tiled=True)
+    student_normed[1] = step(student_normed[1])
+    student_normed.append(swap(student_normed[1], "c"))
+    bias_out, gain_two, shift_two = teacher_vectors[2:5]
+    full32 = (teacher_rows.shape, jnp.float32)
+    t_middle, normed = row_call(
+        mid_norm_kernel, "mid_norm", [full32, full16],
+        teacher_rows, t_near, t_got, step(t_over), bias_out, gain_two, shift_two,
+    )
+    step.mark(normed)
+    teacher_normed = [normed, swap(normed, "x"), swap(normed, "c")]
+    teacher_up = step(teacher_up)
+    teacher_ups = [teacher_up, swap(teacher_up, "x"), swap(teacher_up, "c")]
+    s3 = step(s3)
+    s3y = swap(s3, "y")
+    teacher_normed[1] = step(teacher_normed[1])
+    teacher_normed.append(swap(teacher_normed[1], "c"))
+
+    head_weights = (s0, s1, s2, s3, s0y, s1y, s2y, s3y)
+    qkv, normed_all, weights, heads_low, s_near, s_far, logs = front(
+        step(*student_normed), head_weights, student_spots, bias_rows(student_qv), student_columns, info, ones
+    )
+    student_saved = (qkv, normed_all, weights, heads_low, logs)
+    step.mark(s_near)
+    s_got = swap(s_far, "c")
+    teacher_ups[1] = step(teacher_ups[1])
+    teacher_ups.append(swap(teacher_ups[1], "c"))
+    s_over = swap(step(ahead_sum(s_near, s_got)), "x")
+
+    *teacher_mlp, t_near, t_far, teacher_fc = mlp_main(
+        step(*teacher_normed), teacher_ups, teacher_weights, teacher_fc_bias
+    )
+    step.mark(t_near)
+    t_got = swap(t_far, "c")
+    ahead = step(ahead_sum(t_near, t_got))
+    t_part, t_over = swap(ahead[:64], "x"), swap(ahead[64:], "x")
+    bias_out, gain_two, shift_two = student_vectors[2:5]
+    student32 = (student_rows.shape, jnp.float32)
+    s_middle, normed = row_call(
+        mid_norm_kernel, "mid_norm", [student32, student16],
+        student_rows, s_near, s_got, step(s_over), bias_out, gain_two, shift_two,
+    )
+    step.mark(normed)
+    student_normed = [normed, swap(normed, "x"), swap(normed, "c")]
+    student_up = step(student_up)
+    student_ups = [student_up, swap(student_up, "x"), swap(student_up, "c")]
+    teacher_mlp[0] = after(step(teacher_mlp[0]), t_part)
+    t_out_near, t_out_far, grads = mlp_rest(*teacher_mlp, teacher_weights)
+    step.mark(t_out_near)
+    teacher_hidden = lax.psum_scatter(grads, ("y", "z"), scatter_dimension=0, tiled=True)
+    width = teacher_rows.shape[1]
+    t_dmid, t_ga, teacher_two = row_call(
+        mid_back_kernel, "mid_back", [full32, full16, ((4, width), jnp.float32)],
+        teacher_up, t_near, t_got, jnp.concatenate([t_part, step(t_over)], axis=0), t_middle, teacher_vectors[3],
+    )
+    step.mark(t_ga)
+    teacher_normed = [t_ga, swap(t_ga, "x"), swap(t_ga, "c")]
+
+    student_normed[1] = step(student_normed[1])
+    student_normed.append(swap(student_normed[1], "c"))
+    student_ups[1] = step(student_ups[1])
+    student_ups.append(swap(student_ups[1], "c"))
+
+    *student_mlp, s_near, s_far, student_fc = mlp_main(
+        step(*student_normed), student_ups, student_weights, student_fc_bias
+    )
+    step.mark(s_near)
+    s_got = swap(s_far, "c")
+    teacher_normed[1] = step(teacher_normed[1])
+    teacher_normed.append(swap(teacher_normed[1], "c"))
+    s_over = swap(step(ahead_sum(s_near, s_got)), "x")
+
+    qkv, normed_all, weights, heads_low, logs = teacher_saved
+    t_dq, t_dk, t_dv, t_grad_all, t_near, t_far = rear(
+        step(*teacher_normed), weights, qkv, heads_low, logs, info, keep
+    )
+    step.mark(t_near)
+    t_got = swap(t_far, "c")
+    teacher_saved = ([t_dq, t_dk, t_dv, heads_low], normed_all, t_grad_all)
+    width = student_rows.shape[1]
+    s_dmid, s_ga, student_two = row_call(
+        mid_back_kernel, "mid_back", [student32, student16, ((4, width), jnp.float32)],
+        student_up, s_near, s_got, step(s_over), s_middle, student_vectors[3],
+    )
+    step.mark(s_ga)
+    student_normed = [s_ga, swap(s_ga, "x"), swap(s_ga, "c")]
+    t_over = swap(step(ahead_sum(t_near, t_got)), "x")
+    lefts, right, grad_right = teacher_saved
+    lefts[0] = step(lefts[0])
+    teacher_width, student_width = teacher_rows.shape[1], student_rows.shape[1]
+    th = head_weight_grads(lefts, right, grad_right, teacher_spots, [(2, teacher_count, teacher_width)] * 4)
+    teacher_qv_grad = jnp.stack([jnp.sum(wide(t_dq), axis=0), jnp.sum(wide(t_dv), axis=0)])
+    step.mark(th[0])
+    th_over_got, th_got = swap(th[3], "c"), swap(th[2], "c")
+
+    def planes_of(mine, got):
+        odd = jnp.stack([jnp.where(first, mine[1], got[1]), jnp.where(first, got[1], mine[1])])
+        even = jnp.stack([jnp.where(first, mine[0], got[0]), jnp.where(first, got[0], mine[0])])
+        return odd, even
+
+    odd_over, even_over = planes_of(th[1], step(th_over_got))
+    odd_got, even_got = swap(odd_over, "y"), swap(even_over, "y")
+    th_odd, th_even = planes_of(th[0], th_got)
+    step.mark(odd_over)
+    student_mlp[0] = step(student_mlp[0])
+    s_out_near, s_out_far, grads = mlp_rest(*student_mlp, student_weights)
+    step.mark(s_out_near)
+    student_hidden = lax.psum_scatter(grads, ("y", "z"), scatter_dimension=0, tiled=True)
+    teacher_dx, teacher_one = row_call(
+        first_back_kernel, "first_back", [full16, ((2, teacher_width), jnp.float32)],
+        t_near, t_got, step(t_over), teacher_rows, t_dmid, teacher_vectors[0],
+    )
+    step.mark(teacher_dx)
+    t_out_got = swap(after(t_out_far, teacher_dx), "c")
+    teacher_dx = rows_home(teacher_dx)
+    teacher_hidden = to_plane(split_shards(step(teacher_hidden)))
+    student_normed[1] = step(student_normed[1])
+    student_normed.append(swap(student_normed[1], "c"))
+    qkv, normed_all, weights, heads_low, logs = student_saved
+    s_dq, s_dk, s_dv, s_grad_all, s_near, s_far = rear(
+        step(*student_normed), weights, qkv, heads_low, logs, info, ones
+    )
+    step.mark(s_near)
+    s_got = swap(s_far, "c")
+    odd_got = step(odd_got)
+    th_odd_got = plane_swap(step(low(wide(th_odd) + wide(odd_got))), 1)
+    s_over = swap(step(ahead_sum(s_near, s_got)), "x")
+    teacher_hidden = step(teacher_hidden)
+    sh_near, sh_far = head_weight_grads(
+        [step(s_dq), s_dk, s_dv, heads_low], normed_all, s_grad_all, student_grad_places(student_columns),
+        [(4, student_count, student_width)] * 2,
+    )
+    student_qv_grad = jnp.stack([jnp.sum(wide(s_dq), axis=0), jnp.sum(wide(s_dv), axis=0)])
+    step.mark(sh_near)
+    sh_got = swap(sh_far, "y")
+    t_out_over = swap(step(ahead_sum(t_out_near, t_out_got)), "x")
+    student_dx, student_one = row_call(
+        first_back_kernel, "first_back", [student16, ((2, student_width), jnp.float32)],
+        s_near, s_got, step(s_over), student_rows, s_dmid, student_vectors[0],
+    )
+    step.mark(student_dx)
+    s_out_got = swap(after(s_out_far, student_dx), "c")
+    student_dx = rows_home(student_dx)
+
+    def spread(places, values):
+        hot = (jnp.arange(32)[:, None] == places[None]).astype(jnp.float32)
+        return jnp.dot(hot, values, precision=lax.Precision.HIGHEST)
+
+    head_planes = planes.reshape(2, 2)
+    head_planes = jnp.where(first, head_planes[0], head_planes[1])
+    column_spots = (
+        head_planes[:, None, None] * 8 + x * 4 + near_y[None, None, :] * 2 + near_c[None, :, None]
+    ).reshape(-1)
+    eighth_spots = rank * 8 + eighth
+
+    teacher_qv_grad = teacher_qv_grad.reshape(2, 2, -1, 2, 2, HD // 4)
+    teacher_qv_grad = jnp.transpose(teacher_qv_grad, (1, 3, 4, 0, 2, 5)).reshape(8, -1)
+    student_qv_grad = jnp.transpose(student_qv_grad.reshape(2, -1, 8, HD // 8), (2, 0, 1, 3)).reshape(8, -1)
+    hidden_grads = jnp.concatenate([teacher_fc.reshape(8, -1), student_fc.reshape(8, -1)], axis=1)
+    hidden_grads = spread(hidden_spots, hidden_grads)
+    lanes = hidden_grads.shape[1]
+    column_grads = jnp.concatenate(
+        [spread(column_spots, teacher_qv_grad), spread(eighth_spots, student_qv_grad)], axis=1
+    )
+    column_grads = jnp.pad(column_grads, ((0, 0), (0, lanes - column_grads.shape[1])))
+
+    def stacked(one, two):
+        tall = jnp.concatenate([one, two, jnp.zeros_like(one)], axis=0)
+        return [tall[:, i : i + lanes] for i in range(0, tall.shape[1], lanes)]
+
+    total = jnp.concatenate(
+        [hidden_grads, column_grads] + stacked(teacher_one, teacher_two) + stacked(student_one, student_two), axis=0
+    )
+    total = step(total)
+    other = swap(total, "c")
+    th_odd_got, even_got = step(th_odd_got, even_got)
+    th_even = wide(th_even) + wide(even_got)
+    th_even_got = plane_swap(low(th_even[1] + wide(th_odd_got[1])), 2)
+    sh_total = step(wide(sh_near) + wide(sh_got))
+    sh_odd_got = plane_swap(low(sh_total[1::2]), 1)
+    total = total + step(other)
+    other = swap(total, "x")
+    s_out_over = swap(step(ahead_sum(s_out_near, s_out_got)), "x")
+    count = t_middle.shape[0]
+    teacher_out = low(
+        t_middle + (wide(t_out_near[:count]) + wide(t_out_got[:count]) + wide(step(t_out_over)) + teacher_vectors[5])
+    )
+    teacher_out = rows_home(teacher_out)
+    sh_even = step(sh_total[0::2] + wide(sh_odd_got))
+    sh_even_got = plane_swap(low(sh_even[1]), 2)
+    teacher_head = low(th_even[0] + wide(th_odd_got[0]) + wide(step(th_even_got)))
+    teacher_head = to_plane(split_shards(teacher_head))
+    total = total + step(other)
+    other = swap(total, "y")
+    student_head = cross(low(sh_even[0] + wide(step(sh_even_got))))
+    count = s_middle.shape[0]
+    student_out = low(
+        s_middle + (wide(s_out_near[:count]) + wide(s_out_got[:count]) + wide(step(s_out_over)) + student_vectors[5])
+    )
+    student_out = rows_home(student_out)
+    total = total + step(other)
+    other = plane_swap(total, 1)
+    student_got = jnp.concatenate([step(student_head), student_hidden], axis=0)
+    teacher_grads = (teacher_unblock(step(teacher_head)), *hidden_unblock(teacher_hidden))
+    student_got = to_plane(split_shards(student_got))
+    total = total + step(other)
+    other = plane_swap(total, 2)
+    student_got = step(student_got)
+    teacher_dx, student_dx, teacher_out, student_out = step(teacher_dx, student_dx, teacher_out, student_out)
+    student_grads = (student_unblock(student_got[:, :student_count]), *hidden_unblock(student_got[:, student_count:]))
+    total = total + other
+    teacher_out, teacher_dx = teacher_out[None], teacher_dx[None]
+    student_out, student_dx = student_out[None], student_dx[None]
+
+    def matrices(grads):
+        stack, fc_grad, proj_grad = grads
+        return (
+            wide(jnp.transpose(stack[:3], (0, 2, 1))), wide(stack[3]),
+            wide(jnp.transpose(fc_grad)), wide(proj_grad),
+        )
+
+    own = y * 4 + rank
+    units, student_units = teacher_fc.size // 8, student_fc.size // 8
+    columns, student_columns = teacher_columns // 4, student_columns // 4
+    hidden_grads = pick(total[:32].reshape(4, 8, lanes), z)
+    teacher_fc = hidden_grads[:, :units].reshape(-1)
+    student_fc = hidden_grads[:, units : units + student_units].reshape(-1)
+    column_grads = pick(total[32:64].reshape(4, 8, lanes), z)
+    block = column_grads[:, :columns].reshape(2, 2, 2, 2, -1, HD // 4)
+    teacher_qv_grad = jnp.transpose(block, (3, 0, 4, 1, 2, 5)).reshape(2, -1)
+    block = column_grads[:, columns : columns + student_columns].reshape(8, 2, -1, HD // 8)
+    student_qv_grad = jnp.transpose(block, (1, 2, 0, 3)).reshape(2, -1)
+    tall = total[64:].reshape(-1, 8, lanes)
+    runs = teacher_width // lanes
+
+    def width_grads(tall, count):
+        tall = jnp.concatenate([tall[i] for i in range(count)], axis=1)[:6]
+        return tuple(pick(tall.reshape(6, 8, -1), own, 1))
+
+    def arranged(outputs, input_grad, grads, sums, qv_grad, fc_grad):
+        return (
+            outputs, input_grad, sums[0], sums[1], grads[0], qv_grad, grads[1],
+            sums[2], sums[3], sums[4], grads[2], fc_grad, grads[3], sums[5],
+        )
+
+    return arranged(
+        teacher_out, teacher_dx, matrices(teacher_grads), width_grads(tall[:runs], runs), teacher_qv_grad, teacher_fc
+    ) + arranged(
+        student_out, student_dx, matrices(student_grads), width_grads(tall[runs:], student_width // lanes), student_qv_grad, student_fc
+    )
+
+
+def on_plane(spec):
+    names = {"dp": PLANE, "tensor": "z"}
+    return P(*(names.get(entry, None) for entry in spec))
+
+
 def solution(mesh):
     in_specs = (
         P("dp", "tensor", None),
@@ -442,6 +1584,15 @@
         P("tensor", "dp"),
         P("dp"),
     )
+    if tuple(mesh.devices.shape) == (8, 4):
+        finer = Mesh(mesh.devices.reshape(2, 2, 2, 4), EVERY)
+        return jax.shard_map(
+            on_pairs,
+            mesh=finer,
+            in_specs=tuple(on_plane(spec) for spec in in_specs),
+            out_specs=tuple(on_plane(spec) for spec in out_specs),
+            check_vma=False,
+        )
     return jax.shard_map(
         on_device, mesh=mesh, in_specs=in_specs, out_specs=out_specs, check_vma=False
     )

time: 1430 us -> 718 us (0.50)
  waiting for transfers between devices: 967 us -> 218 us
  matrix products: 200 us -> 2.21 us
  Pallas kernels: 0 us -> 188 us
  starting transfers between devices: 2.84 us -> 154 us
  blocking collectives: 96.9 us -> 0 us
  other arithmetic: 80.6 us -> 55.2 us
  local copies, waits for them, and re-layouts: 57.9 us -> 76.1 us
    reduce_scatter x13 -> x2, waiting for transfers between devices: 474 us -> 0.02 us  [on_pairs(): lax.psum_scatter(grads, ('y', 'z'), scatter_dimension=0, tiled=True)]
    all_gather x13 -> x2, waiting for transfers between devices: 383 us -> 0.04 us  [the longest x1 0.02 us: on_pairs(): student_weights = lax.all_gather(sf0, ('y', 'z'), axis=0, tiled=True)]
    dot_general x46 -> x6, matrix products: 194 us -> 2.21 us  [the longest x3 1.78 us: spread(): return jnp.dot(hot, values, precision=lax.Precision.HIGHEST)]
    pallas_call x0 -> x18, Pallas kernels: none -> 188 us  [the longest x10 162 us: matmul_call(): pl.pallas_call(kernel, in_specs=specs, out_specs=[spec for _, _, spec in...]
    ppermute x0 -> x84, waiting for transfers between devices: none -> 151 us  [the longest x15 82.7 us: plane_swap(): return lax.ppermute(values, 'z', tuple(((i, i ^ bit) for i in range(4))))]
    ppermute x0 -> x84, starting transfers between devices: none -> 118 us  [the longest x59 68.4 us: swap(): return lax.ppermute(values, axis, ((0, 1), (1, 0)))]
    unnamed x32 -> x4, waiting for transfers between devices: 110 us -> 0.07 us
    all_to_all x0 -> x7, waiting for transfers between devices: none -> 67.6 us  [to_plane(): return lax.all_to_all(blocks, PLANE, 0, 0)]
  transfers between devices with their start and end apart: 29 -> 95, of which waited for: 25 -> 32; matrix products, arithmetic and copies ran while one was open for 22% -> 15% of each run, Pallas kernels for 0% -> 26%
where the time goes in v2:
time: 718 us; the launch traced here: 710 us
  waiting for transfers between devices  218 us (30%)
  Pallas kernels  188 us (26%)
  starting transfers between devices  154 us (21%)
  local copies, waits for them, and re-layouts  76.1 us (11%)
  other arithmetic  55.2 us (8%)
  between operations  16.6 us (2%)
    pallas_call x10, Pallas kernels, matmul_call(): pl.pallas_call(kernel, in_specs=specs, out_specs=[spec for _, _, spec in...  162 us
    ppermute x15, waiting for transfers between devices, plane_swap(): return lax.ppermute(values, 'z', tuple(((i, i ^ bit) for i in range(4))))  82.7 us
    ppermute x59, starting transfers between devices, swap(): return lax.ppermute(values, axis, ((0, 1), (1, 0)))  68.4 us
    ppermute x59, waiting for transfers between devices, swap(): return lax.ppermute(values, axis, ((0, 1), (1, 0)))  67.9 us
    all_to_all x7, waiting for transfers between devices, to_plane(): return lax.all_to_all(blocks, PLANE, 0, 0)  67.6 us
    all_to_all x7, starting transfers between devices, to_plane(): return lax.all_to_all(blocks, PLANE, 0, 0)  35 us
    unnamed x237, local copies, waits for them, and re-layouts  26.8 us
    pallas_call x8, Pallas kernels, row_call(): pl.pallas_call(kernel, grid=(1,), in_specs=[spec(a.shape) for a in args],...  25.9 us
  transfers between devices with their start and end apart: 95, of which 32 were waited for; matrix products, arithmetic and copies ran while one was open for 15% of the time, Pallas kernels for 26%

profile of v2, /device:TPU:0, one launch (start us, length us, event | category | flops | bytes accessed | tf_op | source)
XLA Modules:
  0.0 709.8 jit_solution(12401516036259364442)
XLA Ops:
  27.8 16.4 %all-to-all-done = bf16[8,208,160]{1,2,0:T(8,128)(2,1)S(1)} async-done(((bf16[8,208,160]{1,2,0:T(8,128)(2,1)}), bf16[8,208,160]{1,2,0:T(8,128)(2,1)S(1)}, u32[]{:S(2)}, u32[]{:S(2)}) %all-to-all-start) | async-done | bytes 532512 | tf_op jit(solution)/shard_map/all_to_all | solution.py:463
  82.1 9.8 %collective-permute-done.1 = bf16[192,1280]{1,0:T(8,128)(2,1)S(1)} collective-permute-done((bf16[192,1280]{1,0:T(8,128)(2,1)}, bf16[192,1280]{1,0:T(8,128)(2,1)S(1)}, u32[]{:S(2)}, u32[]{:S(2)}) %collective-permute-start.1) | collective-permute-done | bytes 491552 | tf_op jit(solution)/shard_map/ppermute | solution.py:480
  93.8 16.5 %collective-permute-done.6 = bf16[192,1280]{1,0:T(8,128)(2,1)S(1)} collective-permute-done((bf16[192,1280]{1,0:T(8,128)(2,1)}, bf16[192,1280]{1,0:T(8,128)(2,1)S(1)}, u32[]{:S(2)}, u32[]{:S(2)}) %collective-permute-start.6) | collective-permute-done | bytes 491552 | tf_op jit(solution)/shard_map/ppermute | solution.py:480
  129.1 7.9 %collective-permute-done.8 = bf16[192,1280]{1,0:T(8,128)(2,1)} collective-permute-done((bf16[192,1280]{1,0:T(8,128)(2,1)S(1)}, bf16[192,1280]{1,0:T(8,128)(2,1)}, u32[]{:S(2)}, u32[]{:S(2)}) %collective-permute-start.8) | collective-permute-done | bytes 491552 | tf_op jit(solution)/shard_map/ppermute | solution.py:394
  157.7 24.0 %front.2 = (bf16[3,1024,384]{2,1,0:T(8,128)(2,1)}, bf16[1024,1280]{1,0:T(8,128)(2,1)}, bf16[4,384,1280]{2,1,0:T(8,128)(2,1)}, bf16[1024,384]{1,0:T(8,128)(2,1)},...) custom-call(bf16[256,1280]{1,0:T(8,128)(2,1)} %first_norm.2.refs_0_, ...), custom_call_target="tpu_custom_call" | custom-call | flops 352321536 | bytes 819780 | tf_op jit(solution)/shard_map/front/pallas_call | solution.py:731
  204.0 30.5 %all-to-all-done.3 = bf16[8,192,96]{2,1,0:T(8,128)(2,1)S(1)} async-done(((bf16[8,192,96]{2,1,0:T(8,128)(2,1)}), bf16[8,192,96]{2,1,0:T(8,128)(2,1)S(1)}, u32[]{:S(2)}, u32[]{:S(2)}) %all-to-all-start.3) | async-done | bytes 294944 | tf_op jit(solution)/shard_map/all_to_all | solution.py:463
  244.7 7.3 %collective-permute-done.25.refs_7_ = bf16[96,768]{1,0:T(8,128)(2,1)S(1)} collective-permute-done((bf16[96,768]{1,0:T(8,128)(2,1)}, bf16[96,768]{1,0:T(8,128)(2,1)S(1)}, u32[]{:S(2)}, u32[]{:S(2)}) %collective-permute-start.25) | collective-permute-done | bytes 147488 | tf_op jit(solution)/shard_map/ppermute | solution.py:480
  262.7 14.5 %front.3 = (bf16[3,1024,192]{2,1,0:T(8,128)(2,1)}, bf16[1024,768]{1,0:T(8,128)(2,1)}, bf16[4,192,768]{2,1,0:T(8,128)(2,1)}, bf16[1024,192]{1,0:T(8,128)(2,1)}, b...) custom-call(bf16[256,768]{1,0:T(8,128)(2,1)} %first_norm.3.refs_0_, ...), custom_call_target="tpu_custom_call" | custom-call | flops 125829120 | bytes 344354 | tf_op jit(solution)/shard_map/front/pallas_call | solution.py:731
  277.2 12.3 %collective-permute-start.34 = (bf16[512,768]{1,0:T(8,128)(2,1)}, bf16[512,768]{1,0:T(8,128)(2,1)S(1)}, u32[]{:S(2)}, u32[]{:S(2)}) collective-permute-start(bf16[512,768]{1,0:T(8,128)(2,1)} %get-tuple-element.234), channel_id=1, source_target_pairs={{0,4},{4,0},{1,5},{5,1},{2,6},{6,2},{3,7},{7,3},{8,12},{12,8},{9,1... | collective-permute-start | bytes 2359304 | tf_op jit(solution)/shard_map/ppermute | solution.py:394
  295.4 20.2 %mlp_main.2 = (bf16[1024,1280]{1,0:T(8,128)(2,1)}, bf16[1024,1280]{1,0:T(8,128)(2,1)}, bf16[1024,1280]{1,0:T(8,128)(2,1)}, bf16[1024,1280]{1,0:T(8,128)(2,1)}, b...) custom-call(bf16[256,1280]{1,0:T(8,128)(2,1)} %get-tuple-element.237.refs_0_, ...), custom_call_target="tpu_custom_call" | custom-call | flops 629145600 | bytes 1475200 | tf_op jit(solution)/shard_map/mlp_main/pallas_call | solution.py:731
  327.8 12.6 %collective-permute-done.42.c_ref = bf16[256,768]{1,0:T(8,128)(2,1)S(1)} collective-permute-done((bf16[256,768]{1,0:T(8,128)(2,1)S(1)}, bf16[256,768]{1,0:T(8,128)(2,1)S(1)}, u32[]{:S(2)}, u32[]{:S(2)}) %collective-permute-start.42) | collective-permute-done | bytes 393248 | tf_op jit(solution)/shard_map/ppermute | solution.py:394
  343.9 17.7 %mlp_rest.2 = (bf16[512,1280]{1,0:T(8,128)(2,1)}, bf16[512,1280]{1,0:T(8,128)(2,1)}, bf16[2560,1280]{1,0:T(8,128)(2,1)}) custom-call(bf16[1024,1280]{1,0:T(8,128)(2,1)} %get-tuple-element.251.refs_0_, bf16[1024,1280]{1,0:T(8,128)(2,1)} %get-tuple-element.252.refs_1_, bf16[1024,1280]{1,0:T(8,128)(2,1)} %get-tuple-element.253.refs_2_, ...), custom_call_target="tpu_custom_call" | custom-call | flops 629145600 | bytes 2129920 | tf_op jit(solution)/shard_map/mlp_rest/pallas_call | solution.py:731
  367.0 9.5 %collective-permute-done.40 = bf16[192,1280]{1,0:T(8,128)(2,1)S(1)} collective-permute-done((bf16[192,1280]{1,0:T(8,128)(2,1)S(1)}, bf16[192,1280]{1,0:T(8,128)(2,1)S(1)}, u32[]{:S(2)}, u32[]{:S(2)}) %collective-permute-start.40) | collective-permute-done | bytes 491552 | tf_op jit(solution)/shard_map/ppermute | solution.py:394
  384.9 7.8 %collective-permute-done.47.refs_5_ = bf16[256,768]{1,0:T(8,128)(2,1)S(1)} collective-permute-done((bf16[256,768]{1,0:T(8,128)(2,1)S(1)}, bf16[256,768]{1,0:T(8,128)(2,1)S(1)}, u32[]{:S(2)}, u32[]{:S(2)}) %collective-permute-start.47) | collective-permute-done | bytes 393248 | tf_op jit(solution)/shard_map/ppermute | solution.py:394
  396.1 11.5 %mlp_main.3 = (bf16[1024,768]{1,0:T(8,128)(2,1)}, bf16[1024,768]{1,0:T(8,128)(2,1)}, bf16[1024,768]{1,0:T(8,128)(2,1)}, bf16[1024,768]{1,0:T(8,128)(2,1)}, bf16[...) custom-call(bf16[256,768]{1,0:T(8,128)(2,1)} %get-tuple-element.261.refs_0_, ...), custom_call_target="tpu_custom_call" | custom-call | flops 226492416 | bytes 688512 | tf_op jit(solution)/shard_map/mlp_main/pallas_call | solution.py:731
  413.4 32.6 %rear.2 = (bf16[1024,384]{1,0:T(8,128)(2,1)}, bf16[1024,384]{1,0:T(8,128)(2,1)}, bf16[1024,384]{1,0:T(8,128)(2,1)}, bf16[1024,1280]{1,0:T(8,128)(2,1)}, bf16[512...) custom-call(bf16[256,1280]{1,0:T(8,128)(2,1)} %get-tuple-element.269.refs_0_, bf16[256,1280]{1,0:T(8,128)(2,1)} %copy-done.29, ...), custom_call_target="tpu_custom_call" | custom-call | flops 503316480 | bytes 1215492 | tf_op jit(solution)/shard_map/rear/pallas_call | solution.py:731
  450.7 7.9 %collective-permute-done.54.c_ref = bf16[256,768]{1,0:T(8,128)(2,1)S(1)} collective-permute-done((bf16[256,768]{1,0:T(8,128)(2,1)}, bf16[256,768]{1,0:T(8,128)(2,1)S(1)}, u32[]{:S(2)}, u32[]{:S(2)}) %collective-permute-start.54) | collective-permute-done | bytes 393248 | tf_op jit(solution)/shard_map/ppermute | solution.py:394
  464.2 9.7 %head_weight_grads.2 = (bf16[2,192,1280]{2,1,0:T(8,128)(2,1)}, bf16[2,192,1280]{2,1,0:T(8,128)(2,1)}, bf16[2,192,1280]{2,1,0:T(8,128)(2,1)}, bf16[2,192,1280]{2,1,0:T(8,128)(2,1)}) custom-call(bf16[1024,384]{1,0:T(8,128)(2,1)} %get-tuple-element.285.refs_0_, bf16[1024,384]{1,0:T(8,128)(2,1)} %get-tuple-element.286.refs_1_, ...), custom_call_target="tpu_custom_call" | custom-call | flops 251658240 | bytes 1048576 | tf_op jit(solution)/shard_map/head_weight_grads/pallas_call | solution.py:731
  484.2 8.6 %mlp_rest.3 = (bf16[512,768]{1,0:T(8,128)(2,1)}, bf16[512,768]{1,0:T(8,128)(2,1)}, bf16[1536,768]{1,0:T(8,128)(2,1)}) custom-call(bf16[1024,768]{1,0:T(8,128)(2,1)} %get-tuple-element.294.refs_0_, bf16[1024,768]{1,0:T(8,128)(2,1)} %get-tuple-element.295.refs_1_, bf16[1024,768]{1,0:T(8,128)(2,1)} %get-tuple-element.296.refs_2_, ...), custom_call_target="tpu_custom_call" | custom-call | flops 226492416 | bytes 1081344 | tf_op jit(solution)/shard_map/mlp_rest/pallas_call | solution.py:731
  524.5 17.9 %rear.3 = (bf16[1024,192]{1,0:T(8,128)(2,1)}, bf16[1024,192]{1,0:T(8,128)(2,1)}, bf16[1024,192]{1,0:T(8,128)(2,1)}, bf16[1024,768]{1,0:T(8,128)(2,1)}, bf16[512,...) custom-call(bf16[256,768]{1,0:T(8,128)(2,1)} %get-tuple-element.305.refs_0_, bf16[256,768]{1,0:T(8,128)(2,1)} %copy-done.50, ...), custom_call_target="tpu_custom_call" | custom-call | flops 201326592 | bytes 542210 | tf_op jit(solution)/shard_map/rear/pallas_call | solution.py:731
  557.6 15.7 %all-to-all-done.4 = bf16[8,320,160]{1,2,0:T(8,128)(2,1)S(1)} async-done(((bf16[8,320,160]{1,2,0:T(8,128)(2,1)}), bf16[8,320,160]{1,2,0:T(8,128)(2,1)S(1)}, u32[]{:S(2)}, u32[]{:S(2)}) %all-to-all-start.4) | async-done | bytes 819232 | tf_op jit(solution)/shard_map/all_to_all | solution.py:463
  609.6 24.3 %collective-permute-done.78 = bf16[192,1280]{1,0:T(8,128)(2,1)S(1)} collective-permute-done((bf16[192,1280]{1,0:T(8,128)(2,1)S(1)}, bf16[192,1280]{1,0:T(8,128)(2,1)S(1)}, u32[]{:S(2)}, u32[]{:S(2)}) %collective-permute-start.78) | collective-permute-done | bytes 491552 | tf_op jit(solution)/shard_map/ppermute | solution.py:480
  663.5 7.6 %all-to-all-start.5 = ((bf16[8,288,96]{2,1,0:T(8,128)(2,1)}), bf16[8,288,96]{2,1,0:T(8,128)(2,1)S(1)}, u32[]{:S(2)}, u32[]{:S(2)}) async-start(bf16[8,288,96]{2,1,0:T(8,128)(2,1)} %bitcast.206), calls=%async_computation.7 | async-start | bytes 1179648 | tf_op jit(solution)/shard_map/all_to_all | solution.py:463
  675.2 13.1 %collective-permute-done.83 = f32[128,256]{1,0:T(8,128)S(1)} collective-permute-done((f32[128,256]{1,0:T(8,128)S(1)}, f32[128,256]{1,0:T(8,128)S(1)}, u32[]{:S(2)}, u32[]{:S(2)}) %collective-permute-start.83) | collective-permute-done | bytes 131104 | tf_op jit(solution)/shard_map/ppermute | solution.py:480
  (647 shorter events, 337.3 us)
Async XLA Ops:
  21.8 40.9 %collective-permute-start.3 = (bf16[256,1280]{1,0:T(8,128)(2,1)}, bf16[256,1280]{1,0:T(8,128)(2,1)S(1)}, u32[]{:S(2)}, u32[]{:S(2)}) collective-permute-start(bf16[256,1280]{1,0:T(8,128)(2,1)} %bitcast.24), channel_id=1, source_target_pairs={{0,0},{1,8},{2,4},{3,12},{4,9},{5,1},{6,13},{7,5},{8,2},{9,10},{10... | collective-permute-start | bytes 1966088 | tf_op jit(solution)/shard_map/ppermute | solution.py:419
  55.1 38.4 %all-to-all-start.2 = ((bf16[8,320,160]{1,2,0:T(8,128)(2,1)}), bf16[8,320,160]{1,2,0:T(8,128)(2,1)S(1)}, u32[]{:S(2)}, u32[]{:S(2)}) async-start(bf16[8,320,160]{1,2,0:T(8,128)(2,1)} %pad_maximum_fusion), calls=%async_computation.2 | async-start | bytes 1966080 | tf_op jit(solution)/shard_map/all_to_all | solution.py:463
  58.7 236.7 %all-gather.3.cloned.1.call-start = ((), (), s32[]{:S(2)}) async-start(), calls=%async_computation.9 | async-start | bytes 7372800 | tf_op jit(solution)/shard_map/all_gather | solution.py:1223
  77.4 35.0 %collective-permute-start.12 = (bf16[256,768]{1,0:T(8,128)(2,1)}, bf16[256,768]{1,0:T(8,128)(2,1)S(1)}, u32[]{:S(2)}, u32[]{:S(2)}) collective-permute-start(bf16[256,768]{1,0:T(8,128)(2,1)} %bitcast.29), channel_id=1, source_target_pairs={{0,0},{1,8},{2,4},{3,12},{4,9},{5,1},{6,13},{7,5},{8,2},{9,10},{10... | collective-permute-start | bytes 1179656 | tf_op jit(solution)/shard_map/ppermute | solution.py:419
  91.8 37.2 %collective-permute-start = (bf16[192,1280]{1,0:T(8,128)(2,1)}, bf16[192,1280]{1,0:T(8,128)(2,1)S(1)}, u32[]{:S(2)}, u32[]{:S(2)}) collective-permute-start(bf16[192,1280]{1,0:T(8,128)(2,1)} %copy.302), channel_id=1, source_target_pairs={{0,16},{16,0},{1,17},{17,1},{2,18},{18,2},{3,19},{19,3},{4,20},{20... | collective-permute-start | bytes 1474568 | tf_op jit(solution)/shard_map/ppermute | solution.py:394
  93.5 35.6 %collective-permute-start.4 = (bf16[192,1280]{1,0:T(8,128)(2,1)S(1)}, bf16[192,1280]{1,0:T(8,128)(2,1)}, u32[]{:S(2)}, u32[]{:S(2)}) collective-permute-start(bf16[192,1280]{1,0:T(8,128)(2,1)S(1)} %collective-permute-done.1), channel_id=1, source_target_pairs={{0,16},{16,0},{1,17},{17,1},{2,18},{18,2},{3,19},{19,3},{4,20},{20... | collective-permute-start | bytes 1474568 | tf_op jit(solution)/shard_map/ppermute | solution.py:394
  186.9 49.5 %collective-permute-start.22 = (bf16[256,1280]{1,0:T(8,128)(2,1)S(1)}, bf16[256,1280]{1,0:T(8,128)(2,1)S(1)}, u32[]{:S(2)}, u32[]{:S(2)}) collective-permute-start(bf16[256,1280]{1,0:T(8,128)(2,1)S(1)} %add_convert_fusion.5), channel_id=1, source_target_pairs={{0,8},{8,0},{1,9},{9,1},{2,10},{10,2},{3,11},{11,3},{4,12},{12,4},... | collective-permute-start | bytes 1966088 | tf_op jit(solution)/shard_map/ppermute | solution.py:394
  193.2 42.6 %collective-permute-start.23 = (bf16[256,768]{1,0:T(8,128)(2,1)S(1)}, bf16[256,768]{1,0:T(8,128)(2,1)}, u32[]{:S(2)}, u32[]{:S(2)}) collective-permute-start(bf16[256,768]{1,0:T(8,128)(2,1)S(1)} %copy-done.17), channel_id=1, source_target_pairs={{0,8},{8,0},{1,9},{9,1},{2,10},{10,2},{3,11},{11,3},{4,12},{12,4},... | collective-permute-start | bytes 1179656 | tf_op jit(solution)/shard_map/ppermute | solution.py:394
  195.3 39.2 %all-to-all-start.3 = ((bf16[8,192,96]{2,1,0:T(8,128)(2,1)}), bf16[8,192,96]{2,1,0:T(8,128)(2,1)S(1)}, u32[]{:S(2)}, u32[]{:S(2)}) async-start(bf16[8,192,96]{2,1,0:T(8,128)(2,1)} %pad_maximum_fusion.10), calls=%async_computation.3 | async-start | bytes 786432 | tf_op jit(solution)/shard_map/all_to_all | solution.py:463
  199.6 195.8 %all-gather.5.cloned.1.call-start = ((), (), s32[]{:S(2)}) async-start(), calls=%async_computation.10 | async-start | bytes 2654208 | tf_op jit(solution)/shard_map/all_gather | solution.py:1267
  200.2 44.0 %collective-permute-start.13 = (bf16[256,1280]{1,0:T(8,128)(2,1)}, bf16[256,1280]{1,0:T(8,128)(2,1)S(1)}, u32[]{:S(2)}, u32[]{:S(2)}) collective-permute-start(bf16[256,1280]{1,0:T(8,128)(2,1)} %bitcast.283), channel_id=1, source_target_pairs={{0,0},{1,8},{2,4},{3,12},{4,9},{5,1},{6,13},{7,5},{8,2},{9,10},{10... | collective-permute-start | bytes 1966088 | tf_op jit(solution)/shard_map/ppermute | solution.py:419
  235.9 280.6 %reduce-scatter.3.cloned.1.call-start = ((), (), s32[]{:S(2)}) async-start(), calls=%async_computation.11 | async-start | bytes 7372800 | tf_op jit(solution)/shard_map/reduce_scatter | solution.py:1316
  244.2 45.9 %collective-permute-start.35 = (bf16[256,1280]{1,0:T(8,128)(2,1)S(1)}, bf16[256,1280]{1,0:T(8,128)(2,1)}, u32[]{:S(2)}, u32[]{:S(2)}) collective-permute-start(bf16[256,1280]{1,0:T(8,128)(2,1)S(1)} %collective-permute-done.13.refs_4_.g_ref), channel_id=1, source_target_pairs={{0,8},{8,0},{1,9},{9,1},{2,10},{10,2},{3,11},{11,3},{4,12},{12,4},... | collective-permute-start | bytes 1966088 | tf_op jit(solution)/shard_map/ppermute | solution.py:394
  361.6 295.2 %reduce-scatter.5.cloned.1.call-start = ((), (), s32[]{:S(2)}) async-start(), calls=%async_computation.12 | async-start | bytes 2654208 | tf_op jit(solution)/shard_map/reduce_scatter | solution.py:1374
  504.9 37.5 %collective-permute-start.63 = (bf16[2,192,1280]{2,1,0:T(8,128)(2,1)}, bf16[2,192,1280]{2,1,0:T(8,128)(2,1)}, u32[]{:S(2)}, u32[]{:S(2)}) collective-permute-start(bf16[2,192,1280]{2,1,0:T(8,128)(2,1)} %pad_maximum_fusion.5), channel_id=1, source_target_pairs={{0,16},{16,0},{1,17},{17,1},{2,18},{18,2},{3,19},{19,3},{4,20},{20... | collective-permute-start | bytes 2949128 | tf_op jit(solution)/shard_map/ppermute | solution.py:394
  507.6 188.8 %collective-permute-start.57 = (bf16[256,1280]{1,0:T(8,128)(2,1)}, bf16[256,1280]{1,0:T(8,128)(2,1)}, u32[]{:S(2)}, u32[]{:S(2)}) collective-permute-start(bf16[256,1280]{1,0:T(8,128)(2,1)} %get-tuple-element.301), channel_id=1, source_target_pairs={{0,0},{8,1},{4,2},{12,3},{9,4},{1,5},{13,6},{5,7},{2,8},{10,9},{6,... | collective-permute-start | bytes 1966088 | tf_op jit(solution)/shard_map/ppermute | solution.py:423
  516.5 73.5 %collective-permute-start.72 = (bf16[2,192,1280]{2,1,0:T(8,128)(2,1)}, bf16[2,192,1280]{2,1,0:T(8,128)(2,1)}, u32[]{:S(2)}, u32[]{:S(2)}) collective-permute-start(bf16[2,192,1280]{2,1,0:T(8,128)(2,1)} %pad_maximum_fusion.6), channel_id=1, source_target_pairs={{0,16},{16,0},{1,17},{17,1},{2,18},{18,2},{3,19},{19,3},{4,20},{20... | collective-permute-start | bytes 2949128 | tf_op jit(solution)/shard_map/ppermute | solution.py:394
  520.6 52.6 %all-to-all-start.4 = ((bf16[8,320,160]{1,2,0:T(8,128)(2,1)}), bf16[8,320,160]{1,2,0:T(8,128)(2,1)S(1)}, u32[]{:S(2)}, u32[]{:S(2)}) async-start(bf16[8,320,160]{1,2,0:T(8,128)(2,1)} %bitcast.69), calls=%async_computation.5 | async-start | bytes 1966080 | tf_op jit(solution)/shard_map/all_to_all | solution.py:463
  550.7 39.3 %collective-permute-start.71 = (bf16[2,192,1280]{2,1,0:T(8,128)(2,1)}, bf16[2,192,1280]{2,1,0:T(8,128)(2,1)}, u32[]{:S(2)}, u32[]{:S(2)}) collective-permute-start(bf16[2,192,1280]{2,1,0:T(8,128)(2,1)} %add_convert_fusion), channel_id=1, source_target_pairs={{0,1},{1,0},{2,3},{3,2},{4,5},{5,4},{6,7},{7,6},{8,9},{9,8},{10,11... | collective-permute-start | bytes 2949128 | tf_op jit(solution)/shard_map/ppermute | solution.py:480
  597.8 98.5 %collective-permute-start.66 = (bf16[256,768]{1,0:T(8,128)(2,1)}, bf16[256,768]{1,0:T(8,128)(2,1)}, u32[]{:S(2)}, u32[]{:S(2)}) collective-permute-start(bf16[256,768]{1,0:T(8,128)(2,1)} %get-tuple-element.332), channel_id=1, source_target_pairs={{0,0},{8,1},{4,2},{12,3},{9,4},{1,5},{13,6},{5,7},{2,8},{10,9},{6,... | collective-permute-start | bytes 1179656 | tf_op jit(solution)/shard_map/ppermute | solution.py:423
  605.0 37.7 %collective-permute-start.77 = (f32[128,256]{1,0:T(8,128)S(1)}, f32[128,256]{1,0:T(8,128)}, u32[]{:S(2)}, u32[]{:S(2)}) collective-permute-start(f32[128,256]{1,0:T(8,128)S(1)} %add.330), channel_id=1, source_target_pairs={{0,8},{8,0},{1,9},{9,1},{2,10},{10,2},{3,11},{11,3},{4,12},{12,4},... | collective-permute-start | bytes 393224 | tf_op jit(solution)/shard_map/ppermute | solution.py:394
  609.5 40.7 %collective-permute-start.74 = (bf16[256,768]{1,0:T(8,128)(2,1)}, bf16[256,768]{1,0:T(8,128)(2,1)}, u32[]{:S(2)}, u32[]{:S(2)}) collective-permute-start(bf16[256,768]{1,0:T(8,128)(2,1)} %add_convert_fusion.7), channel_id=1, source_target_pairs={{0,8},{8,0},{1,9},{9,1},{2,10},{10,2},{3,11},{11,3},{4,12},{12,4},... | collective-permute-start | bytes 1179656 | tf_op jit(solution)/shard_map/ppermute | solution.py:394
  650.2 46.2 %collective-permute-start.73 = (bf16[256,1280]{1,0:T(8,128)(2,1)}, bf16[256,1280]{1,0:T(8,128)(2,1)}, u32[]{:S(2)}, u32[]{:S(2)}) collective-permute-start(bf16[256,1280]{1,0:T(8,128)(2,1)} %add_convert_fusion.1), channel_id=1, source_target_pairs={{0,0},{8,1},{4,2},{12,3},{9,4},{1,5},{13,6},{5,7},{2,8},{10,9},{6,... | collective-permute-start | bytes 1966088 | tf_op jit(solution)/shard_map/ppermute | solution.py:423
  661.8 34.5 %collective-permute-start.79 = (bf16[256,768]{1,0:T(8,128)(2,1)}, bf16[256,768]{1,0:T(8,128)(2,1)S(1)}, u32[]{:S(2)}, u32[]{:S(2)}) collective-permute-start(bf16[256,768]{1,0:T(8,128)(2,1)} %add_convert_fusion.6), channel_id=1, source_target_pairs={{0,0},{8,1},{4,2},{12,3},{9,4},{1,5},{13,6},{5,7},{2,8},{10,9},{6,... | collective-permute-start | bytes 1179656 | tf_op jit(solution)/shard_map/ppermute | solution.py:423
  (177 other events, 2138.6 us)
Sparse Core Ops, SparseCore 0:
  138.4 130.4 all-gather.2
  271.6 50.9 all-gather.4
  361.7 122.6 reduce-scatter.2
  506.6 87.2 reduce-scatter.4

commit v3 on v2

--- a/solution.py
+++ b/solution.py
@@ -1164,9 +1164,10 @@
     deep = jnp.concatenate([part.reshape(-1, 128) for part in parts], axis=0)
     deep = [deep] + [plane_swap(deep, step) for step in (1, 2, 3)]
 
-    student_got = to_plane(after(student_blocks(student_in[4], student_in[6]), teacher_got))
-    teacher_hidden_got = to_plane(after(hidden_blocks(teacher_in[10], teacher_in[12]), student_got))
-    student_hidden_got = to_plane(after(hidden_blocks(student_in[10], student_in[12]), teacher_hidden_got))
+    blocks = jnp.concatenate(
+        [student_blocks(student_in[4], student_in[6]), hidden_blocks(student_in[10], student_in[12])], axis=1
+    )
+    student_got = to_plane(after(blocks, teacher_got))
 
     vectors = teacher_got[:, teacher_count:]
 
@@ -1191,12 +1192,12 @@
     )
     teacher_normed = [normed, swap(normed, "x"), swap(normed, "c")]
     step.mark(normed)
-    student_cross = cross(step(join_shards(student_got)))
+    student_cross = cross(step(join_shards(student_got[:, :student_count])))
     t2 = step(t2)
     t3, t2y = plane_swap(t2, 1), swap(t2, "y")
     t1 = step(t1)
     t1y = swap(t1, "y")
-    tf0 = step(join_shards(teacher_hidden_got))
+    teacher_hidden_got = to_plane(after(hidden_blocks(teacher_in[10], teacher_in[12]), t1))
     teacher_normed[1] = step(teacher_normed[1])
     teacher_normed.append(swap(teacher_normed[1], "c"))
     t3 = step(t3)
@@ -1218,10 +1219,11 @@
     s3, s2y = plane_swap(s2, 1), swap(s2, "y")
     s1 = step(s1)
     s1y = swap(s1, "y")
+    teacher_up = rows_out(after(teacher_in[1][0], s1))
+    tf0 = step(join_shards(teacher_hidden_got))
     t0y, t1y, t2y, t3y = step(t0y, t1y, t2y, t3y)
     own_over, near_over = halves(t0y, t1y, t2y, t3y)
     teacher_weights = lax.all_gather(after(tf0, t3y), ("y", "z"), axis=0, tiled=True)
-    teacher_up, student_up = rows_out(after(teacher_in[1][0], t3y)), rows_out(after(student_in[1][0], t3y))
 
     deep = jnp.stack(deep)
     deep = [deep[:, limits[i] : limits[i + 1]].reshape(4, -1) for i in range(5)]
@@ -1263,10 +1265,8 @@
     step.mark(t_near)
     t_got = swap(t_far, "c")
     t_over = swap(step(ahead_sum(t_near, t_got)), "x")
-    sf0 = step(join_shards(student_hidden_got))
+    sf0 = step(join_shards(student_got[:, student_count:]))
     student_weights = lax.all_gather(sf0, ("y", "z"), axis=0, tiled=True)
-    student_normed[1] = step(student_normed[1])
-    student_normed.append(swap(student_normed[1], "c"))
     bias_out, gain_two, shift_two = teacher_vectors[2:5]
     full32 = (teacher_rows.shape, jnp.float32)
     t_middle, normed = row_call(
@@ -1275,10 +1275,13 @@
     )
     step.mark(normed)
     teacher_normed = [normed, swap(normed, "x"), swap(normed, "c")]
+    student_normed[1] = step(student_normed[1])
+    student_normed.append(swap(student_normed[1], "c"))
+    s3 = step(s3)
+    s3y = swap(s3, "y")
     teacher_up = step(teacher_up)
     teacher_ups = [teacher_up, swap(teacher_up, "x"), swap(teacher_up, "c")]
-    s3 = step(s3)
-    s3y = swap(s3, "y")
+    student_up = rows_out(after(student_in[1][0], teacher_up))
     teacher_normed[1] = step(teacher_normed[1])
     teacher_normed.append(swap(teacher_normed[1], "c"))
 
@@ -1291,10 +1294,11 @@
     s_got = swap(s_far, "c")
     teacher_ups[1] = step(teacher_ups[1])
     teacher_ups.append(swap(teacher_ups[1], "c"))
-    s_over = swap(step(ahead_sum(s_near, s_got)), "x")
+    ahead = step(ahead_sum(s_near, s_got))
+    s_part, s_over = swap(ahead[:64], "x"), swap(ahead[64:], "x")
 
     *teacher_mlp, t_near, t_far, teacher_fc = mlp_main(
-        step(*teacher_normed), teacher_ups, teacher_weights, teacher_fc_bias
+        step(after(teacher_normed[0], s_part), *teacher_normed[1:]), teacher_ups, teacher_weights, teacher_fc_bias
     )
     step.mark(t_near)
     t_got = swap(t_far, "c")
@@ -1304,7 +1308,7 @@
     student32 = (student_rows.shape, jnp.float32)
     s_middle, normed = row_call(
         mid_norm_kernel, "mid_norm", [student32, student16],
-        student_rows, s_near, s_got, step(s_over), bias_out, gain_two, shift_two,
+        student_rows, s_near, s_got, jnp.concatenate([s_part, step(s_over)], axis=0), bias_out, gain_two, shift_two,
     )
     step.mark(normed)
     student_normed = [normed, swap(normed, "x"), swap(normed, "c")]
@@ -1391,7 +1395,6 @@
     odd_got = step(odd_got)
     th_odd_got = plane_swap(step(low(wide(th_odd) + wide(odd_got))), 1)
     s_over = swap(step(ahead_sum(s_near, s_got)), "x")
-    teacher_hidden = step(teacher_hidden)
     sh_near, sh_far = head_weight_grads(
         [step(s_dq), s_dk, s_dv, heads_low], normed_all, s_grad_all, student_grad_places(student_columns),
         [(4, student_count, student_width)] * 2,
@@ -1399,6 +1402,9 @@
     student_qv_grad = jnp.stack([jnp.sum(wide(s_dq), axis=0), jnp.sum(wide(s_dv), axis=0)])
     step.mark(sh_near)
     sh_got = swap(sh_far, "y")
+    th_odd_got, even_got = step(th_odd_got, even_got)
+    th_even = wide(th_even) + wide(even_got)
+    th_even_got = plane_swap(low(th_even[1] + wide(th_odd_got[1])), 2)
     t_out_over = swap(step(ahead_sum(t_out_near, t_out_got)), "x")
     student_dx, student_one = row_call(
         first_back_kernel, "first_back", [student16, ((2, student_width), jnp.float32)],
@@ -1439,13 +1445,11 @@
     )
     total = step(total)
     other = swap(total, "c")
-    th_odd_got, even_got = step(th_odd_got, even_got)
-    th_even = wide(th_even) + wide(even_got)
-    th_even_got = plane_swap(low(th_even[1] + wide(th_odd_got[1])), 2)
     sh_total = step(wide(sh_near) + wide(sh_got))
     sh_odd_got = plane_swap(low(sh_total[1::2]), 1)
     total = total + step(other)
     other = swap(total, "x")
+    teacher_hidden = step(teacher_hidden)
     s_out_over = swap(step(ahead_sum(s_out_near, s_out_got)), "x")
     count = t_middle.shape[0]
     teacher_out = low(
@@ -1471,8 +1475,8 @@
     student_got = to_plane(split_shards(student_got))
     total = total + step(other)
     other = plane_swap(total, 2)
+    teacher_dx, student_dx, teacher_out, student_out = step(teacher_dx, student_dx, teacher_out, student_out)
     student_got = step(student_got)
-    teacher_dx, student_dx, teacher_out, student_out = step(teacher_dx, student_dx, teacher_out, student_out)
     student_grads = (student_unblock(student_got[:, :student_count]), *hidden_unblock(student_got[:, student_count:]))
     total = total + other
     teacher_out, teacher_dx = teacher_out[None], teacher_dx[None]

time: 718 us -> 706 us (0.983)
  starting transfers between devices: 154 us -> 140 us
    ppermute x59 -> x60, waiting for transfers between devices: 67.9 us -> 119 us  [swap(): return lax.ppermute(values, axis, ((0, 1), (1, 0)))]
    all_to_all x7 -> x6, waiting for transfers between devices: 67.6 us -> 20.1 us  [to_plane(): return lax.all_to_all(blocks, PLANE, 0, 0)]
    ppermute x59 -> x60, starting transfers between devices: 68.4 us -> 57.5 us  [swap(): return lax.ppermute(values, axis, ((0, 1), (1, 0)))]
    all_to_all x7 -> x6, starting transfers between devices: 35 us -> 30.8 us  [to_plane(): return lax.all_to_all(blocks, PLANE, 0, 0)]
    unnamed x237 -> x221, local copies, waits for them, and re-layouts: 26.8 us -> 26.6 us
  transfers between devices with their start and end apart: 95 -> 95, of which waited for: 32 -> 38; matrix products, arithmetic and copies ran while one was open for 15% -> 15% of each run, Pallas kernels for 26% -> 27%
where the time goes in v3:
time: 706 us; the launch traced here: 695 us
  waiting for transfers between devices  216 us (31%)
  Pallas kernels  188 us (27%)
  starting transfers between devices  140 us (20%)
  local copies, waits for them, and re-layouts  77.6 us (11%)
  other arithmetic  55.3 us (8%)
  between operations  16.7 us (2%)
    pallas_call x10, Pallas kernels, matmul_call(): pl.pallas_call(kernel, in_specs=specs, out_specs=[spec for _, _, spec in...  162 us
    ppermute x60, waiting for transfers between devices, swap(): return lax.ppermute(values, axis, ((0, 1), (1, 0)))  119 us
    ppermute x15, waiting for transfers between devices, plane_swap(): return lax.ppermute(values, 'z', tuple(((i, i ^ bit) for i in range(4))))  76.5 us
    ppermute x60, starting transfers between devices, swap(): return lax.ppermute(values, axis, ((0, 1), (1, 0)))  57.5 us
    all_to_all x6, starting transfers between devices, to_plane(): return lax.all_to_all(blocks, PLANE, 0, 0)  30.8 us
    unnamed x221, local copies, waits for them, and re-layouts  26.6 us
    pallas_call x8, Pallas kernels, row_call(): pl.pallas_call(kernel, grid=(1,), in_specs=[spec(a.shape) for a in args],...  25.9 us
    convert_element_type x14, other arithmetic, low(): return values.astype(jnp.bfloat16)  25.6 us
  transfers between devices with their start and end apart: 95, of which 38 were waited for; matrix products, arithmetic and copies ran while one was open for 15% of the time, Pallas kernels for 27%

profile of v3, /device:TPU:0, one launch (start us, length us, event | category | flops | bytes accessed | tf_op | source)
XLA Modules:
  0.0 694.7 jit_solution(2659084440222157911)
XLA Ops:
  25.1 19.0 %all-to-all-done = bf16[8,208,160]{1,2,0:T(8,128)(2,1)S(1)} async-done(((bf16[8,208,160]{1,2,0:T(8,128)(2,1)}), bf16[8,208,160]{1,2,0:T(8,128)(2,1)S(1)}, u32[]{:S(2)}, u32[]{:S(2)}) %all-to-all-start) | async-done | bytes 532512 | tf_op jit(solution)/shard_map/all_to_all | solution.py:463
  60.6 16.7 %collective-permute-done.2 = bf16[192,1280]{1,0:T(8,128)(2,1)} collective-permute-done((bf16[192,1280]{1,0:T(8,128)(2,1)}, bf16[192,1280]{1,0:T(8,128)(2,1)}, u32[]{:S(2)}, u32[]{:S(2)}) %collective-permute-start.2) | collective-permute-done | bytes 491552 | tf_op jit(solution)/shard_map/ppermute | solution.py:480
  100.0 7.3 %collective-permute-start.7 = (bf16[96,768]{1,0:T(8,128)(2,1)S(1)}, bf16[96,768]{1,0:T(8,128)(2,1)S(1)}, u32[]{:S(2)}, u32[]{:S(2)}) collective-permute-start(bf16[96,768]{1,0:T(8,128)(2,1)S(1)} %collective-permute-done.1.refs_4_), channel_id=1, source_target_pairs={{0,2},{1,3},{2,0},{3,1},{4,6},{5,7},{6,4},{7,5},{8,10},{9,11},{10,... | collective-permute-start | bytes 442376 | tf_op jit(solution)/shard_map/ppermute | solution.py:480
  125.4 10.5 %collective-permute-done.16 = bf16[192,1280]{1,0:T(8,128)(2,1)} collective-permute-done((bf16[192,1280]{1,0:T(8,128)(2,1)}, bf16[192,1280]{1,0:T(8,128)(2,1)}, u32[]{:S(2)}, u32[]{:S(2)}) %collective-permute-start.16) | collective-permute-done | bytes 491552 | tf_op jit(solution)/shard_map/ppermute | solution.py:394
  135.9 10.1 %collective-permute-done.17 = bf16[192,1280]{1,0:T(8,128)(2,1)} collective-permute-done((bf16[192,1280]{1,0:T(8,128)(2,1)}, bf16[192,1280]{1,0:T(8,128)(2,1)}, u32[]{:S(2)}, u32[]{:S(2)}) %collective-permute-start.17) | collective-permute-done | bytes 491552 | tf_op jit(solution)/shard_map/ppermute | solution.py:394
  168.1 24.0 %front.2 = (bf16[3,1024,384]{2,1,0:T(8,128)(2,1)}, bf16[1024,1280]{1,0:T(8,128)(2,1)}, bf16[4,384,1280]{2,1,0:T(8,128)(2,1)}, bf16[1024,384]{1,0:T(8,128)(2,1)},...) custom-call(bf16[256,1280]{1,0:T(8,128)(2,1)} %first_norm.2.refs_0_, ...), custom_call_target="tpu_custom_call" | custom-call | flops 352321536 | bytes 819780 | tf_op jit(solution)/shard_map/front/pallas_call | solution.py:731
  205.9 12.2 %collective-permute-done.24.c_ref = bf16[256,1280]{1,0:T(8,128)(2,1)} collective-permute-done((bf16[256,1280]{1,0:T(8,128)(2,1)}, bf16[256,1280]{1,0:T(8,128)(2,1)}, u32[]{:S(2)}, u32[]{:S(2)}) %collective-permute-start.24) | collective-permute-done | bytes 655392 | tf_op jit(solution)/shard_map/ppermute | solution.py:394
  225.1 8.4 %collective-permute-done.11.refs_1_ = bf16[256,768]{1,0:T(8,128)(2,1)} collective-permute-done((bf16[256,768]{1,0:T(8,128)(2,1)S(1)}, bf16[256,768]{1,0:T(8,128)(2,1)}, u32[]{:S(2)}, u32[]{:S(2)}) %collective-permute-start.11) | collective-permute-done | bytes 393248 | tf_op jit(solution)/shard_map/ppermute | solution.py:394
  234.0 22.4 %collective-permute-done.10.refs_7_ = bf16[96,768]{1,0:T(8,128)(2,1)S(1)} collective-permute-done((bf16[96,768]{1,0:T(8,128)(2,1)S(1)}, bf16[96,768]{1,0:T(8,128)(2,1)S(1)}, u32[]{:S(2)}, u32[]{:S(2)}) %collective-permute-start.10) | collective-permute-done | bytes 147488 | tf_op jit(solution)/shard_map/ppermute | solution.py:480
  267.1 14.5 %front.3 = (bf16[3,1024,192]{2,1,0:T(8,128)(2,1)}, bf16[1024,768]{1,0:T(8,128)(2,1)}, bf16[4,192,768]{2,1,0:T(8,128)(2,1)}, bf16[1024,192]{1,0:T(8,128)(2,1)}, b...) custom-call(bf16[256,768]{1,0:T(8,128)(2,1)} %first_norm.3.refs_0_, ...), custom_call_target="tpu_custom_call" | custom-call | flops 125829120 | bytes 344354 | tf_op jit(solution)/shard_map/front/pallas_call | solution.py:731
  281.6 10.2 %collective-permute-start.32 = (bf16[512,768]{1,0:T(8,128)(2,1)}, bf16[512,768]{1,0:T(8,128)(2,1)S(1)}, u32[]{:S(2)}, u32[]{:S(2)}) collective-permute-start(bf16[512,768]{1,0:T(8,128)(2,1)} %get-tuple-element.233), channel_id=1, source_target_pairs={{0,4},{4,0},{1,5},{5,1},{2,6},{6,2},{3,7},{7,3},{8,12},{12,8},{9,1... | collective-permute-start | bytes 2359304 | tf_op jit(solution)/shard_map/ppermute | solution.py:394
  300.7 20.2 %mlp_main.2 = (bf16[1024,1280]{1,0:T(8,128)(2,1)}, bf16[1024,1280]{1,0:T(8,128)(2,1)}, bf16[1024,1280]{1,0:T(8,128)(2,1)}, bf16[1024,1280]{1,0:T(8,128)(2,1)}, b...) custom-call(bf16[256,1280]{1,0:T(8,128)(2,1)} %get-tuple-element.237.refs_0_, ...), custom_call_target="tpu_custom_call" | custom-call | flops 629145600 | bytes 1475200 | tf_op jit(solution)/shard_map/mlp_main/pallas_call | solution.py:731
  331.7 10.1 %collective-permute-done.43 = bf16[192,768]{1,0:T(8,128)(2,1)S(1)} collective-permute-done((bf16[192,768]{1,0:T(8,128)(2,1)S(1)}, bf16[192,768]{1,0:T(8,128)(2,1)S(1)}, u32[]{:S(2)}, u32[]{:S(2)}) %collective-permute-start.43) | collective-permute-done | bytes 294944 | tf_op jit(solution)/shard_map/ppermute | solution.py:394
  345.2 17.8 %mlp_rest.2 = (bf16[512,1280]{1,0:T(8,128)(2,1)}, bf16[512,1280]{1,0:T(8,128)(2,1)}, bf16[2560,1280]{1,0:T(8,128)(2,1)}) custom-call(bf16[1024,1280]{1,0:T(8,128)(2,1)} %get-tuple-element.251.refs_0_, bf16[1024,1280]{1,0:T(8,128)(2,1)} %get-tuple-element.252.refs_1_, bf16[1024,1280]{1,0:T(8,128)(2,1)} %get-tuple-element.253.refs_2_, ...), custom_call_target="tpu_custom_call" | custom-call | flops 629145600 | bytes 2129920 | tf_op jit(solution)/shard_map/mlp_rest/pallas_call | solution.py:731
  368.5 9.5 %collective-permute-done.41 = bf16[192,1280]{1,0:T(8,128)(2,1)S(1)} collective-permute-done((bf16[192,1280]{1,0:T(8,128)(2,1)S(1)}, bf16[192,1280]{1,0:T(8,128)(2,1)S(1)}, u32[]{:S(2)}, u32[]{:S(2)}) %collective-permute-start.41) | collective-permute-done | bytes 491552 | tf_op jit(solution)/shard_map/ppermute | solution.py:394
  386.4 7.7 %collective-permute-done.48.refs_5_ = bf16[256,768]{1,0:T(8,128)(2,1)S(1)} collective-permute-done((bf16[256,768]{1,0:T(8,128)(2,1)S(1)}, bf16[256,768]{1,0:T(8,128)(2,1)S(1)}, u32[]{:S(2)}, u32[]{:S(2)}) %collective-permute-start.48) | collective-permute-done | bytes 393248 | tf_op jit(solution)/shard_map/ppermute | solution.py:394
  397.5 11.6 %mlp_main.3 = (bf16[1024,768]{1,0:T(8,128)(2,1)}, bf16[1024,768]{1,0:T(8,128)(2,1)}, bf16[1024,768]{1,0:T(8,128)(2,1)}, bf16[1024,768]{1,0:T(8,128)(2,1)}, bf16[...) custom-call(bf16[256,768]{1,0:T(8,128)(2,1)} %get-tuple-element.261.refs_0_, ...), custom_call_target="tpu_custom_call" | custom-call | flops 226492416 | bytes 688512 | tf_op jit(solution)/shard_map/mlp_main/pallas_call | solution.py:731
  414.9 32.6 %rear.2 = (bf16[1024,384]{1,0:T(8,128)(2,1)}, bf16[1024,384]{1,0:T(8,128)(2,1)}, bf16[1024,384]{1,0:T(8,128)(2,1)}, bf16[1024,1280]{1,0:T(8,128)(2,1)}, bf16[512...) custom-call(bf16[256,1280]{1,0:T(8,128)(2,1)} %get-tuple-element.269.refs_0_, bf16[256,1280]{1,0:T(8,128)(2,1)} %copy-done.31, ...), custom_call_target="tpu_custom_call" | custom-call | flops 503316480 | bytes 1215492 | tf_op jit(solution)/shard_map/rear/pallas_call | solution.py:731
  450.1 9.5 %collective-permute-done.55.c_ref = bf16[256,768]{1,0:T(8,128)(2,1)S(1)} collective-permute-done((bf16[256,768]{1,0:T(8,128)(2,1)}, bf16[256,768]{1,0:T(8,128)(2,1)S(1)}, u32[]{:S(2)}, u32[]{:S(2)}) %collective-permute-start.55) | collective-permute-done | bytes 393248 | tf_op jit(solution)/shard_map/ppermute | solution.py:394
  465.2 9.9 %head_weight_grads.2 = (bf16[2,192,1280]{2,1,0:T(8,128)(2,1)}, bf16[2,192,1280]{2,1,0:T(8,128)(2,1)}, bf16[2,192,1280]{2,1,0:T(8,128)(2,1)}, bf16[2,192,1280]{2,1,0:T(8,128)(2,1)}) custom-call(bf16[1024,384]{1,0:T(8,128)(2,1)} %get-tuple-element.285.refs_0_, bf16[1024,384]{1,0:T(8,128)(2,1)} %get-tuple-element.286.refs_1_, ...), custom_call_target="tpu_custom_call" | custom-call | flops 251658240 | bytes 1048576 | tf_op jit(solution)/shard_map/head_weight_grads/pallas_call | solution.py:731
  482.6 8.6 %mlp_rest.3 = (bf16[512,768]{1,0:T(8,128)(2,1)}, bf16[512,768]{1,0:T(8,128)(2,1)}, bf16[1536,768]{1,0:T(8,128)(2,1)}) custom-call(bf16[1024,768]{1,0:T(8,128)(2,1)} %get-tuple-element.294.refs_0_, bf16[1024,768]{1,0:T(8,128)(2,1)} %get-tuple-element.295.refs_1_, bf16[1024,768]{1,0:T(8,128)(2,1)} %get-tuple-element.296.refs_2_, ...), custom_call_target="tpu_custom_call" | custom-call | flops 226492416 | bytes 1081344 | tf_op jit(solution)/shard_map/mlp_rest/pallas_call | solution.py:731
  522.4 17.9 %rear.3 = (bf16[1024,192]{1,0:T(8,128)(2,1)}, bf16[1024,192]{1,0:T(8,128)(2,1)}, bf16[1024,192]{1,0:T(8,128)(2,1)}, bf16[1024,768]{1,0:T(8,128)(2,1)}, bf16[512,...) custom-call(bf16[256,768]{1,0:T(8,128)(2,1)} %get-tuple-element.305.refs_0_, bf16[256,768]{1,0:T(8,128)(2,1)} %collective-permute-done.59.refs_1_, ...), custom_call_target="tpu_custom_call" | custom-call | flops 201326592 | bytes 542210 | tf_op jit(solution)/shard_map/rear/pallas_call | solution.py:731
  602.5 9.9 %collective-permute-done.76 = bf16[2,96,768]{2,1,0:T(8,128)(2,1)} collective-permute-done((bf16[2,96,768]{2,1,0:T(8,128)(2,1)}, bf16[2,96,768]{2,1,0:T(8,128)(2,1)}, u32[]{:S(2)}, u32[]{:S(2)}) %collective-permute-start.76) | collective-permute-done | bytes 294944 | tf_op jit(solution)/shard_map/ppermute | solution.py:480
  661.4 11.9 %collective-permute-done.84 = f32[128,256]{1,0:T(8,128)S(1)} collective-permute-done((f32[128,256]{1,0:T(8,128)S(1)}, f32[128,256]{1,0:T(8,128)S(1)}, u32[]{:S(2)}, u32[]{:S(2)}) %collective-permute-start.84) | collective-permute-done | bytes 131104 | tf_op jit(solution)/shard_map/ppermute | solution.py:480
  (635 shorter events, 345.6 us)
Async XLA Ops:
  21.9 32.1 %collective-permute-start = (bf16[256,1280]{1,0:T(8,128)(2,1)}, bf16[256,1280]{1,0:T(8,128)(2,1)S(1)}, u32[]{:S(2)}, u32[]{:S(2)}) collective-permute-start(bf16[256,1280]{1,0:T(8,128)(2,1)} %bitcast.24), channel_id=1, source_target_pairs={{0,0},{1,8},{2,4},{3,12},{4,9},{5,1},{6,13},{7,5},{8,2},{9,10},{10... | collective-permute-start | bytes 1966088 | tf_op jit(solution)/shard_map/ppermute | solution.py:419
  45.2 32.1 %collective-permute-start.2 = (bf16[192,1280]{1,0:T(8,128)(2,1)}, bf16[192,1280]{1,0:T(8,128)(2,1)}, u32[]{:S(2)}, u32[]{:S(2)}) collective-permute-start(bf16[192,1280]{1,0:T(8,128)(2,1)} %copy.309), channel_id=1, source_target_pairs={{0,2},{1,3},{2,0},{3,1},{4,6},{5,7},{6,4},{7,5},{8,10},{9,11},{10,... | collective-permute-start | bytes 1474568 | tf_op jit(solution)/shard_map/ppermute | solution.py:480
  45.2 38.0 %collective-permute-start.5 = (bf16[192,1280]{1,0:T(8,128)(2,1)}, bf16[192,1280]{1,0:T(8,128)(2,1)}, u32[]{:S(2)}, u32[]{:S(2)}) collective-permute-start(bf16[192,1280]{1,0:T(8,128)(2,1)} %copy.309), channel_id=1, source_target_pairs={{0,1},{1,0},{2,3},{3,2},{4,5},{5,4},{6,7},{7,6},{8,9},{9,8},{10,11... | collective-permute-start | bytes 1474568 | tf_op jit(solution)/shard_map/ppermute | solution.py:480
  57.2 35.6 %collective-permute-start.4 = (bf16[256,1280]{1,0:T(8,128)(2,1)}, bf16[256,1280]{1,0:T(8,128)(2,1)}, u32[]{:S(2)}, u32[]{:S(2)}) collective-permute-start(bf16[256,1280]{1,0:T(8,128)(2,1)} %first_norm.2.refs_0_), channel_id=1, source_target_pairs={{0,8},{8,0},{1,9},{9,1},{2,10},{10,2},{3,11},{11,3},{4,12},{12,4},... | collective-permute-start | bytes 1966088 | tf_op jit(solution)/shard_map/ppermute | solution.py:394
  83.2 40.0 %all-to-all-start.2 = ((bf16[8,320,160]{1,2,0:T(8,128)(2,1)}), bf16[8,320,160]{1,2,0:T(8,128)(2,1)S(1)}, u32[]{:S(2)}, u32[]{:S(2)}) async-start(bf16[8,320,160]{1,2,0:T(8,128)(2,1)} %pad_maximum_fusion), calls=%async_computation.2 | async-start | bytes 1966080 | tf_op jit(solution)/shard_map/all_to_all | solution.py:463
  90.0 210.6 %all-gather.3.cloned.1.call-start = ((), (), s32[]{:S(2)}) async-start(), calls=%async_computation.8 | async-start | bytes 7372800 | tf_op jit(solution)/shard_map/all_gather | solution.py:1226
  90.7 32.6 %collective-permute-start.14 = (bf16[192,1280]{1,0:T(8,128)(2,1)}, bf16[192,1280]{1,0:T(8,128)(2,1)S(1)}, u32[]{:S(2)}, u32[]{:S(2)}) collective-permute-start(bf16[192,1280]{1,0:T(8,128)(2,1)} %copy.309), channel_id=1, source_target_pairs={{0,16},{16,0},{1,17},{17,1},{2,18},{18,2},{3,19},{19,3},{4,20},{20... | collective-permute-start | bytes 1474568 | tf_op jit(solution)/shard_map/ppermute | solution.py:394
  92.8 32.6 %collective-permute-start.15 = (bf16[192,1280]{1,0:T(8,128)(2,1)}, bf16[192,1280]{1,0:T(8,128)(2,1)}, u32[]{:S(2)}, u32[]{:S(2)}) collective-permute-start(bf16[192,1280]{1,0:T(8,128)(2,1)} %collective-permute-done.5), channel_id=1, source_target_pairs={{0,16},{16,0},{1,17},{17,1},{2,18},{18,2},{3,19},{19,3},{4,20},{20... | collective-permute-start | bytes 1474568 | tf_op jit(solution)/shard_map/ppermute | solution.py:394
  97.9 38.0 %collective-permute-start.16 = (bf16[192,1280]{1,0:T(8,128)(2,1)}, bf16[192,1280]{1,0:T(8,128)(2,1)}, u32[]{:S(2)}, u32[]{:S(2)}) collective-permute-start(bf16[192,1280]{1,0:T(8,128)(2,1)} %collective-permute-done.2), channel_id=1, source_target_pairs={{0,16},{16,0},{1,17},{17,1},{2,18},{18,2},{3,19},{19,3},{4,20},{20... | collective-permute-start | bytes 1474568 | tf_op jit(solution)/shard_map/ppermute | solution.py:394
  99.5 46.5 %collective-permute-start.17 = (bf16[192,1280]{1,0:T(8,128)(2,1)}, bf16[192,1280]{1,0:T(8,128)(2,1)}, u32[]{:S(2)}, u32[]{:S(2)}) collective-permute-start(bf16[192,1280]{1,0:T(8,128)(2,1)} %collective-permute-done.3), channel_id=1, source_target_pairs={{0,16},{16,0},{1,17},{17,1},{2,18},{18,2},{3,19},{19,3},{4,20},{20... | collective-permute-start | bytes 1474568 | tf_op jit(solution)/shard_map/ppermute | solution.py:394
  147.3 249.4 %all-gather.5.cloned.1.call-start = ((), (), s32[]{:S(2)}) async-start(), calls=%async_computation.9 | async-start | bytes 2654208 | tf_op jit(solution)/shard_map/all_gather | solution.py:1269
  204.0 54.0 %collective-permute-start.9 = (bf16[256,1280]{1,0:T(8,128)(2,1)}, bf16[256,1280]{1,0:T(8,128)(2,1)S(1)}, u32[]{:S(2)}, u32[]{:S(2)}) collective-permute-start(bf16[256,1280]{1,0:T(8,128)(2,1)} %bitcast.282), channel_id=1, source_target_pairs={{0,0},{1,8},{2,4},{3,12},{4,9},{5,1},{6,13},{7,5},{8,2},{9,10},{10... | collective-permute-start | bytes 1966088 | tf_op jit(solution)/shard_map/ppermute | solution.py:419
  221.4 39.2 %collective-permute-start.27 = (bf16[256,1280]{1,0:T(8,128)(2,1)}, bf16[256,1280]{1,0:T(8,128)(2,1)S(1)}, u32[]{:S(2)}, u32[]{:S(2)}) collective-permute-start(bf16[256,1280]{1,0:T(8,128)(2,1)} %get-tuple-element.237.refs_0_), channel_id=1, source_target_pairs={{0,8},{8,0},{1,9},{9,1},{2,10},{10,2},{3,11},{11,3},{4,12},{12,4},... | collective-permute-start | bytes 1966088 | tf_op jit(solution)/shard_map/ppermute | solution.py:394
  224.4 287.7 %reduce-scatter.3.cloned.1.call-start = ((), (), s32[]{:S(2)}) async-start(), calls=%async_computation.10 | async-start | bytes 7372800 | tf_op jit(solution)/shard_map/reduce_scatter | solution.py:1320
  225.0 33.6 %collective-permute-start.25 = (bf16[256,768]{1,0:T(8,128)(2,1)S(1)}, bf16[256,768]{1,0:T(8,128)(2,1)S(1)}, u32[]{:S(2)}, u32[]{:S(2)}) collective-permute-start(bf16[256,768]{1,0:T(8,128)(2,1)S(1)} %copy-done.20), channel_id=1, source_target_pairs={{0,4},{4,0},{1,5},{5,1},{2,6},{6,2},{3,7},{7,3},{8,12},{12,8},{9,1... | collective-permute-start | bytes 1179656 | tf_op jit(solution)/shard_map/ppermute | solution.py:394
  363.1 280.0 %reduce-scatter.5.cloned.1.call-start = ((), (), s32[]{:S(2)}) async-start(), calls=%async_computation.11 | async-start | bytes 2654208 | tf_op jit(solution)/shard_map/reduce_scatter | solution.py:1378
  502.0 38.3 %collective-permute-start.64 = (bf16[2,192,1280]{2,1,0:T(8,128)(2,1)}, bf16[2,192,1280]{2,1,0:T(8,128)(2,1)}, u32[]{:S(2)}, u32[]{:S(2)}) collective-permute-start(bf16[2,192,1280]{2,1,0:T(8,128)(2,1)} %pad_maximum_fusion.5), channel_id=1, source_target_pairs={{0,16},{16,0},{1,17},{17,1},{2,18},{18,2},{3,19},{19,3},{4,20},{20... | collective-permute-start | bytes 2949128 | tf_op jit(solution)/shard_map/ppermute | solution.py:394
  504.1 173.6 %collective-permute-start.58 = (bf16[256,1280]{1,0:T(8,128)(2,1)}, bf16[256,1280]{1,0:T(8,128)(2,1)}, u32[]{:S(2)}, u32[]{:S(2)}) collective-permute-start(bf16[256,1280]{1,0:T(8,128)(2,1)} %get-tuple-element.301), channel_id=1, source_target_pairs={{0,0},{8,1},{4,2},{12,3},{9,4},{1,5},{13,6},{5,7},{2,8},{10,9},{6,... | collective-permute-start | bytes 1966088 | tf_op jit(solution)/shard_map/ppermute | solution.py:423
  512.9 52.7 %collective-permute-start.68 = (bf16[2,192,1280]{2,1,0:T(8,128)(2,1)}, bf16[2,192,1280]{2,1,0:T(8,128)(2,1)}, u32[]{:S(2)}, u32[]{:S(2)}) collective-permute-start(bf16[2,192,1280]{2,1,0:T(8,128)(2,1)} %pad_maximum_fusion.6), channel_id=1, source_target_pairs={{0,16},{16,0},{1,17},{17,1},{2,18},{18,2},{3,19},{19,3},{4,20},{20... | collective-permute-start | bytes 2949128 | tf_op jit(solution)/shard_map/ppermute | solution.py:394
  517.9 72.1 %all-to-all-start.3 = ((bf16[8,320,160]{1,2,0:T(8,128)(2,1)}), bf16[8,320,160]{1,2,0:T(8,128)(2,1)}, u32[]{:S(2)}, u32[]{:S(2)}) async-start(bf16[8,320,160]{1,2,0:T(8,128)(2,1)} %bitcast.69), calls=%async_computation.4 | async-start | bytes 1966080 | tf_op jit(solution)/shard_map/all_to_all | solution.py:463
  572.5 49.4 %collective-permute-start.79 = (bf16[192,1280]{1,0:T(8,128)(2,1)}, bf16[192,1280]{1,0:T(8,128)(2,1)}, u32[]{:S(2)}, u32[]{:S(2)}) collective-permute-start(bf16[192,1280]{1,0:T(8,128)(2,1)} %fusion.4), channel_id=1, source_target_pairs={{0,2},{1,3},{2,0},{3,1},{4,6},{5,7},{6,4},{7,5},{8,10},{9,11},{10,... | collective-permute-start | bytes 1474568 | tf_op jit(solution)/shard_map/ppermute | solution.py:480
  573.1 46.9 %collective-permute-start.70 = (bf16[256,1280]{1,0:T(8,128)(2,1)}, bf16[256,1280]{1,0:T(8,128)(2,1)}, u32[]{:S(2)}, u32[]{:S(2)}) collective-permute-start(bf16[256,1280]{1,0:T(8,128)(2,1)} %add_convert_fusion.2), channel_id=1, source_target_pairs={{0,8},{8,0},{1,9},{9,1},{2,10},{10,2},{3,11},{11,3},{4,12},{12,4},... | collective-permute-start | bytes 1966088 | tf_op jit(solution)/shard_map/ppermute | solution.py:394
  612.5 65.3 %collective-permute-start.69 = (bf16[256,768]{1,0:T(8,128)(2,1)}, bf16[256,768]{1,0:T(8,128)(2,1)}, u32[]{:S(2)}, u32[]{:S(2)}) collective-permute-start(bf16[256,768]{1,0:T(8,128)(2,1)} %get-tuple-element.332), channel_id=1, source_target_pairs={{0,0},{8,1},{4,2},{12,3},{9,4},{1,5},{13,6},{5,7},{2,8},{10,9},{6,... | collective-permute-start | bytes 1179656 | tf_op jit(solution)/shard_map/ppermute | solution.py:423
  636.5 41.3 %collective-permute-start.74 = (bf16[256,1280]{1,0:T(8,128)(2,1)}, bf16[256,1280]{1,0:T(8,128)(2,1)}, u32[]{:S(2)}, u32[]{:S(2)}) collective-permute-start(bf16[256,1280]{1,0:T(8,128)(2,1)} %add_convert_fusion.1), channel_id=1, source_target_pairs={{0,0},{8,1},{4,2},{12,3},{9,4},{1,5},{13,6},{5,7},{2,8},{10,9},{6,... | collective-permute-start | bytes 1966088 | tf_op jit(solution)/shard_map/ppermute | solution.py:423
  (168 other events, 2414.4 us)
Sparse Core Ops, SparseCore 0:
  147.4 126.2 all-gather.2
  276.4 51.0 all-gather.4
  363.2 123.4 reduce-scatter.2
  502.1 106.4 reduce-scatter.4

commit v4 on v3

--- a/solution.py
+++ b/solution.py
@@ -493,7 +493,7 @@
         in_specs=[spec(a.shape) for a in args],
         out_specs=[spec(shape) for shape, _ in outs],
         out_shape=[jax.ShapeDtypeStruct(shape, dtype) for shape, dtype in outs],
-        cost_estimate=pl.CostEstimate(flops=args[0].size * 20, transcendentals=0, bytes_accessed=2 * size),
+        cost_estimate=pl.CostEstimate(flops=args[0].size // 16, transcendentals=0, bytes_accessed=size // 128),
         name=name,
     )(*args)
 
@@ -735,7 +735,7 @@
         out_shape=[jax.ShapeDtypeStruct(shape, dtype) for shape, dtype, _ in outs],
         scratch_shapes=scratches,
         compiler_params=pltpu.CompilerParams(vmem_limit_bytes=LIMIT),
-        cost_estimate=pl.CostEstimate(flops=flops // 16, transcendentals=0, bytes_accessed=size // 8),
+        cost_estimate=pl.CostEstimate(flops=flops // 256, transcendentals=0, bytes_accessed=size // 128),
         name=name,
     )(*args)
 

time: 706 us -> 705 us (level)
  transfers between devices with their start and end apart: 95 -> 95, of which waited for: 38 -> 36; matrix products, arithmetic and copies ran while one was open for 15% -> 15% of each run, Pallas kernels for 27% -> 27%
where the time goes in v4:
time: 705 us; the launch traced here: 694 us
  waiting for transfers between devices  213 us (30%)
  Pallas kernels  188 us (27%)
  starting transfers between devices  143 us (20%)
  local copies, waits for them, and re-layouts  77.6 us (11%)
  other arithmetic  55.3 us (8%)
  between operations  16.7 us (2%)
    pallas_call x10, Pallas kernels, matmul_call(): pl.pallas_call(kernel, in_specs=specs, out_specs=[spec for _, _, spec in...  162 us
    ppermute x60, waiting for transfers between devices, swap(): return lax.ppermute(values, axis, ((0, 1), (1, 0)))  118 us
    ppermute x15, waiting for transfers between devices, plane_swap(): return lax.ppermute(values, 'z', tuple(((i, i ^ bit) for i in range(4))))  74 us
    ppermute x60, starting transfers between devices, swap(): return lax.ppermute(values, axis, ((0, 1), (1, 0)))  59.9 us
    all_to_all x6, starting transfers between devices, to_plane(): return lax.all_to_all(blocks, PLANE, 0, 0)  30.9 us
    unnamed x221, local copies, waits for them, and re-layouts  26.6 us
    pallas_call x8, Pallas kernels, row_call(): pl.pallas_call(kernel, grid=(1,), in_specs=[spec(a.shape) for a in args],...  26 us
    convert_element_type x14, other arithmetic, low(): return values.astype(jnp.bfloat16)  25.6 us
  transfers between devices with their start and end apart: 95, of which 36 were waited for; matrix products, arithmetic and copies ran while one was open for 15% of the time, Pallas kernels for 27%

profile of v4, /device:TPU:0, one launch (start us, length us, event | category | flops | bytes accessed | tf_op | source)
XLA Modules:
  0.0 694.1 jit_solution(2464023055550869799)
XLA Ops:
  25.1 19.0 %all-to-all-done = bf16[8,208,160]{1,2,0:T(8,128)(2,1)S(1)} async-done(((bf16[8,208,160]{1,2,0:T(8,128)(2,1)}), bf16[8,208,160]{1,2,0:T(8,128)(2,1)S(1)}, u32[]{:S(2)}, u32[]{:S(2)}) %all-to-all-start) | async-done | bytes 532512 | tf_op jit(solution)/shard_map/all_to_all | solution.py:463
  60.6 16.7 %collective-permute-done.2 = bf16[192,1280]{1,0:T(8,128)(2,1)} collective-permute-done((bf16[192,1280]{1,0:T(8,128)(2,1)}, bf16[192,1280]{1,0:T(8,128)(2,1)}, u32[]{:S(2)}, u32[]{:S(2)}) %collective-permute-start.2) | collective-permute-done | bytes 491552 | tf_op jit(solution)/shard_map/ppermute | solution.py:480
  125.4 10.5 %collective-permute-done.16 = bf16[192,1280]{1,0:T(8,128)(2,1)} collective-permute-done((bf16[192,1280]{1,0:T(8,128)(2,1)}, bf16[192,1280]{1,0:T(8,128)(2,1)}, u32[]{:S(2)}, u32[]{:S(2)}) %collective-permute-start.16) | collective-permute-done | bytes 491552 | tf_op jit(solution)/shard_map/ppermute | solution.py:394
  135.9 10.1 %collective-permute-done.17 = bf16[192,1280]{1,0:T(8,128)(2,1)} collective-permute-done((bf16[192,1280]{1,0:T(8,128)(2,1)}, bf16[192,1280]{1,0:T(8,128)(2,1)}, u32[]{:S(2)}, u32[]{:S(2)}) %collective-permute-start.17) | collective-permute-done | bytes 491552 | tf_op jit(solution)/shard_map/ppermute | solution.py:394
  168.1 24.0 %front.2 = (bf16[3,1024,384]{2,1,0:T(8,128)(2,1)}, bf16[1024,1280]{1,0:T(8,128)(2,1)}, bf16[4,384,1280]{2,1,0:T(8,128)(2,1)}, bf16[1024,384]{1,0:T(8,128)(2,1)},...) custom-call(bf16[256,1280]{1,0:T(8,128)(2,1)} %first_norm.2.refs_0_, ...), custom_call_target="tpu_custom_call" | custom-call | flops 22020096 | bytes 51236 | tf_op jit(solution)/shard_map/front/pallas_call | solution.py:731
  206.3 11.9 %collective-permute-done.24.c_ref = bf16[256,1280]{1,0:T(8,128)(2,1)} collective-permute-done((bf16[256,1280]{1,0:T(8,128)(2,1)}, bf16[256,1280]{1,0:T(8,128)(2,1)}, u32[]{:S(2)}, u32[]{:S(2)}) %collective-permute-start.24) | collective-permute-done | bytes 655392 | tf_op jit(solution)/shard_map/ppermute | solution.py:394
  224.7 8.8 %collective-permute-done.11.refs_1_ = bf16[256,768]{1,0:T(8,128)(2,1)} collective-permute-done((bf16[256,768]{1,0:T(8,128)(2,1)S(1)}, bf16[256,768]{1,0:T(8,128)(2,1)}, u32[]{:S(2)}, u32[]{:S(2)}) %collective-permute-start.11) | collective-permute-done | bytes 393248 | tf_op jit(solution)/shard_map/ppermute | solution.py:394
  234.1 22.4 %collective-permute-done.10.refs_7_ = bf16[96,768]{1,0:T(8,128)(2,1)S(1)} collective-permute-done((bf16[96,768]{1,0:T(8,128)(2,1)S(1)}, bf16[96,768]{1,0:T(8,128)(2,1)S(1)}, u32[]{:S(2)}, u32[]{:S(2)}) %collective-permute-start.10) | collective-permute-done | bytes 147488 | tf_op jit(solution)/shard_map/ppermute | solution.py:480
  267.1 14.5 %front.3 = (bf16[3,1024,192]{2,1,0:T(8,128)(2,1)}, bf16[1024,768]{1,0:T(8,128)(2,1)}, bf16[4,192,768]{2,1,0:T(8,128)(2,1)}, bf16[1024,192]{1,0:T(8,128)(2,1)}, b...) custom-call(bf16[256,768]{1,0:T(8,128)(2,1)} %first_norm.3.refs_0_, ...), custom_call_target="tpu_custom_call" | custom-call | flops 7864320 | bytes 21522 | tf_op jit(solution)/shard_map/front/pallas_call | solution.py:731
  281.6 10.0 %collective-permute-start.32 = (bf16[512,768]{1,0:T(8,128)(2,1)}, bf16[512,768]{1,0:T(8,128)(2,1)S(1)}, u32[]{:S(2)}, u32[]{:S(2)}) collective-permute-start(bf16[512,768]{1,0:T(8,128)(2,1)} %get-tuple-element.233), channel_id=1, source_target_pairs={{0,4},{4,0},{1,5},{5,1},{2,6},{6,2},{3,7},{7,3},{8,12},{12,8},{9,1... | collective-permute-start | bytes 2359304 | tf_op jit(solution)/shard_map/ppermute | solution.py:394
  300.6 20.2 %mlp_main.2 = (bf16[1024,1280]{1,0:T(8,128)(2,1)}, bf16[1024,1280]{1,0:T(8,128)(2,1)}, bf16[1024,1280]{1,0:T(8,128)(2,1)}, bf16[1024,1280]{1,0:T(8,128)(2,1)}, b...) custom-call(bf16[256,1280]{1,0:T(8,128)(2,1)} %get-tuple-element.237.refs_0_, ...), custom_call_target="tpu_custom_call" | custom-call | flops 39321600 | bytes 92200 | tf_op jit(solution)/shard_map/mlp_main/pallas_call | solution.py:731
  331.8 9.9 %collective-permute-done.43 = bf16[192,768]{1,0:T(8,128)(2,1)S(1)} collective-permute-done((bf16[192,768]{1,0:T(8,128)(2,1)S(1)}, bf16[192,768]{1,0:T(8,128)(2,1)S(1)}, u32[]{:S(2)}, u32[]{:S(2)}) %collective-permute-start.43) | collective-permute-done | bytes 294944 | tf_op jit(solution)/shard_map/ppermute | solution.py:394
  345.2 17.8 %mlp_rest.2 = (bf16[512,1280]{1,0:T(8,128)(2,1)}, bf16[512,1280]{1,0:T(8,128)(2,1)}, bf16[2560,1280]{1,0:T(8,128)(2,1)}) custom-call(bf16[1024,1280]{1,0:T(8,128)(2,1)} %get-tuple-element.251.refs_0_, bf16[1024,1280]{1,0:T(8,128)(2,1)} %get-tuple-element.252.refs_1_, bf16[1024,1280]{1,0:T(8,128)(2,1)} %get-tuple-element.253.refs_2_, ...), custom_call_target="tpu_custom_call" | custom-call | flops 39321600 | bytes 133120 | tf_op jit(solution)/shard_map/mlp_rest/pallas_call | solution.py:731
  368.4 9.5 %collective-permute-done.41 = bf16[192,1280]{1,0:T(8,128)(2,1)S(1)} collective-permute-done((bf16[192,1280]{1,0:T(8,128)(2,1)S(1)}, bf16[192,1280]{1,0:T(8,128)(2,1)S(1)}, u32[]{:S(2)}, u32[]{:S(2)}) %collective-permute-start.41) | collective-permute-done | bytes 491552 | tf_op jit(solution)/shard_map/ppermute | solution.py:394
  386.3 7.7 %collective-permute-done.48.refs_5_ = bf16[256,768]{1,0:T(8,128)(2,1)S(1)} collective-permute-done((bf16[256,768]{1,0:T(8,128)(2,1)S(1)}, bf16[256,768]{1,0:T(8,128)(2,1)S(1)}, u32[]{:S(2)}, u32[]{:S(2)}) %collective-permute-start.48) | collective-permute-done | bytes 393248 | tf_op jit(solution)/shard_map/ppermute | solution.py:394
  397.4 11.6 %mlp_main.3 = (bf16[1024,768]{1,0:T(8,128)(2,1)}, bf16[1024,768]{1,0:T(8,128)(2,1)}, bf16[1024,768]{1,0:T(8,128)(2,1)}, bf16[1024,768]{1,0:T(8,128)(2,1)}, bf16[...) custom-call(bf16[256,768]{1,0:T(8,128)(2,1)} %get-tuple-element.261.refs_0_, ...), custom_call_target="tpu_custom_call" | custom-call | flops 14155776 | bytes 43032 | tf_op jit(solution)/shard_map/mlp_main/pallas_call | solution.py:731
  414.7 32.6 %rear.2 = (bf16[1024,384]{1,0:T(8,128)(2,1)}, bf16[1024,384]{1,0:T(8,128)(2,1)}, bf16[1024,384]{1,0:T(8,128)(2,1)}, bf16[1024,1280]{1,0:T(8,128)(2,1)}, bf16[512...) custom-call(bf16[256,1280]{1,0:T(8,128)(2,1)} %get-tuple-element.269.refs_0_, bf16[256,1280]{1,0:T(8,128)(2,1)} %copy-done.31, ...), custom_call_target="tpu_custom_call" | custom-call | flops 31457280 | bytes 75968 | tf_op jit(solution)/shard_map/rear/pallas_call | solution.py:731
  450.0 9.4 %collective-permute-done.55.c_ref = bf16[256,768]{1,0:T(8,128)(2,1)S(1)} collective-permute-done((bf16[256,768]{1,0:T(8,128)(2,1)}, bf16[256,768]{1,0:T(8,128)(2,1)S(1)}, u32[]{:S(2)}, u32[]{:S(2)}) %collective-permute-start.55) | collective-permute-done | bytes 393248 | tf_op jit(solution)/shard_map/ppermute | solution.py:394
  465.0 9.9 %head_weight_grads.2 = (bf16[2,192,1280]{2,1,0:T(8,128)(2,1)}, bf16[2,192,1280]{2,1,0:T(8,128)(2,1)}, bf16[2,192,1280]{2,1,0:T(8,128)(2,1)}, bf16[2,192,1280]{2,1,0:T(8,128)(2,1)}) custom-call(bf16[1024,384]{1,0:T(8,128)(2,1)} %get-tuple-element.285.refs_0_, bf16[1024,384]{1,0:T(8,128)(2,1)} %get-tuple-element.286.refs_1_, ...), custom_call_target="tpu_custom_call" | custom-call | flops 15728640 | bytes 65536 | tf_op jit(solution)/shard_map/head_weight_grads/pallas_call | solution.py:731
  482.5 8.6 %mlp_rest.3 = (bf16[512,768]{1,0:T(8,128)(2,1)}, bf16[512,768]{1,0:T(8,128)(2,1)}, bf16[1536,768]{1,0:T(8,128)(2,1)}) custom-call(bf16[1024,768]{1,0:T(8,128)(2,1)} %get-tuple-element.294.refs_0_, bf16[1024,768]{1,0:T(8,128)(2,1)} %get-tuple-element.295.refs_1_, bf16[1024,768]{1,0:T(8,128)(2,1)} %get-tuple-element.296.refs_2_, ...), custom_call_target="tpu_custom_call" | custom-call | flops 14155776 | bytes 67584 | tf_op jit(solution)/shard_map/mlp_rest/pallas_call | solution.py:731
  522.3 17.9 %rear.3 = (bf16[1024,192]{1,0:T(8,128)(2,1)}, bf16[1024,192]{1,0:T(8,128)(2,1)}, bf16[1024,192]{1,0:T(8,128)(2,1)}, bf16[1024,768]{1,0:T(8,128)(2,1)}, bf16[512,...) custom-call(bf16[256,768]{1,0:T(8,128)(2,1)} %get-tuple-element.305.refs_0_, bf16[256,768]{1,0:T(8,128)(2,1)} %collective-permute-done.59.refs_1_, ...), custom_call_target="tpu_custom_call" | custom-call | flops 12582912 | bytes 33888 | tf_op jit(solution)/shard_map/rear/pallas_call | solution.py:731
  578.2 7.8 %collective-permute-done.73 = bf16[4,96,768]{2,1,0:T(8,128)(2,1)S(1)} collective-permute-done((bf16[4,96,768]{2,1,0:T(8,128)(2,1)}, bf16[4,96,768]{2,1,0:T(8,128)(2,1)S(1)}, u32[]{:S(2)}, u32[]{:S(2)}) %collective-permute-start.73) | collective-permute-done | bytes 589856 | tf_op jit(solution)/shard_map/ppermute | solution.py:394
  602.2 9.1 %collective-permute-done.76 = bf16[2,96,768]{2,1,0:T(8,128)(2,1)} collective-permute-done((bf16[2,96,768]{2,1,0:T(8,128)(2,1)}, bf16[2,96,768]{2,1,0:T(8,128)(2,1)}, u32[]{:S(2)}, u32[]{:S(2)}) %collective-permute-start.76) | collective-permute-done | bytes 294944 | tf_op jit(solution)/shard_map/ppermute | solution.py:480
  661.2 11.5 %collective-permute-done.84 = f32[128,256]{1,0:T(8,128)S(1)} collective-permute-done((f32[128,256]{1,0:T(8,128)S(1)}, f32[128,256]{1,0:T(8,128)S(1)}, u32[]{:S(2)}, u32[]{:S(2)}) %collective-permute-start.84) | collective-permute-done | bytes 131104 | tf_op jit(solution)/shard_map/ppermute | solution.py:480
  (635 shorter events, 346.1 us)
Async XLA Ops:
  21.9 32.1 %collective-permute-start = (bf16[256,1280]{1,0:T(8,128)(2,1)}, bf16[256,1280]{1,0:T(8,128)(2,1)S(1)}, u32[]{:S(2)}, u32[]{:S(2)}) collective-permute-start(bf16[256,1280]{1,0:T(8,128)(2,1)} %bitcast.24), channel_id=1, source_target_pairs={{0,0},{1,8},{2,4},{3,12},{4,9},{5,1},{6,13},{7,5},{8,2},{9,10},{10... | collective-permute-start | bytes 1966088 | tf_op jit(solution)/shard_map/ppermute | solution.py:419
  45.2 32.1 %collective-permute-start.2 = (bf16[192,1280]{1,0:T(8,128)(2,1)}, bf16[192,1280]{1,0:T(8,128)(2,1)}, u32[]{:S(2)}, u32[]{:S(2)}) collective-permute-start(bf16[192,1280]{1,0:T(8,128)(2,1)} %copy.309), channel_id=1, source_target_pairs={{0,2},{1,3},{2,0},{3,1},{4,6},{5,7},{6,4},{7,5},{8,10},{9,11},{10,... | collective-permute-start | bytes 1474568 | tf_op jit(solution)/shard_map/ppermute | solution.py:480
  45.2 38.0 %collective-permute-start.5 = (bf16[192,1280]{1,0:T(8,128)(2,1)}, bf16[192,1280]{1,0:T(8,128)(2,1)}, u32[]{:S(2)}, u32[]{:S(2)}) collective-permute-start(bf16[192,1280]{1,0:T(8,128)(2,1)} %copy.309), channel_id=1, source_target_pairs={{0,1},{1,0},{2,3},{3,2},{4,5},{5,4},{6,7},{7,6},{8,9},{9,8},{10,11... | collective-permute-start | bytes 1474568 | tf_op jit(solution)/shard_map/ppermute | solution.py:480
  57.2 35.6 %collective-permute-start.4 = (bf16[256,1280]{1,0:T(8,128)(2,1)}, bf16[256,1280]{1,0:T(8,128)(2,1)}, u32[]{:S(2)}, u32[]{:S(2)}) collective-permute-start(bf16[256,1280]{1,0:T(8,128)(2,1)} %first_norm.2.refs_0_), channel_id=1, source_target_pairs={{0,8},{8,0},{1,9},{9,1},{2,10},{10,2},{3,11},{11,3},{4,12},{12,4},... | collective-permute-start | bytes 1966088 | tf_op jit(solution)/shard_map/ppermute | solution.py:394
  83.2 40.0 %all-to-all-start.2 = ((bf16[8,320,160]{1,2,0:T(8,128)(2,1)}), bf16[8,320,160]{1,2,0:T(8,128)(2,1)S(1)}, u32[]{:S(2)}, u32[]{:S(2)}) async-start(bf16[8,320,160]{1,2,0:T(8,128)(2,1)} %pad_maximum_fusion), calls=%async_computation.2 | async-start | bytes 1966080 | tf_op jit(solution)/shard_map/all_to_all | solution.py:463
  90.0 210.5 %all-gather.3.cloned.1.call-start = ((), (), s32[]{:S(2)}) async-start(), calls=%async_computation.8 | async-start | bytes 7372800 | tf_op jit(solution)/shard_map/all_gather | solution.py:1226
  90.7 32.6 %collective-permute-start.14 = (bf16[192,1280]{1,0:T(8,128)(2,1)}, bf16[192,1280]{1,0:T(8,128)(2,1)S(1)}, u32[]{:S(2)}, u32[]{:S(2)}) collective-permute-start(bf16[192,1280]{1,0:T(8,128)(2,1)} %copy.309), channel_id=1, source_target_pairs={{0,16},{16,0},{1,17},{17,1},{2,18},{18,2},{3,19},{19,3},{4,20},{20... | collective-permute-start | bytes 1474568 | tf_op jit(solution)/shard_map/ppermute | solution.py:394
  92.8 32.6 %collective-permute-start.15 = (bf16[192,1280]{1,0:T(8,128)(2,1)}, bf16[192,1280]{1,0:T(8,128)(2,1)}, u32[]{:S(2)}, u32[]{:S(2)}) collective-permute-start(bf16[192,1280]{1,0:T(8,128)(2,1)} %collective-permute-done.5), channel_id=1, source_target_pairs={{0,16},{16,0},{1,17},{17,1},{2,18},{18,2},{3,19},{19,3},{4,20},{20... | collective-permute-start | bytes 1474568 | tf_op jit(solution)/shard_map/ppermute | solution.py:394
  97.9 38.0 %collective-permute-start.16 = (bf16[192,1280]{1,0:T(8,128)(2,1)}, bf16[192,1280]{1,0:T(8,128)(2,1)}, u32[]{:S(2)}, u32[]{:S(2)}) collective-permute-start(bf16[192,1280]{1,0:T(8,128)(2,1)} %collective-permute-done.2), channel_id=1, source_target_pairs={{0,16},{16,0},{1,17},{17,1},{2,18},{18,2},{3,19},{19,3},{4,20},{20... | collective-permute-start | bytes 1474568 | tf_op jit(solution)/shard_map/ppermute | solution.py:394
  99.5 46.5 %collective-permute-start.17 = (bf16[192,1280]{1,0:T(8,128)(2,1)}, bf16[192,1280]{1,0:T(8,128)(2,1)}, u32[]{:S(2)}, u32[]{:S(2)}) collective-permute-start(bf16[192,1280]{1,0:T(8,128)(2,1)} %collective-permute-done.3), channel_id=1, source_target_pairs={{0,16},{16,0},{1,17},{17,1},{2,18},{18,2},{3,19},{19,3},{4,20},{20... | collective-permute-start | bytes 1474568 | tf_op jit(solution)/shard_map/ppermute | solution.py:394
  147.3 249.4 %all-gather.5.cloned.1.call-start = ((), (), s32[]{:S(2)}) async-start(), calls=%async_computation.9 | async-start | bytes 2654208 | tf_op jit(solution)/shard_map/all_gather | solution.py:1269
  204.0 54.0 %collective-permute-start.9 = (bf16[256,1280]{1,0:T(8,128)(2,1)}, bf16[256,1280]{1,0:T(8,128)(2,1)S(1)}, u32[]{:S(2)}, u32[]{:S(2)}) collective-permute-start(bf16[256,1280]{1,0:T(8,128)(2,1)} %bitcast.282), channel_id=1, source_target_pairs={{0,0},{1,8},{2,4},{3,12},{4,9},{5,1},{6,13},{7,5},{8,2},{9,10},{10... | collective-permute-start | bytes 1966088 | tf_op jit(solution)/shard_map/ppermute | solution.py:419
  205.8 307.1 %reduce-scatter.3.cloned.1.call-start = ((), (), s32[]{:S(2)}) async-start(), calls=%async_computation.10 | async-start | bytes 7372800 | tf_op jit(solution)/shard_map/reduce_scatter | solution.py:1320
  221.5 39.1 %collective-permute-start.27 = (bf16[256,1280]{1,0:T(8,128)(2,1)}, bf16[256,1280]{1,0:T(8,128)(2,1)S(1)}, u32[]{:S(2)}, u32[]{:S(2)}) collective-permute-start(bf16[256,1280]{1,0:T(8,128)(2,1)} %get-tuple-element.237.refs_0_), channel_id=1, source_target_pairs={{0,8},{8,0},{1,9},{9,1},{2,10},{10,2},{3,11},{11,3},{4,12},{12,4},... | collective-permute-start | bytes 1966088 | tf_op jit(solution)/shard_map/ppermute | solution.py:394
  224.6 34.0 %collective-permute-start.25 = (bf16[256,768]{1,0:T(8,128)(2,1)S(1)}, bf16[256,768]{1,0:T(8,128)(2,1)S(1)}, u32[]{:S(2)}, u32[]{:S(2)}) collective-permute-start(bf16[256,768]{1,0:T(8,128)(2,1)S(1)} %copy-done.20), channel_id=1, source_target_pairs={{0,4},{4,0},{1,5},{5,1},{2,6},{6,2},{3,7},{7,3},{8,12},{12,8},{9,1... | collective-permute-start | bytes 1179656 | tf_op jit(solution)/shard_map/ppermute | solution.py:394
  363.0 279.5 %reduce-scatter.5.cloned.1.call-start = ((), (), s32[]{:S(2)}) async-start(), calls=%async_computation.11 | async-start | bytes 2654208 | tf_op jit(solution)/shard_map/reduce_scatter | solution.py:1378
  501.9 38.3 %collective-permute-start.64 = (bf16[2,192,1280]{2,1,0:T(8,128)(2,1)}, bf16[2,192,1280]{2,1,0:T(8,128)(2,1)}, u32[]{:S(2)}, u32[]{:S(2)}) collective-permute-start(bf16[2,192,1280]{2,1,0:T(8,128)(2,1)} %pad_maximum_fusion.5), channel_id=1, source_target_pairs={{0,16},{16,0},{1,17},{17,1},{2,18},{18,2},{3,19},{19,3},{4,20},{20... | collective-permute-start | bytes 2949128 | tf_op jit(solution)/shard_map/ppermute | solution.py:394
  504.9 172.2 %collective-permute-start.58 = (bf16[256,1280]{1,0:T(8,128)(2,1)}, bf16[256,1280]{1,0:T(8,128)(2,1)}, u32[]{:S(2)}, u32[]{:S(2)}) collective-permute-start(bf16[256,1280]{1,0:T(8,128)(2,1)} %get-tuple-element.301), channel_id=1, source_target_pairs={{0,0},{8,1},{4,2},{12,3},{9,4},{1,5},{13,6},{5,7},{2,8},{10,9},{6,... | collective-permute-start | bytes 1966088 | tf_op jit(solution)/shard_map/ppermute | solution.py:423
  512.9 52.8 %collective-permute-start.68 = (bf16[2,192,1280]{2,1,0:T(8,128)(2,1)}, bf16[2,192,1280]{2,1,0:T(8,128)(2,1)}, u32[]{:S(2)}, u32[]{:S(2)}) collective-permute-start(bf16[2,192,1280]{2,1,0:T(8,128)(2,1)} %pad_maximum_fusion.6), channel_id=1, source_target_pairs={{0,16},{16,0},{1,17},{17,1},{2,18},{18,2},{3,19},{19,3},{4,20},{20... | collective-permute-start | bytes 2949128 | tf_op jit(solution)/shard_map/ppermute | solution.py:394
  517.8 71.9 %all-to-all-start.3 = ((bf16[8,320,160]{1,2,0:T(8,128)(2,1)}), bf16[8,320,160]{1,2,0:T(8,128)(2,1)}, u32[]{:S(2)}, u32[]{:S(2)}) async-start(bf16[8,320,160]{1,2,0:T(8,128)(2,1)} %bitcast.69), calls=%async_computation.4 | async-start | bytes 1966080 | tf_op jit(solution)/shard_map/all_to_all | solution.py:463
  571.5 49.2 %collective-permute-start.79 = (bf16[192,1280]{1,0:T(8,128)(2,1)}, bf16[192,1280]{1,0:T(8,128)(2,1)}, u32[]{:S(2)}, u32[]{:S(2)}) collective-permute-start(bf16[192,1280]{1,0:T(8,128)(2,1)} %fusion.4), channel_id=1, source_target_pairs={{0,2},{1,3},{2,0},{3,1},{4,6},{5,7},{6,4},{7,5},{8,10},{9,11},{10,... | collective-permute-start | bytes 1474568 | tf_op jit(solution)/shard_map/ppermute | solution.py:480
  572.1 46.7 %collective-permute-start.70 = (bf16[256,1280]{1,0:T(8,128)(2,1)}, bf16[256,1280]{1,0:T(8,128)(2,1)}, u32[]{:S(2)}, u32[]{:S(2)}) collective-permute-start(bf16[256,1280]{1,0:T(8,128)(2,1)} %add_convert_fusion.2), channel_id=1, source_target_pairs={{0,8},{8,0},{1,9},{9,1},{2,10},{10,2},{3,11},{11,3},{4,12},{12,4},... | collective-permute-start | bytes 1966088 | tf_op jit(solution)/shard_map/ppermute | solution.py:394
  611.2 65.9 %collective-permute-start.69 = (bf16[256,768]{1,0:T(8,128)(2,1)}, bf16[256,768]{1,0:T(8,128)(2,1)}, u32[]{:S(2)}, u32[]{:S(2)}) collective-permute-start(bf16[256,768]{1,0:T(8,128)(2,1)} %get-tuple-element.332), channel_id=1, source_target_pairs={{0,0},{8,1},{4,2},{12,3},{9,4},{1,5},{13,6},{5,7},{2,8},{10,9},{6,... | collective-permute-start | bytes 1179656 | tf_op jit(solution)/shard_map/ppermute | solution.py:423
  635.9 41.3 %collective-permute-start.74 = (bf16[256,1280]{1,0:T(8,128)(2,1)}, bf16[256,1280]{1,0:T(8,128)(2,1)}, u32[]{:S(2)}, u32[]{:S(2)}) collective-permute-start(bf16[256,1280]{1,0:T(8,128)(2,1)} %add_convert_fusion.1), channel_id=1, source_target_pairs={{0,0},{8,1},{4,2},{12,3},{9,4},{1,5},{13,6},{5,7},{2,8},{10,9},{6,... | collective-permute-start | bytes 1966088 | tf_op jit(solution)/shard_map/ppermute | solution.py:423
  (168 other events, 2414.4 us)
Sparse Core Ops, SparseCore 0:
  147.4 126.2 all-gather.2
  276.4 51.0 all-gather.4
  363.1 123.2 reduce-scatter.2
  502.9 104.4 reduce-scatter.4
